TPU v7x, 128 devices: a whole 4x4x4 slice. The times are simulated.
128 devices in a mesh: op: 16 (over x, y), sec: 8 (over z, core).
Axes of the slice: x: 4, y: 4, z: 4, core: 2. Of those that a mesh axis runs over, the one named last changes fastest.
Arguments:
- wave: bfloat16 [32, 256, 4, 256], P('op'), may hold values from -6 to 6
- sector_dims: int32 [32], replicated, may hold values from 64 to 256, as said below
- left_ops: bfloat16 [32, 128, 256, 256], P(None, ('op', 'sec')), may hold values from -0.375 to 0.375
- right_ops: bfloat16 [32, 16, 8, 256, 256], P('op', None, 'sec'), may hold values from -0.375 to 0.375
- site_ops: float32 [128, 4, 4], replicated, may hold values from -0.25 to 0.25
Outputs:
- sigma: bfloat16 [32, 256, 4, 256], P('op', 'sec')
Inputs may be any that keep to these rules, and one draw needn't show every extreme that they name: `sector_dims`: every entry is a multiple of 64, and at least one sector has exactly 256 states.
All inputs are finite; a program needn't handle non-finite values.
Results may differ from a plain program's by a relative error of at most 0.005.
Values may be sent and summed in bfloat16 or wider, within the bound.
No kernel may reach another device: no remote copies, remote signals or barrier semaphores. Data moves between devices by JAX's collectives and lax.ppermute only.
A program may use at most 128 MiB of HBM per device.

v0:
```python
import jax
import jax.numpy as jnp
from jax import lax
from jax.sharding import PartitionSpec as P


def sector_mask(sizes, width):
    places = lax.broadcasted_iota(jnp.int32, (sizes.shape[0], width), 1)
    return (places < sizes[:, None]).astype(jnp.float32)


def left_step(blocks, waves, site_mats):

    def one_sector(inputs):
        ops_block, wave_block = inputs
        first = jnp.einsum(
            "klm,mpr->klpr", ops_block, wave_block, preferred_element_type=jnp.float32
        )
        second = jnp.einsum("klpr,kqp->klqr", first, site_mats, precision=lax.Precision.HIGHEST)
        return second.astype(jnp.bfloat16)

    return lax.map(one_sector, (blocks, waves))


def shards(wave, sector_dims, left_ops, right_ops, site_ops):
    sec_count = lax.axis_size("sec")
    op_index = lax.axis_index("op")
    sec_index = lax.axis_index("sec")
    local_sectors = wave.shape[0]
    width = wave.shape[1]
    term_count = left_ops.shape[1]
    own_sizes = lax.dynamic_slice_in_dim(sector_dims, op_index * local_sectors, local_sectors)
    own_mask = sector_mask(own_sizes, width)
    masked = (
        wave.astype(jnp.float32) * own_mask[:, :, None, None] * own_mask[:, None, None, :]
    ).astype(jnp.bfloat16)
    first_term = (op_index * sec_count + sec_index) * term_count
    site_local = lax.dynamic_slice_in_dim(site_ops, first_term, term_count)
    inter = left_step(left_ops, lax.all_gather(masked, "op", axis=0, tiled=True), site_local)
    inter = lax.all_to_all(inter, "op", split_axis=0, concat_axis=1, tiled=True)
    right_local = right_ops.reshape(local_sectors, -1, width, width)
    partial_sum = jnp.einsum(
        "sklqm,skrm->slqr", inter, right_local, preferred_element_type=jnp.float32
    )
    row_count = width // sec_count
    summed = lax.psum(partial_sum, "sec")
    share = lax.dynamic_slice_in_dim(summed, sec_index * row_count, row_count, 1)
    row_mask = lax.dynamic_slice_in_dim(own_mask, sec_index * row_count, row_count, 1)
    return (share * row_mask[:, :, None, None] * own_mask[:, None, None, :]).astype(jnp.bfloat16)


def solution(mesh):
    placed = (
        P("op", None, None, None),
        P(),
        P(None, ("op", "sec"), None, None),
        P("op", None, "sec", None, None),
        P(),
    )
    return jax.shard_map(
        shards, mesh=mesh, in_specs=placed, out_specs=P("op", "sec", None, None), check_vma=False
    )
```

profile of v0, /device:TPU:8, one launch (start us, length us, event | category | flops | bytes accessed | tf_op | source)
XLA Modules:
  0.0 555.0 jit_solution(4734230497809991994)
XLA Ops:
  7.4 2.5 multiply_convert_fusion
  10.2 113.3 %all-gather.2.cloned.1.call-done = bf16[32,256,4,256]{3,1,2,0:T(8,128)(2,1)} async-done(((bf16[2,256,4,256]{3,1,2,0:T(8,128)(2,1)}), bf16[32,256,4,256]{3,1,2,0:T(8,128)(2,1)}) %all-gather.2.cloned.1.call-update) | async-done | bytes 16777232 | tf_op jit(solution)/shard_map/all_gather | solution.py:39
  123.5 153.4 %while.10 = (s32[]{:T(128)}, bf16[32,1,256,4,256]{4,2,3,1,0:T(8,128)(2,1)}, bf16[32,1,256,256]{3,2,1,0:T(8,128)(2,1)}, bf16[32,256,4,256]{3,1,2,0:T(8,128)(2,1)}, f32[1,4,4]{2,1,0:T(4,128)S(1)}, /*index=5*/s32[]{:T(128)}) while((s32[]{:T(128)}, bf16[32,1,256,4,256]{4,2,3,1,0:T(8,128)(2,1)}, bf16[32,1,256,256]{3,2,1,0:T(8,128)(2,1)}, ...), condition=%wide.region_1.2_spmd, body=%wide.region_0.1_spmd.sunk | while | flops 147062784 | bytes 4327045 | solution.py:22
  123.5 1.4 fusion.23
  124.9 2.5 fusion.24
  128.3 1.4 fusion.23
  129.7 2.5 fusion.24
  133.0 1.4 fusion.23
  134.5 2.5 fusion.24
  137.8 1.4 fusion.23
  139.2 2.5 fusion.24
  142.6 1.4 fusion.23
  144.0 2.5 fusion.24
  148.8 2.5 fusion.24
  152.2 1.4 fusion.23
  153.6 2.5 fusion.24
  157.0 1.4 fusion.23
  158.4 2.5 fusion.24
  163.2 2.5 fusion.24
  166.5 1.4 fusion.23
  168.0 2.5 fusion.24
  171.3 1.4 fusion.23
  172.8 2.5 fusion.24
  176.1 1.4 fusion.23
  177.6 2.5 fusion.24
  182.4 2.5 fusion.24
  185.7 1.4 fusion.23
  187.2 2.5 fusion.24
  190.5 1.4 fusion.23
  191.9 2.5 fusion.24
  195.3 1.4 fusion.23
  196.7 2.5 fusion.24
  200.1 1.4 fusion.23
  201.5 2.5 fusion.24
  206.4 2.5 fusion.24
  209.8 1.4 fusion.23
  211.2 2.5 fusion.24
  214.6 1.4 fusion.23
  216.0 2.5 fusion.24
  219.3 1.4 fusion.23
  220.7 2.5 fusion.24
  224.1 1.4 fusion.23
  225.6 2.5 fusion.24
  228.9 1.4 fusion.23
  230.3 2.5 fusion.24
  233.7 1.4 fusion.23
  235.1 2.5 fusion.24
  239.9 2.5 fusion.24
  243.3 1.4 fusion.23
  244.7 2.5 fusion.24
  248.1 1.4 fusion.23
  249.5 2.5 fusion.24
  252.9 1.4 fusion.23
  254.3 2.5 fusion.24
  257.7 1.4 fusion.23
  259.1 2.5 fusion.24
  262.5 1.4 fusion.23
  263.9 2.5 fusion.24
  268.7 2.5 fusion.24
  273.5 2.5 fusion.24
  276.9 190.9 %all_to_all.18 = bf16[32,1,256,4,256]{4,2,3,1,0:T(8,128)(2,1)} all-to-all(bf16[32,1,256,4,256]{4,2,3,1,0:T(8,128)(2,1)} %get-tuple-element.32), channel_id=1, replica_groups=mesh['op'=16,'sec'=8] {'op'}, dimensions={0} | all-to-all | bytes 33554432 | tf_op jit(solution)/shard_map/all_to_all | solution.py:40
  467.8 9.4 %fusion.9 = f32[2,256,4,256,1]{3,1,2,0,4:T(8,128)S(1)} fusion(bf16[2,16,256,4,256]{4,2,3,0,1:T(8,128)(2,1)} %bitcast.43, bf16[2,16,1,256,256]{4,3,2,1,0:T(8,128)(2,1)} %param.10), kind=kOutput, calls=%fused_computation.11 | convolution fusion | flops 4294967296 | bytes 23068672 | tf_op jit(solution)/shard_map/sklqm,skrm->slqr/dot_general | solution.py:42
  477.2 1.5 copy.35
  478.8 67.5 %all-reduce.2.cloned.1.call-done = f32[2,256,4,256]{3,1,0,2:T(8,128)} async-done(((f32[2,256,4,256]{3,1,0,2:T(8,128)}), f32[2,256,4,256]{3,1,0,2:T(8,128)}) %all-reduce.2.cloned.1.call-update) | async-done | bytes 2097168 | tf_op jit(solution)/shard_map/psum | solution.py:46
  (55 shorter events, 41.0 us)
Async XLA Ops:
  6.5 3.4 copy-start
  6.5 116.9 %all-gather.2.cloned.1.call-start = ((), (), s32[]{:S(2)}) async-start(), calls=%async_computation.1 | async-start | bytes 17825792 | tf_op jit(solution)/shard_map/all_gather | solution.py:39
  9.9 536.4 %all-reduce.2.cloned.1.call-start = ((), (), s32[]{:S(2)}) async-start(), calls=%async_computation.2 | async-start | bytes 4194304 | tf_op jit(solution)/shard_map/psum | solution.py:46
  467.8 80.3 %copy-start.1 = (f32[128,4,4]{0,2,1:T(4,128)S(1)}, f32[128,4,4]{0,2,1:T(4,128)}, u32[]{:S(2)}) copy-start(f32[128,4,4]{0,2,1:T(4,128)} %param.11) | copy-start | bytes 24580
Sparse Core Ops, SparseCore 0:
  10.0 113.4 all-gather.1
  478.9 67.4 all-reduce.1
where the time goes:
time: 556 us; the launch traced here: 555 us
  blocking collectives  191 us (34%)
  waiting for transfers between devices  181 us (33%)
  matrix products  134 us (24%)
  local copies, waits for them, and re-layouts  31.5 us (6%)
  between operations  13.4 us (2%)
    all_to_all x1, blocking collectives, shards(): inter = lax.all_to_all(inter, 'op', split_axis=0, concat_axis=1, tiled=True)  191 us
    all_gather x1, waiting for transfers between devices, shards(): lax.all_gather(masked, 'op', axis=0, tiled=True)  113 us
    dot_general x32, matrix products, one_sector(): jnp.einsum('klpr,kqp->klqr', first, site_mats, precision=lax.Precision.HI...  79.6 us
    psum x1, waiting for transfers between devices, shards(): summed = lax.psum(partial_sum, 'sec')  67.5 us
    dot_general x32, matrix products, one_sector(): jnp.einsum('klm,mpr->klpr', ops_block, wave_block, preferred_element_type...  45.2 us
    dynamic_update_slice x32, local copies, waits for them, and re-layouts, left_step(): return lax.map(one_sector, (blocks, waves))  28.2 us
  transfers between devices with their start and end apart: 2, of which 2 were waited for; matrix products, arithmetic and copies ran while one was open for 0% of the time, Pallas kernels for 0%

commit v1 on v0

v1 whole, which is shorter than its diff:
```python
import functools

import jax
import jax.numpy as jnp
from jax import lax
from jax.experimental import pallas as pl
from jax.experimental.pallas import tpu as pltpu
from jax.sharding import Mesh, PartitionSpec as P

CORES = 2
GROUP = 2


def sigma_kernel(z_count, group, meta, site_ref, left_ref, wave_ref, own_ref, other_ref, *refs):
    outs, total = refs[:z_count], refs[z_count]
    step = pl.program_id(0)
    core, z_at, sec_count = meta[0], meta[1], meta[2]

    @pl.when(step == 0)
    def _():
        total[...] = jnp.zeros_like(total)

    p_size = wave_ref.shape[0]
    mixed = [[] for _ in range(p_size)]
    rights = []
    for at in range(group):
        source = step * group + at
        for slot in range(CORES):
            side = core if slot == 0 else 1 - core
            term = source * sec_count + z_at * CORES + side
            left = left_ref[at * CORES + side]
            first = [
                jnp.dot(left, wave_ref[p], preferred_element_type=jnp.float32)
                for p in range(p_size)
            ]
            for q in range(p_size):
                second = first[0] * site_ref[term, q * p_size]
                for p in range(1, p_size):
                    second = second + first[p] * site_ref[term, q * p_size + p]
                mixed[q].append(second.astype(jnp.bfloat16))
            rights.append((own_ref if slot == 0 else other_ref)[0, at, 0])
    right = jnp.concatenate(rights, axis=1)
    for q in range(p_size):
        total[q] += lax.dot_general(
            jnp.concatenate(mixed[q], axis=1),
            right,
            (((1,), (1,)), ((), ())),
            preferred_element_type=jnp.float32,
        )

    @pl.when(step == pl.num_programs(0) - 1)
    def _():
        rows = total.shape[1] // z_count
        for shift in range(z_count):
            start = pl.multiple_of(lax.rem(z_at + shift, z_count) * rows, rows)
            block = total[:, pl.ds(start, rows), :]
            outs[shift][...] = block.astype(outs[shift].dtype)


def sigma_call(meta, site, left, wave, own, other, z_count):
    sources, width = own.shape[1], own.shape[-1]
    p_size = wave.shape[0]
    rows = width // z_count
    group = GROUP
    right_spec = pl.BlockSpec(
        (1, group, 1, width, width), lambda step, meta: (meta[0], step, 0, 0, 0)
    )
    return pl.pallas_call(
        functools.partial(sigma_kernel, z_count, group),
        grid_spec=pltpu.PrefetchScalarGridSpec(
            num_scalar_prefetch=1,
            grid=(sources // group,),
            in_specs=[
                pl.BlockSpec(memory_space=pltpu.SMEM),
                pl.BlockSpec((group * CORES, width, width), lambda step, meta: (step, 0, 0)),
                pl.BlockSpec((p_size, width, width), lambda step, meta: (0, 0, 0)),
                right_spec,
                right_spec,
            ],
            out_specs=[
                pl.BlockSpec((p_size, rows, width), lambda step, meta: (0, 0, 0))
            ] * z_count,
            scratch_shapes=[pltpu.VMEM((p_size, width, width), jnp.float32)],
        ),
        out_shape=[
            jax.ShapeDtypeStruct((p_size, rows, width), jnp.float32 if s == 0 else jnp.bfloat16)
            for s in range(z_count)
        ],
        compiler_params=pltpu.CompilerParams(
            dimension_semantics=("arbitrary",), vmem_limit_bytes=48 << 20
        ),
        name="sigma_terms",
    )(meta, site, left, wave, own, other)


def shards(wave, sector_dims, left_ops, right_ops, site_ops):
    z_count = lax.axis_size("z")
    op_at, z_at, core = lax.axis_index("op"), lax.axis_index("z"), lax.axis_index("core")
    width, p_size = wave.shape[1], wave.shape[2]
    swap = [(0, 1), (1, 0)]

    other = lax.ppermute(right_ops, "core", swap)
    left = lax.all_to_all(left_ops[:, 0], ("op", "core"), split_axis=0, concat_axis=0, tiled=True)

    size = lax.dynamic_slice_in_dim(sector_dims, op_at * CORES + core, 1)
    mask = (lax.iota(jnp.int32, width) < size).astype(jnp.float32)
    block = lax.dynamic_index_in_dim(wave, core, 0, keepdims=False)
    masked = block.astype(jnp.float32) * mask[:, None, None] * mask[None, None, :]
    masked = masked.astype(jnp.bfloat16).transpose(1, 0, 2)

    meta = jnp.stack([core, z_at, jnp.int32(z_count * CORES)]).astype(jnp.int32)
    site = site_ops.reshape(site_ops.shape[0], -1)
    parts = sigma_call(meta, site, left, masked, right_ops, other, z_count)

    total = parts[0]
    for shift in range(1, z_count):
        ring = [(z, (z + shift) % z_count) for z in range(z_count)]
        total = total + lax.ppermute(parts[shift], "z", ring).astype(jnp.float32)

    rows = width // z_count
    row_mask = lax.dynamic_slice_in_dim(mask, z_at * rows, rows)
    share = (total * row_mask[None, :, None] * mask[None, None, :]).astype(jnp.bfloat16)
    share = share.transpose(1, 0, 2).reshape(CORES, rows // CORES, p_size, width)
    keep = lax.dynamic_index_in_dim(share, core, 0, keepdims=False)
    give = lax.dynamic_index_in_dim(share, 1 - core, 0, keepdims=False)
    take = lax.ppermute(give, "core", swap)
    first = core == 0
    return jnp.stack([jnp.where(first, keep, take), jnp.where(first, take, keep)])


def solution(mesh):
    op_count, sec_count = mesh.shape["op"], mesh.shape["sec"]
    split = Mesh(
        mesh.devices.reshape(op_count, sec_count // CORES, CORES), ("op", "z", "core")
    )
    placed = (
        P("op", None, None, None),
        P(),
        P(None, ("op", "z", "core"), None, None),
        P("op", None, ("z", "core"), None, None),
        P(),
    )
    return jax.shard_map(
        shards, mesh=split, in_specs=placed,
        out_specs=P("op", ("z", "core"), None, None), check_vma=False,
    )
```

time: 556 us -> 93.2 us (0.17)
  blocking collectives: 191 us -> 0 us
  matrix products: 134 us -> 0 us
  waiting for transfers between devices: 181 us -> 58.6 us
  local copies, waits for them, and re-layouts: 31.5 us -> 1.1 us
  Pallas kernels: 0 us -> 16.5 us
  starting transfers between devices: 0.04 us -> 14.5 us
  between operations: 13.4 us -> 0.13 us
    all_to_all x1 -> x0, blocking collectives: 191 us -> none  [shards(): inter = lax.all_to_all(inter, 'op', split_axis=0, concat_axis=1, tiled=True)]
    dot_general x65 -> x0, matrix products: 134 us -> none  [the longest x32 79.6 us: one_sector(): jnp.einsum('klpr,kqp->klqr', first, site_mats, precision=lax.Precision.HI...]
    all_gather x1 -> x0, waiting for transfers between devices: 113 us -> none  [shards(): lax.all_gather(masked, 'op', axis=0, tiled=True)]
    psum x1 -> x0, waiting for transfers between devices: 67.5 us -> none  [shards(): summed = lax.psum(partial_sum, 'sec')]
    all_to_all x0 -> x1, waiting for transfers between devices: none -> 52.7 us  [shards(): lax.all_to_all(left_ops[:, 0], ('op', 'core'), split_axis=0, concat_axis=...]
    dynamic_update_slice x32 -> x0, local copies, waits for them, and re-layouts: 28.2 us -> none  [left_step(): return lax.map(one_sector, (blocks, waves))]
    pallas_call x0 -> x1, Pallas kernels: none -> 16.5 us  [sigma_call(): pl.pallas_call(functools.partial(sigma_kernel, z_count, group), grid_spec...]
    all_to_all x0 -> x1, starting transfers between devices: none -> 7.81 us  [shards(): lax.all_to_all(left_ops[:, 0], ('op', 'core'), split_axis=0, concat_axis=...]
  transfers between devices with their start and end apart: 2 -> 6, of which waited for: 2 -> 4; matrix products, arithmetic and copies ran while one was open for 0% -> 2% of each run, Pallas kernels for 0% -> 0%
where the time goes in v1:
time: 93.2 us; the launch traced here: 92.7 us
  waiting for transfers between devices  58.6 us (63%)
  Pallas kernels  16.5 us (18%)
  starting transfers between devices  14.5 us (16%)
  other arithmetic  1.81 us (2%)
  local copies, waits for them, and re-layouts  1.1 us (1%)
    all_to_all x1, waiting for transfers between devices, shards(): lax.all_to_all(left_ops[:, 0], ('op', 'core'), split_axis=0, concat_axis=...  52.7 us
    pallas_call x1, Pallas kernels, sigma_call(): pl.pallas_call(functools.partial(sigma_kernel, z_count, group), grid_spec...  16.5 us
    all_to_all x1, starting transfers between devices, shards(): lax.all_to_all(left_ops[:, 0], ('op', 'core'), split_axis=0, concat_axis=...  7.81 us
    ppermute x3, starting transfers between devices, shards(): total = total + lax.ppermute(parts[shift], 'z', ring).astype(jnp.float32)  6.57 us
    ppermute x3, waiting for transfers between devices, shards(): total = total + lax.ppermute(parts[shift], 'z', ring).astype(jnp.float32)  4.74 us
  transfers between devices with their start and end apart: 6, of which 4 were waited for; matrix products, arithmetic and copies ran while one was open for 2% of the time, Pallas kernels for 0%

profile of v1, /device:TPU:8, one launch (start us, length us, event | category | flops | bytes accessed | tf_op | source)
XLA Modules:
  0.0 92.7 jit_solution(17804151110486944587)
XLA Ops:
  0.0 0.0 copy-start
  0.0 0.0 collective-permute-start
  0.0 0.0 copy-start.1
  0.0 0.0 copy-start.2
  0.0 7.8 %all-to-all-start = ((bf16[32,256,256]{2,1,0:T(8,128)(2,1)}), bf16[32,256,256]{2,1,0:T(8,128)(2,1)}, u32[]{:S(2)}, u32[]{:S(2)}) async-start(bf16[32,256,256]{2,1,0:T(8,128)(2,1)} %bitcast.29), calls=%async_computation | async-start | bytes 8388608 | tf_op jit(solution)/shard_map/all_to_all | solution.py:103
  7.9 0.0 copy-done.1
  7.9 0.1 copy.11.site_ref
  8.0 0.0 copy-done.2
  8.0 0.7 dynamic_slice.18
  8.6 0.1 pad_add_fusion.meta
  8.7 0.6 compare_convert_fusion
  9.3 0.0 copy-done
  9.3 0.2 constant_dynamic-slice_fusion.2
  9.5 0.2 fusion.2.wave_ref
  9.7 52.7 %all-to-all-done.left_ref = bf16[32,256,256]{2,1,0:T(8,128)(2,1)} async-done(((bf16[32,256,256]{2,1,0:T(8,128)(2,1)}), bf16[32,256,256]{2,1,0:T(8,128)(2,1)}, u32[]{:S(2)}, u32[]{:S(2)}) %all-to-all-start) | async-done | bytes 4194336 | tf_op jit(solution)/shard_map/all_to_all | solution.py:103
  62.4 0.0 collective-permute-done.other_ref
  62.4 16.5 %sigma_terms.1 = (f32[4,64,256]{2,1,0:T(8,128)S(1)}, bf16[4,64,256]{2,1,0:T(8,128)(2,1)S(1)}, bf16[4,64,256]{2,1,0:T(8,128)(2,1)S(1)}, bf16[4,64,256]{2,1,0:T(8,128)(2,1)S(1)}) custom-call(s32[3]{0:T(128)S(1)} %pad_add_fusion.meta, f32[128,16]{1,0:T(8,128)S(1)} %copy.11.site_ref, bf16[32,256,256]{2,1,0:T(8,128)(2,1)} %all-to-all-done.left_ref, ...), custom_call_target="tpu_custom_call" | custom-call | tf_op jit(solution)/shard_map/sigma_terms/pallas_call | solution.py:68
  78.9 2.0 %collective-permute-start.1 = (bf16[4,64,256]{2,1,0:T(8,128)(2,1)S(1)}, bf16[4,64,256]{2,1,0:T(8,128)(2,1)S(1)}, u32[]{:S(2)}, u32[]{:S(2)}) collective-permute-start(bf16[4,64,256]{2,1,0:T(8,128)(2,1)S(1)} %get-tuple-element.10), channel_id=1, source_target_pairs={{0,2},{2,4},{4,6},{6,0},{1,3},{3,5},{5,7},{7,1},{8,10},{10,12},{12... | collective-permute-start | bytes 393224 | tf_op jit(solution)/shard_map/ppermute | solution.py:118
  80.9 3.6 %collective-permute-start.2 = (bf16[4,64,256]{2,1,0:T(8,128)(2,1)S(1)}, bf16[4,64,256]{2,1,0:T(8,128)(2,1)S(1)}, u32[]{:S(2)}, u32[]{:S(2)}) collective-permute-start(bf16[4,64,256]{2,1,0:T(8,128)(2,1)S(1)} %get-tuple-element.11), channel_id=1, source_target_pairs={{0,4},{2,6},{4,0},{6,2},{1,5},{3,7},{5,1},{7,3},{8,12},{10,14},{12... | collective-permute-start | bytes 393224 | tf_op jit(solution)/shard_map/ppermute | solution.py:118
  84.5 1.0 %collective-permute-start.3 = (bf16[4,64,256]{2,1,0:T(8,128)(2,1)S(1)}, bf16[4,64,256]{2,1,0:T(8,128)(2,1)S(1)}, u32[]{:S(2)}, u32[]{:S(2)}) collective-permute-start(bf16[4,64,256]{2,1,0:T(8,128)(2,1)S(1)} %get-tuple-element.12), channel_id=1, source_target_pairs={{0,6},{2,0},{4,2},{6,4},{1,7},{3,1},{5,3},{7,5},{8,14},{10,8},{12,... | collective-permute-start | bytes 393224 | tf_op jit(solution)/shard_map/ppermute | solution.py:118
  85.5 0.1 dynamic_slice.19
  85.6 1.0 %collective-permute-done.1 = bf16[4,64,256]{2,1,0:T(8,128)(2,1)S(1)} collective-permute-done((bf16[4,64,256]{2,1,0:T(8,128)(2,1)S(1)}, bf16[4,64,256]{2,1,0:T(8,128)(2,1)S(1)}, u32[]{:S(2)}, u32[]{:S(2)}) %collective-permute-start.1) | collective-permute-done | bytes 131104 | tf_op jit(solution)/shard_map/ppermute | solution.py:118
  86.5 3.8 %collective-permute-done.2 = bf16[4,64,256]{2,1,0:T(8,128)(2,1)S(1)} collective-permute-done((bf16[4,64,256]{2,1,0:T(8,128)(2,1)S(1)}, bf16[4,64,256]{2,1,0:T(8,128)(2,1)S(1)}, u32[]{:S(2)}, u32[]{:S(2)}) %collective-permute-start.2) | collective-permute-done | bytes 131104 | tf_op jit(solution)/shard_map/ppermute | solution.py:118
  90.3 0.0 collective-permute-done.3
  90.3 0.1 multiply_convert_fusion
  90.5 0.1 copy.21
  90.5 0.1 collective-permute-start.4
  90.6 1.2 %collective-permute-done.4 = bf16[32,4,256]{2,1,0:T(4,128)(2,1)S(1)} collective-permute-done((bf16[32,4,256]{2,1,0:T(4,128)(2,1)S(1)}, bf16[32,4,256]{2,1,0:T(4,128)(2,1)S(1)}, u32[]{:S(2)}, u32[]{:S(2)}) %collective-permute-start.4) | collective-permute-done | bytes 65568 | tf_op jit(solution)/shard_map/ppermute | solution.py:126
  91.8 0.1 fusion.3
  91.9 0.7 pad_maximum_fusion
  (1 shorter events, 0.0 us)
Async XLA Ops:
  0.0 9.3 %copy-start = (bf16[2,256,4,256]{3,2,1,0:T(4,128)(2,1)S(1)}, bf16[2,256,4,256]{3,2,1,0:T(4,128)(2,1)}, u32[]{:S(2)}) copy-start(bf16[2,256,4,256]{3,2,1,0:T(4,128)(2,1)} %param.5) | copy-start | bytes 3145732
  0.0 62.4 %collective-permute-start = (bf16[2,16,1,256,256]{4,3,2,1,0:T(8,128)(2,1)}, bf16[2,16,1,256,256]{4,3,2,1,0:T(8,128)(2,1)}, u32[]{:S(2)}, u32[]{:S(2)}) collective-permute-start(bf16[2,16,1,256,256]{4,3,2,1,0:T(8,128)(2,1)} %own_ref.1), channel_id=1, source_target_pairs={{0,1},{1,0},{2,3},{3,2},{4,5},{5,4},{6,7},{7,6},{8,9},{9,8},{10,11... | collective-permute-start | bytes 12582920 | tf_op jit(solution)/shard_map/ppermute | solution.py:102
  0.0 7.9 %copy-start.1 = (f32[128,4,4]{0,2,1:T(4,128)S(1)}, f32[128,4,4]{0,2,1:T(4,128)}, u32[]{:S(2)}) copy-start(f32[128,4,4]{0,2,1:T(4,128)} %param.9) | copy-start | bytes 24580
  0.0 8.0 %copy-start.2 = (s32[32]{0:T(128)S(1)}, s32[32]{0:T(128)}, u32[]{:S(2)}) copy-start(s32[32]{0:T(128)} %param.6) | copy-start | bytes 388
  0.0 62.4 %all-to-all-start = ((bf16[32,256,256]{2,1,0:T(8,128)(2,1)}), bf16[32,256,256]{2,1,0:T(8,128)(2,1)}, u32[]{:S(2)}, u32[]{:S(2)}) async-start(bf16[32,256,256]{2,1,0:T(8,128)(2,1)} %bitcast.29), calls=%async_computation | async-start | bytes 8388608 | tf_op jit(solution)/shard_map/all_to_all | solution.py:103
  78.9 7.6 %collective-permute-start.1 = (bf16[4,64,256]{2,1,0:T(8,128)(2,1)S(1)}, bf16[4,64,256]{2,1,0:T(8,128)(2,1)S(1)}, u32[]{:S(2)}, u32[]{:S(2)}) collective-permute-start(bf16[4,64,256]{2,1,0:T(8,128)(2,1)S(1)} %get-tuple-element.10), channel_id=1, source_target_pairs={{0,2},{2,4},{4,6},{6,0},{1,3},{3,5},{5,7},{7,1},{8,10},{10,12},{12... | collective-permute-start | bytes 393224 | tf_op jit(solution)/shard_map/ppermute | solution.py:118
  80.9 9.4 %collective-permute-start.2 = (bf16[4,64,256]{2,1,0:T(8,128)(2,1)S(1)}, bf16[4,64,256]{2,1,0:T(8,128)(2,1)S(1)}, u32[]{:S(2)}, u32[]{:S(2)}) collective-permute-start(bf16[4,64,256]{2,1,0:T(8,128)(2,1)S(1)} %get-tuple-element.11), channel_id=1, source_target_pairs={{0,4},{2,6},{4,0},{6,2},{1,5},{3,7},{5,1},{7,3},{8,12},{10,14},{12... | collective-permute-start | bytes 393224 | tf_op jit(solution)/shard_map/ppermute | solution.py:118
  84.5 5.8 %collective-permute-start.3 = (bf16[4,64,256]{2,1,0:T(8,128)(2,1)S(1)}, bf16[4,64,256]{2,1,0:T(8,128)(2,1)S(1)}, u32[]{:S(2)}, u32[]{:S(2)}) collective-permute-start(bf16[4,64,256]{2,1,0:T(8,128)(2,1)S(1)} %get-tuple-element.12), channel_id=1, source_target_pairs={{0,6},{2,0},{4,2},{6,4},{1,7},{3,1},{5,3},{7,5},{8,14},{10,8},{12,... | collective-permute-start | bytes 393224 | tf_op jit(solution)/shard_map/ppermute | solution.py:118
  90.5 1.3 %collective-permute-start.4 = (bf16[32,4,256]{2,1,0:T(4,128)(2,1)S(1)}, bf16[32,4,256]{2,1,0:T(4,128)(2,1)S(1)}, u32[]{:S(2)}, u32[]{:S(2)}) collective-permute-start(bf16[32,4,256]{2,1,0:T(4,128)(2,1)S(1)} %bitcast.31), channel_id=1, source_target_pairs={{0,1},{1,0},{2,3},{3,2},{4,5},{5,4},{6,7},{7,6},{8,9},{9,8},{10,11... | collective-permute-start | bytes 196616 | tf_op jit(solution)/shard_map/ppermute | solution.py:126

commit v2 on v1

v2 whole, which is shorter than its diff:
```python
import functools

import jax
import jax.numpy as jnp
from jax import lax
from jax.experimental import pallas as pl
from jax.experimental.pallas import tpu as pltpu
from jax.sharding import Mesh, PartitionSpec as P

CORES = 2
GROUP = 2
ROWS = 16
LEFT_TERMS = 2
VMEM_LIMIT = 48 << 20


def right_kernel(group, meta, site_ref, wave_ref, own_ref, other_ref, held_ref, first):
    step = pl.program_id(0)
    core, z_at, sec_count = meta[0], meta[1], meta[2]
    p_size, width = wave_ref.shape[0], wave_ref.shape[1]
    waves = wave_ref[...].reshape(p_size * width, width)
    for at in range(group):
        source = step * group + at
        for slot in range(CORES):
            side = core if slot == 0 else 1 - core
            term = source * sec_count + z_at * CORES + side
            buf = (at * CORES + slot) % 2
            first[buf] = lax.dot_general(
                waves, (own_ref if slot == 0 else other_ref)[0, at, 0],
                (((1,), (1,)), ((), ())), preferred_element_type=jnp.float32,
            )
            scale = [[site_ref[term, q * p_size + p] for p in range(p_size)] for q in range(p_size)]
            place = at * CORES + side
            for low in range(0, width, ROWS):
                parts = [first[buf, p * width + low : p * width + low + ROWS] for p in range(p_size)]
                for q in range(p_size):
                    second = parts[0] * scale[q][0]
                    for p in range(1, p_size):
                        second = second + parts[p] * scale[q][p]
                    held_ref[place, low : low + ROWS, q * width : (q + 1) * width] = second.astype(
                        jnp.bfloat16
                    )


def right_call(meta, site, wave, own, other):
    sources, width = own.shape[1], own.shape[-1]
    p_size = wave.shape[0]
    right_spec = pl.BlockSpec(
        (1, GROUP, 1, width, width), lambda step, meta: (meta[0], step, 0, 0, 0)
    )
    return pl.pallas_call(
        functools.partial(right_kernel, GROUP),
        grid_spec=pltpu.PrefetchScalarGridSpec(
            num_scalar_prefetch=1,
            grid=(sources // GROUP,),
            in_specs=[
                pl.BlockSpec(memory_space=pltpu.SMEM),
                pl.BlockSpec((p_size, width, width), lambda step, meta: (0, 0, 0)),
                right_spec,
                right_spec,
            ],
            out_specs=pl.BlockSpec(
                (GROUP * CORES, width, p_size * width), lambda step, meta: (step, 0, 0)
            ),
            scratch_shapes=[pltpu.VMEM((2, p_size * width, width), jnp.float32)],
        ),
        out_shape=jax.ShapeDtypeStruct((sources * CORES, width, p_size * width), jnp.bfloat16),
        compiler_params=pltpu.CompilerParams(vmem_limit_bytes=VMEM_LIMIT),
        name="right_terms",
    )(meta, site, wave, own, other)


def left_kernel(z_count, p_size, meta, left_hbm, held_hbm, *refs):
    outs = refs[:z_count]
    left, held, total, left_sem, held_sem = refs[z_count:]
    z_at = meta[1]
    terms, width = left.shape[0], left.shape[1]
    copies = []
    for at in range(0, terms, LEFT_TERMS):
        span = pl.ds(at, LEFT_TERMS)
        slot = at // LEFT_TERMS
        pair = (
            pltpu.make_async_copy(left_hbm.at[span], left.at[span], left_sem.at[slot]),
            pltpu.make_async_copy(held_hbm.at[span], held.at[span], held_sem.at[slot]),
        )
        for copy in pair:
            copy.start()
        copies.append(pair)

    for slot, pair in enumerate(copies):
        for copy in pair:
            copy.wait()
        add = None
        for at in range(slot * LEFT_TERMS, (slot + 1) * LEFT_TERMS):
            product = jnp.dot(left[at], held[at], preferred_element_type=jnp.float32)
            add = product if add is None else add + product
        if slot == 0:
            total[...] = add
        else:
            total[...] += add

    rows = width // z_count
    for shift in range(z_count):
        start = pl.multiple_of(lax.rem(z_at + shift, z_count) * rows, rows)
        block = total[pl.ds(start, rows), :]
        for q in range(p_size):
            outs[shift][q] = block[:, q * width : (q + 1) * width].astype(outs[shift].dtype)


def left_call(meta, left, held, z_count):
    terms, width, columns = held.shape
    p_size = columns // width
    rows = width // z_count
    return pl.pallas_call(
        functools.partial(left_kernel, z_count, p_size),
        in_specs=[
            pl.BlockSpec(memory_space=pltpu.SMEM),
            pl.BlockSpec(memory_space=pl.ANY),
            pl.BlockSpec(memory_space=pl.ANY),
        ],
        out_specs=[pl.BlockSpec(memory_space=pltpu.VMEM)] * z_count,
        out_shape=[
            jax.ShapeDtypeStruct((p_size, rows, width), jnp.float32 if s == 0 else jnp.bfloat16)
            for s in range(z_count)
        ],
        scratch_shapes=[
            pltpu.VMEM((terms, width, width), jnp.bfloat16),
            pltpu.VMEM((terms, width, columns), jnp.bfloat16),
            pltpu.VMEM((width, columns), jnp.float32),
            pltpu.SemaphoreType.DMA((terms // LEFT_TERMS,)),
            pltpu.SemaphoreType.DMA((terms // LEFT_TERMS,)),
        ],
        compiler_params=pltpu.CompilerParams(vmem_limit_bytes=VMEM_LIMIT),
        name="left_terms",
    )(meta, left, held)


def shards(wave, sector_dims, left_ops, right_ops, site_ops):
    z_count = lax.axis_size("z")
    op_at, z_at, core = lax.axis_index("op"), lax.axis_index("z"), lax.axis_index("core")
    width, p_size = wave.shape[1], wave.shape[2]
    swap = [(0, 1), (1, 0)]

    other = lax.ppermute(right_ops, "core", swap)
    left = lax.all_to_all(left_ops[:, 0], ("op", "core"), split_axis=0, concat_axis=0, tiled=True)

    size = lax.dynamic_slice_in_dim(sector_dims, op_at * CORES + core, 1)
    mask = (lax.iota(jnp.int32, width) < size).astype(jnp.float32)
    block = lax.dynamic_index_in_dim(wave, core, 0, keepdims=False)
    masked = block.astype(jnp.float32) * mask[:, None, None] * mask[None, None, :]
    masked = masked.astype(jnp.bfloat16).transpose(1, 0, 2)

    meta = jnp.stack([core, z_at, jnp.int32(z_count * CORES)]).astype(jnp.int32)
    site = site_ops.reshape(site_ops.shape[0], -1)
    held = right_call(meta, site, masked, right_ops, other)
    parts = left_call(meta, left, held, z_count)

    total = parts[0]
    for shift in sorted(range(1, z_count), key=lambda s: -min(s, z_count - s)):
        ring = [(z, (z + shift) % z_count) for z in range(z_count)]
        total = total + lax.ppermute(parts[shift], "z", ring).astype(jnp.float32)

    rows = width // z_count
    row_mask = lax.dynamic_slice_in_dim(mask, z_at * rows, rows)
    share = (total * row_mask[None, :, None] * mask[None, None, :]).astype(jnp.bfloat16)
    share = share.transpose(1, 0, 2).reshape(CORES, rows // CORES, p_size, width)
    keep = lax.dynamic_index_in_dim(share, core, 0, keepdims=False)
    give = lax.dynamic_index_in_dim(share, 1 - core, 0, keepdims=False)
    take = lax.ppermute(give, "core", swap)
    first = core == 0
    return jnp.stack([jnp.where(first, keep, take), jnp.where(first, take, keep)])


def solution(mesh):
    op_count, sec_count = mesh.shape["op"], mesh.shape["sec"]
    split = Mesh(
        mesh.devices.reshape(op_count, sec_count // CORES, CORES), ("op", "z", "core")
    )
    placed = (
        P("op", None, None, None),
        P(),
        P(None, ("op", "z", "core"), None, None),
        P("op", None, ("z", "core"), None, None),
        P(),
    )
    return jax.shard_map(
        shards, mesh=split, in_specs=placed,
        out_specs=P("op", ("z", "core"), None, None), check_vma=False,
    )
```

time: 93.2 us -> 84.4 us (0.906)
  waiting for transfers between devices: 58.6 us -> 38.7 us
  Pallas kernels: 16.5 us -> 25 us
  local copies, waits for them, and re-layouts: 1.1 us -> 3.23 us
    all_to_all x1, waiting for transfers between devices: 52.7 us -> 33.9 us  [shards(): lax.all_to_all(left_ops[:, 0], ('op', 'core'), split_axis=0, concat_axis=...]
    pallas_call x1 -> x2, Pallas kernels: 16.5 us -> 25 us  [the longest x1 16.7 us: right_call(): pl.pallas_call(functools.partial(right_kernel, GROUP), grid_spec=pltpu.Pr...]
    unnamed x6 -> x8, local copies, waits for them, and re-layouts: 0.01 us -> 2.2 us
    ppermute x3, waiting for transfers between devices: 4.74 us -> 3.53 us  [shards(): total = total + lax.ppermute(parts[shift], 'z', ring).astype(jnp.float32)]
  transfers between devices with their start and end apart: 6 -> 6, of which waited for: 4 -> 5; matrix products, arithmetic and copies ran while one was open for 2% -> 2% of each run, Pallas kernels for 0% -> 20%
where the time goes in v2:
time: 84.4 us; the launch traced here: 83.9 us
  waiting for transfers between devices  38.7 us (46%)
  Pallas kernels  25 us (30%)
  starting transfers between devices  15.1 us (18%)
  local copies, waits for them, and re-layouts  3.23 us (4%)
  other arithmetic  1.75 us (2%)
    all_to_all x1, waiting for transfers between devices, shards(): lax.all_to_all(left_ops[:, 0], ('op', 'core'), split_axis=0, concat_axis=...  33.9 us
    pallas_call x1, Pallas kernels, right_call(): pl.pallas_call(functools.partial(right_kernel, GROUP), grid_spec=pltpu.Pr...  16.7 us
    pallas_call x1, Pallas kernels, left_call(): pl.pallas_call(functools.partial(left_kernel, z_count, p_size), in_specs=...  8.33 us
    all_to_all x1, starting transfers between devices, shards(): lax.all_to_all(left_ops[:, 0], ('op', 'core'), split_axis=0, concat_axis=...  7.81 us
    ppermute x3, starting transfers between devices, shards(): total = total + lax.ppermute(parts[shift], 'z', ring).astype(jnp.float32)  7.19 us
    ppermute x3, waiting for transfers between devices, shards(): total = total + lax.ppermute(parts[shift], 'z', ring).astype(jnp.float32)  3.53 us
    unnamed x8, local copies, waits for them, and re-layouts  2.2 us
  transfers between devices with their start and end apart: 6, of which 5 were waited for; matrix products, arithmetic and copies ran while one was open for 2% of the time, Pallas kernels for 20%

profile of v2, /device:TPU:8, one launch (start us, length us, event | category | flops | bytes accessed | tf_op | source)
XLA Modules:
  0.0 83.9 jit_solution(16400609158559525627)
XLA Ops:
  0.0 0.0 copy-start
  0.0 0.0 collective-permute-start
  0.0 0.0 copy-start.2
  0.0 0.0 copy-start.3
  0.0 7.8 %all-to-all-start = ((bf16[32,256,256]{2,1,0:T(8,128)(2,1)}), bf16[32,256,256]{2,1,0:T(8,128)(2,1)}, u32[]{:S(2)}, u32[]{:S(2)}) async-start(bf16[32,256,256]{2,1,0:T(8,128)(2,1)} %bitcast.29), calls=%async_computation | async-start | bytes 8388608 | tf_op jit(solution)/shard_map/all_to_all | solution.py:145
  7.9 0.0 copy-done.2
  7.9 0.1 copy.11.site_ref
  8.0 0.0 copy-done.3
  8.0 0.6 dynamic_slice.18
  8.6 0.1 pad_add_fusion.meta
  8.6 0.6 compare_convert_fusion
  9.2 0.0 copy-done
  9.2 0.2 constant_dynamic-slice_fusion.2
  9.4 0.2 fusion.2.wave_ref
  9.6 0.0 collective-permute-done.other_ref
  9.6 0.0 copy-start.1
  9.6 2.2 %copy-done.1 = bf16[2,16,1,256,256]{4,3,2,1,0:T(8,128)(2,1)S(1)} copy-done((bf16[2,16,1,256,256]{4,3,2,1,0:T(8,128)(2,1)S(1)}, bf16[2,16,1,256,256]{4,3,2,1,0:T(8,128)(2,1)}, u32[]{:S(2)}) %copy-start.1) | copy-done | bytes 4194328
  11.8 16.7 %right_terms.1.held_hbm = bf16[32,256,1024]{2,1,0:T(8,128)(2,1)} custom-call(s32[3]{0:T(128)S(1)} %pad_add_fusion.meta, f32[128,16]{1,0:T(8,128)S(1)} %copy.11.site_ref, bf16[4,256,256]{2,1,0:T(8,128)(2,1)S(1)} %fusion.2.wave_ref, bf16[2,16,1,256,256]{4,3,2,1,0:T(8,128)(2,1)S(1)} %copy-done.1, bf16[2,16,1,256,256]{4,3,2,1,0:T(8,128)(2,1)} %collective-permute-done.other_ref), custom_call_target="tpu_custom_call" | custom-call | tf_op jit(solution)/shard_map/right_terms/pallas_call | solution.py:51
  28.5 33.9 %all-to-all-done.left_hbm = bf16[32,256,256]{2,1,0:T(8,128)(2,1)} async-done(((bf16[32,256,256]{2,1,0:T(8,128)(2,1)}), bf16[32,256,256]{2,1,0:T(8,128)(2,1)}, u32[]{:S(2)}, u32[]{:S(2)}) %all-to-all-start) | async-done | bytes 4194336 | tf_op jit(solution)/shard_map/all_to_all | solution.py:145
  62.4 8.3 %left_terms.1 = (f32[4,64,256]{2,1,0:T(8,128)S(1)}, bf16[4,64,256]{2,1,0:T(8,128)(2,1)S(1)}, bf16[4,64,256]{2,1,0:T(8,128)(2,1)S(1)}, bf16[4,64,256]{2,1,0:T(8,128)(2,1)S(1)}) custom-call(s32[3]{0:T(128)S(1)} %pad_add_fusion.meta, bf16[32,256,256]{2,1,0:T(8,128)(2,1)} %all-to-all-done.left_hbm, bf16[32,256,1024]{2,1,0:T(8,128)(2,1)} %right_terms.1.held_hbm), custom_call_target="tpu_custom_call" | custom-call | tf_op jit(solution)/shard_map/left_terms/pallas_call | solution.py:114
  70.7 4.0 %collective-permute-start.1 = (bf16[4,64,256]{2,1,0:T(8,128)(2,1)S(1)}, bf16[4,64,256]{2,1,0:T(8,128)(2,1)S(1)}, u32[]{:S(2)}, u32[]{:S(2)}) collective-permute-start(bf16[4,64,256]{2,1,0:T(8,128)(2,1)S(1)} %get-tuple-element.10), channel_id=1, source_target_pairs={{0,4},{2,6},{4,0},{6,2},{1,5},{3,7},{5,1},{7,3},{8,12},{10,14},{12... | collective-permute-start | bytes 393224 | tf_op jit(solution)/shard_map/ppermute | solution.py:161
  74.7 1.0 %collective-permute-start.2 = (bf16[4,64,256]{2,1,0:T(8,128)(2,1)S(1)}, bf16[4,64,256]{2,1,0:T(8,128)(2,1)S(1)}, u32[]{:S(2)}, u32[]{:S(2)}) collective-permute-start(bf16[4,64,256]{2,1,0:T(8,128)(2,1)S(1)} %get-tuple-element.11), channel_id=1, source_target_pairs={{0,2},{2,4},{4,6},{6,0},{1,3},{3,5},{5,7},{7,1},{8,10},{10,12},{12... | collective-permute-start | bytes 393224 | tf_op jit(solution)/shard_map/ppermute | solution.py:161
  75.7 2.2 %collective-permute-start.3 = (bf16[4,64,256]{2,1,0:T(8,128)(2,1)S(1)}, bf16[4,64,256]{2,1,0:T(8,128)(2,1)S(1)}, u32[]{:S(2)}, u32[]{:S(2)}) collective-permute-start(bf16[4,64,256]{2,1,0:T(8,128)(2,1)S(1)} %get-tuple-element.12), channel_id=1, source_target_pairs={{0,6},{2,0},{4,2},{6,4},{1,7},{3,1},{5,3},{7,5},{8,14},{10,8},{12,... | collective-permute-start | bytes 393224 | tf_op jit(solution)/shard_map/ppermute | solution.py:161
  77.9 0.1 dynamic_slice.19
  78.0 1.0 %collective-permute-done.1 = bf16[4,64,256]{2,1,0:T(8,128)(2,1)S(1)} collective-permute-done((bf16[4,64,256]{2,1,0:T(8,128)(2,1)S(1)}, bf16[4,64,256]{2,1,0:T(8,128)(2,1)S(1)}, u32[]{:S(2)}, u32[]{:S(2)}) %collective-permute-start.1) | collective-permute-done | bytes 131104 | tf_op jit(solution)/shard_map/ppermute | solution.py:161
  79.0 2.2 %collective-permute-done.2 = bf16[4,64,256]{2,1,0:T(8,128)(2,1)S(1)} collective-permute-done((bf16[4,64,256]{2,1,0:T(8,128)(2,1)S(1)}, bf16[4,64,256]{2,1,0:T(8,128)(2,1)S(1)}, u32[]{:S(2)}, u32[]{:S(2)}) %collective-permute-start.2) | collective-permute-done | bytes 131104 | tf_op jit(solution)/shard_map/ppermute | solution.py:161
  81.3 0.3 collective-permute-done.3
  81.5 0.1 multiply_convert_fusion
  81.7 0.1 copy.21
  81.7 0.1 collective-permute-start.4
  81.8 1.2 %collective-permute-done.4 = bf16[32,4,256]{2,1,0:T(4,128)(2,1)S(1)} collective-permute-done((bf16[32,4,256]{2,1,0:T(4,128)(2,1)S(1)}, bf16[32,4,256]{2,1,0:T(4,128)(2,1)S(1)}, u32[]{:S(2)}, u32[]{:S(2)}) %collective-permute-start.4) | collective-permute-done | bytes 65568 | tf_op jit(solution)/shard_map/ppermute | solution.py:169
  83.0 0.1 fusion.3
  83.1 0.7 pad_maximum_fusion
  (1 shorter events, 0.0 us)
Async XLA Ops:
  0.0 9.2 %copy-start = (bf16[2,256,4,256]{3,2,1,0:T(4,128)(2,1)S(1)}, bf16[2,256,4,256]{3,2,1,0:T(4,128)(2,1)}, u32[]{:S(2)}) copy-start(bf16[2,256,4,256]{3,2,1,0:T(4,128)(2,1)} %param.5) | copy-start | bytes 3145732
  0.0 9.6 %collective-permute-start = (bf16[2,16,1,256,256]{4,3,2,1,0:T(8,128)(2,1)}, bf16[2,16,1,256,256]{4,3,2,1,0:T(8,128)(2,1)}, u32[]{:S(2)}, u32[]{:S(2)}) collective-permute-start(bf16[2,16,1,256,256]{4,3,2,1,0:T(8,128)(2,1)} %own_ref.1), channel_id=1, source_target_pairs={{0,1},{1,0},{2,3},{3,2},{4,5},{5,4},{6,7},{7,6},{8,9},{9,8},{10,11... | collective-permute-start | bytes 12582920 | tf_op jit(solution)/shard_map/ppermute | solution.py:144
  0.0 7.9 %copy-start.2 = (f32[128,4,4]{0,2,1:T(4,128)S(1)}, f32[128,4,4]{0,2,1:T(4,128)}, u32[]{:S(2)}) copy-start(f32[128,4,4]{0,2,1:T(4,128)} %param.9) | copy-start | bytes 24580
  0.0 8.0 %copy-start.3 = (s32[32]{0:T(128)S(1)}, s32[32]{0:T(128)}, u32[]{:S(2)}) copy-start(s32[32]{0:T(128)} %param.6) | copy-start | bytes 388
  0.0 62.4 %all-to-all-start = ((bf16[32,256,256]{2,1,0:T(8,128)(2,1)}), bf16[32,256,256]{2,1,0:T(8,128)(2,1)}, u32[]{:S(2)}, u32[]{:S(2)}) async-start(bf16[32,256,256]{2,1,0:T(8,128)(2,1)} %bitcast.29), calls=%async_computation | async-start | bytes 8388608 | tf_op jit(solution)/shard_map/all_to_all | solution.py:145
  9.6 2.2 %copy-start.1 = (bf16[2,16,1,256,256]{4,3,2,1,0:T(8,128)(2,1)S(1)}, bf16[2,16,1,256,256]{4,3,2,1,0:T(8,128)(2,1)}, u32[]{:S(2)}) copy-start(bf16[2,16,1,256,256]{4,3,2,1,0:T(8,128)(2,1)} %own_ref.1) | copy-start | bytes 12582916
  70.7 8.3 %collective-permute-start.1 = (bf16[4,64,256]{2,1,0:T(8,128)(2,1)S(1)}, bf16[4,64,256]{2,1,0:T(8,128)(2,1)S(1)}, u32[]{:S(2)}, u32[]{:S(2)}) collective-permute-start(bf16[4,64,256]{2,1,0:T(8,128)(2,1)S(1)} %get-tuple-element.10), channel_id=1, source_target_pairs={{0,4},{2,6},{4,0},{6,2},{1,5},{3,7},{5,1},{7,3},{8,12},{10,14},{12... | collective-permute-start | bytes 393224 | tf_op jit(solution)/shard_map/ppermute | solution.py:161
  74.7 6.6 %collective-permute-start.2 = (bf16[4,64,256]{2,1,0:T(8,128)(2,1)S(1)}, bf16[4,64,256]{2,1,0:T(8,128)(2,1)S(1)}, u32[]{:S(2)}, u32[]{:S(2)}) collective-permute-start(bf16[4,64,256]{2,1,0:T(8,128)(2,1)S(1)} %get-tuple-element.11), channel_id=1, source_target_pairs={{0,2},{2,4},{4,6},{6,0},{1,3},{3,5},{5,7},{7,1},{8,10},{10,12},{12... | collective-permute-start | bytes 393224 | tf_op jit(solution)/shard_map/ppermute | solution.py:161
  75.7 5.8 %collective-permute-start.3 = (bf16[4,64,256]{2,1,0:T(8,128)(2,1)S(1)}, bf16[4,64,256]{2,1,0:T(8,128)(2,1)S(1)}, u32[]{:S(2)}, u32[]{:S(2)}) collective-permute-start(bf16[4,64,256]{2,1,0:T(8,128)(2,1)S(1)} %get-tuple-element.12), channel_id=1, source_target_pairs={{0,6},{2,0},{4,2},{6,4},{1,7},{3,1},{5,3},{7,5},{8,14},{10,8},{12,... | collective-permute-start | bytes 393224 | tf_op jit(solution)/shard_map/ppermute | solution.py:161
  81.7 1.3 %collective-permute-start.4 = (bf16[32,4,256]{2,1,0:T(4,128)(2,1)S(1)}, bf16[32,4,256]{2,1,0:T(4,128)(2,1)S(1)}, u32[]{:S(2)}, u32[]{:S(2)}) collective-permute-start(bf16[32,4,256]{2,1,0:T(4,128)(2,1)S(1)} %bitcast.31), channel_id=1, source_target_pairs={{0,1},{1,0},{2,3},{3,2},{4,5},{5,4},{6,7},{7,6},{8,9},{9,8},{10,11... | collective-permute-start | bytes 196616 | tf_op jit(solution)/shard_map/ppermute | solution.py:169

commit v3 on v0

v3 whole, which is shorter than its diff:
```python
import functools
import math

import jax
import jax.numpy as jnp
from jax import lax
from jax.experimental import pallas as pl
from jax.experimental.pallas import tpu as pltpu
from jax.sharding import Mesh, PartitionSpec as P

CORES = 2
ROWS = 16
STEP_TERMS = 2
VMEM_LIMIT = 16 << 20
IN_VMEM = pl.BlockSpec(memory_space=pltpu.VMEM)
IN_SMEM = pl.BlockSpec(memory_space=pltpu.SMEM)


def right_kernel(count, first_term, meta, site_ref, wave_ref, *refs):
    rights, held_ref, first = refs[:count], refs[count], refs[count + 1]
    step = pl.program_id(0)
    p_size, width = wave_ref.shape[1], wave_ref.shape[2]
    waves = wave_ref[0].reshape(p_size * width, width)
    for at in range(count):
        term = meta[1] + meta[2] * meta[3 + first_term + step * count + at]
        first[at] = lax.dot_general(
            waves, rights[at][0, 0, 0], (((1,), (1,)), ((), ())),
            preferred_element_type=jnp.float32,
        )
        scale = [[site_ref[term, q * p_size + p] for p in range(p_size)] for q in range(p_size)]
        for low in range(0, width, ROWS):
            parts = [first[at, p * width + low : p * width + low + ROWS] for p in range(p_size)]
            for q in range(p_size):
                second = parts[0] * scale[q][0]
                for p in range(1, p_size):
                    second = second + parts[p] * scale[q][p]
                held_ref[at, low : low + ROWS, q * width : (q + 1) * width] = second.astype(
                    jnp.bfloat16
                )


def right_call(meta, site, wave, right, sector, first_term, terms):
    width, p_size = right.shape[-1], wave.shape[1]
    count = STEP_TERMS

    def right_at(at, step, meta):
        return sector, meta[3 + first_term + step * count + at], 0, 0, 0

    return pl.pallas_call(
        functools.partial(right_kernel, count, first_term),
        grid_spec=pltpu.PrefetchScalarGridSpec(
            num_scalar_prefetch=1,
            grid=(terms // count,),
            in_specs=[
                IN_SMEM,
                pl.BlockSpec((1, p_size, width, width), lambda step, meta: (sector, 0, 0, 0)),
            ]
            + [
                pl.BlockSpec((1, 1, 1, width, width), functools.partial(right_at, at))
                for at in range(count)
            ],
            out_specs=pl.BlockSpec(
                (count, width, p_size * width), lambda step, meta: (step, 0, 0)
            ),
            scratch_shapes=[pltpu.VMEM((count, p_size * width, width), jnp.float32)],
        ),
        out_shape=jax.ShapeDtypeStruct((terms, width, p_size * width), jnp.bfloat16),
        compiler_params=pltpu.CompilerParams(vmem_limit_bytes=VMEM_LIMIT),
        name="right_terms",
    )(meta, site, wave, *[right] * count)


def left_sum(blocks, helds, places):
    add = None
    for block, block_at, held, held_at in places:
        product = jnp.dot(
            blocks[block][block_at], helds[held][held_at], preferred_element_type=jnp.float32
        )
        add = product if add is None else add + product
    return add


def start_kernel(n_blocks, n_helds, places, *refs):
    blocks, helds = refs[:n_blocks], refs[n_blocks : n_blocks + n_helds]
    refs[-1][...] = left_sum(blocks, helds, places)


def finish_kernel(n_blocks, n_helds, places, z_count, p_size, meta, total_ref, *refs):
    blocks, helds = refs[:n_blocks], refs[n_blocks : n_blocks + n_helds]
    keep_ref, give_ref, total = refs[n_blocks + n_helds :]
    total[...] = total_ref[...] + left_sum(blocks, helds, places)
    width = total.shape[0]
    rows = width // (z_count * CORES)
    for shift in range(z_count):
        z_to = lax.rem(meta[0] + shift, z_count)
        for out, core in ((keep_ref, meta[1] % CORES), (give_ref, 1 - meta[1] % CORES)):
            start = pl.multiple_of((z_to * CORES + core) * rows, rows)
            block = total[pl.ds(start, rows), :]
            for q in range(p_size):
                out[shift, q] = block[:, q * width : (q + 1) * width].astype(out.dtype)


def join_kernel(keep_ref, take_ref, *outs):
    for shift, out in enumerate(outs):
        out[...] = (keep_ref[shift] + take_ref[shift].astype(jnp.float32)).astype(out.dtype)


def left_start(blocks, helds, places):
    width, columns = helds[0].shape[1:]
    return pl.pallas_call(
        functools.partial(start_kernel, len(blocks), len(helds), places),
        in_specs=[IN_VMEM] * (len(blocks) + len(helds)),
        out_specs=IN_VMEM,
        out_shape=jax.ShapeDtypeStruct((width, columns), jnp.float32),
        compiler_params=pltpu.CompilerParams(vmem_limit_bytes=VMEM_LIMIT),
        name="left_start",
    )(*blocks, *helds)


def left_finish(meta, total, blocks, helds, places, z_count):
    width, columns = helds[0].shape[1:]
    p_size = columns // width
    shape = (z_count, p_size, width // (z_count * CORES), width)
    return pl.pallas_call(
        functools.partial(finish_kernel, len(blocks), len(helds), places, z_count, p_size),
        in_specs=[IN_SMEM, IN_VMEM] + [IN_VMEM] * (len(blocks) + len(helds)),
        out_specs=[IN_VMEM, IN_VMEM],
        out_shape=[
            jax.ShapeDtypeStruct(shape, jnp.float32),
            jax.ShapeDtypeStruct(shape, jnp.bfloat16),
        ],
        scratch_shapes=[pltpu.VMEM((width, columns), jnp.float32)],
        compiler_params=pltpu.CompilerParams(vmem_limit_bytes=VMEM_LIMIT),
        name="left_finish",
    )(meta, total, *blocks, *helds)


def join_call(keep, take):
    z_count, shape = keep.shape[0], keep.shape[1:]
    return pl.pallas_call(
        join_kernel,
        in_specs=[IN_VMEM, IN_VMEM],
        out_specs=[IN_VMEM] * z_count,
        out_shape=[
            jax.ShapeDtypeStruct(shape, jnp.float32 if s == 0 else jnp.bfloat16)
            for s in range(z_count)
        ],
        compiler_params=pltpu.CompilerParams(vmem_limit_bytes=VMEM_LIMIT),
        name="join_cores",
    )(keep, take)


def shards(wave, sector_dims, left_ops, right_ops, site_ops):
    op_count, z_count = lax.axis_size("op"), lax.axis_size("z")
    side = math.isqrt(op_count)
    op_at, z_at, core = lax.axis_index("op"), lax.axis_index("z"), lax.axis_index("core")
    sectors, width, p_size = wave.shape[0], wave.shape[1], wave.shape[2]
    swap = [(0, 1), (1, 0)]

    x_at, y_at = op_at // side, op_at % side
    near_at, far_at = jnp.where(core == 0, x_at, y_at), jnp.where(core == 0, y_at, x_at)

    def place(near, far):
        near, far = near % side, far % side
        return jnp.where(core == 0, near * side + far, far * side + near)

    def ring(shift, first):
        pairs = []
        for op in range(op_count):
            for c in range(CORES):
                x, y = op // side, op % side
                if (c == 0) == first:
                    x = (x + shift) % side
                else:
                    y = (y + shift) % side
                pairs.append((op * CORES + c, (x * side + y) * CORES + c))
        return pairs

    order = [0] + sorted(range(1, side), key=lambda s: min(s, side - s))
    last = order[-1]
    left = left_ops.reshape(left_ops.shape[0], width, width)
    sent = [[None] * side for _ in range(sectors)]
    for sector in range(sectors):
        for shift in order:
            sent[sector][shift] = jnp.concatenate(
                [
                    lax.dynamic_slice_in_dim(
                        left, place(near_at + shift, far_at + turn) * sectors + sector, 1
                    )
                    for turn in range(side)
                ]
            )
    arrived = [[None] * side for _ in range(sectors)]
    forwarded = [[None] * side for _ in range(sectors)]
    for sector in range(sectors):
        arrived[sector][0] = sent[sector][0]
        for shift in order[1:]:
            arrived[sector][shift] = lax.ppermute(
                sent[sector][shift], ("op", "core"), ring(shift, True)
            )
        for turn in order[1:]:
            forwarded[sector][turn] = lax.ppermute(
                jnp.stack([arrived[sector][shift][turn] for shift in range(side)]),
                ("op", "core"),
                ring(turn, False),
            )

    sizes = lax.dynamic_slice_in_dim(sector_dims, op_at * sectors, sectors)
    mask = (lax.broadcasted_iota(jnp.int32, (sectors, width), 1) < sizes[:, None]).astype(
        jnp.float32
    )
    masked = wave.astype(jnp.float32) * mask[:, :, None, None] * mask[:, None, None, :]
    masked = masked.astype(jnp.bfloat16).transpose(0, 2, 1, 3)
    site = site_ops.reshape(site_ops.shape[0], -1)
    sources = [place(near_at - shift, far_at - turn) for turn in range(side) for shift in range(side)]
    meta = jnp.stack(
        [z_at, z_at * CORES + core, jnp.int32(z_count * CORES)] + sources
    ).astype(jnp.int32)

    rows = width // (z_count * CORES)
    own_rows = (z_at * CORES + core) * rows
    shares = []
    for sector in range(sectors):
        half = side // 2 * side
        helds = [
            right_call(meta, site, masked, right_ops, sector, part * half, half)
            for part in range(2)
        ]

        def held_place(turn, shift):
            at = turn * side + shift
            return at // half, at % half

        early = [(shift, 0, *held_place(0, shift)) for shift in range(side)]
        blocks = list(arrived[sector])
        for turn in order[1:-1]:
            early += [(len(blocks), shift, *held_place(turn, shift)) for shift in range(side)]
            blocks.append(forwarded[sector][turn])
        total = left_start(blocks, helds, early)
        held_at = held_place(last, 0)
        late = [(0, shift, 0, held_at[1] + shift) for shift in range(side)]
        keep, give = left_finish(
            meta, total, [forwarded[sector][last]], [helds[held_at[0]]], late, z_count
        )
        parts = join_call(keep, lax.ppermute(give, "core", swap))
        summed = parts[0]
        for shift in sorted(range(1, z_count), key=lambda s: -min(s, z_count - s)):
            z_ring = [(z, (z + shift) % z_count) for z in range(z_count)]
            summed = summed + lax.ppermute(parts[shift], "z", z_ring).astype(jnp.float32)
        row_mask = lax.dynamic_slice_in_dim(mask[sector], own_rows, rows)
        share = summed * row_mask[None, :, None] * mask[sector][None, None, :]
        shares.append(share.astype(jnp.bfloat16).transpose(1, 0, 2))
    return jnp.stack(shares)


def solution(mesh):
    op_count, sec_count = mesh.shape["op"], mesh.shape["sec"]
    split = Mesh(
        mesh.devices.reshape(op_count, sec_count // CORES, CORES), ("op", "z", "core")
    )
    placed = (
        P("op", None, None, None),
        P(),
        P(None, ("op", "z", "core"), None, None),
        P("op", None, ("z", "core"), None, None),
        P(),
    )
    return jax.shard_map(
        shards, mesh=split, in_specs=placed,
        out_specs=P("op", ("z", "core"), None, None), check_vma=False,
    )
```

time: 556 us -> 115 us (0.21)
  blocking collectives: 191 us -> 0 us
  waiting for transfers between devices: 181 us -> 26.8 us
  matrix products: 134 us -> 0 us
  Pallas kernels: 0 us -> 31.6 us
  starting transfers between devices: 0.04 us -> 28.5 us
  local copies, waits for them, and re-layouts: 31.5 us -> 18.4 us
  between operations: 13.4 us -> 0.44 us
    all_to_all x1 -> x0, blocking collectives: 191 us -> none  [shards(): inter = lax.all_to_all(inter, 'op', split_axis=0, concat_axis=1, tiled=True)]
    dot_general x65 -> x0, matrix products: 134 us -> none  [the longest x32 79.6 us: one_sector(): jnp.einsum('klpr,kqp->klqr', first, site_mats, precision=lax.Precision.HI...]
    all_gather x1 -> x0, waiting for transfers between devices: 113 us -> none  [shards(): lax.all_gather(masked, 'op', axis=0, tiled=True)]
    psum x1 -> x0, waiting for transfers between devices: 67.5 us -> none  [shards(): summed = lax.psum(partial_sum, 'sec')]
    pallas_call x0 -> x10, Pallas kernels: none -> 31.6 us  [the longest x4 22.7 us: right_call(): pl.pallas_call(functools.partial(right_kernel, count, first_term), grid_s...]
    ppermute x0 -> x20, starting transfers between devices: none -> 28.5 us  [the longest x6 10.6 us: shards(): lax.ppermute(parts[shift], 'z', z_ring).astype(jnp.float32)]
    dynamic_update_slice x32 -> x0, local copies, waits for them, and re-layouts: 28.2 us -> none  [left_step(): return lax.map(one_sector, (blocks, waves))]
    ppermute x0 -> x20, waiting for transfers between devices: none -> 26.8 us  [the longest x6 24 us: shards(): lax.ppermute(sent[sector][shift], ('op', 'core'), ring(shift, True))]
  transfers between devices with their start and end apart: 2 -> 20, of which waited for: 2 -> 4; matrix products, arithmetic and copies ran while one was open for 0% -> 10% of each run, Pallas kernels for 0% -> 28%
where the time goes in v3:
time: 115 us
  Pallas kernels  31.6 us (27%)
  starting transfers between devices  28.5 us (25%)
  waiting for transfers between devices  26.8 us (23%)
  local copies, waits for them, and re-layouts  18.4 us (16%)
  other arithmetic  8.83 us (8%)
    ppermute x6, waiting for transfers between devices, shards(): lax.ppermute(sent[sector][shift], ('op', 'core'), ring(shift, True))  24 us
    pallas_call x4, Pallas kernels, right_call(): pl.pallas_call(functools.partial(right_kernel, count, first_term), grid_s...  22.7 us
    unnamed x44, local copies, waits for them, and re-layouts  12.1 us
    ppermute x6, starting transfers between devices, shards(): lax.ppermute(parts[shift], 'z', z_ring).astype(jnp.float32)  10.6 us
    ppermute x6, starting transfers between devices, shards(): lax.ppermute(sent[sector][shift], ('op', 'core'), ring(shift, True))  9.67 us
    ppermute x6, starting transfers between devices, shards(): lax.ppermute(jnp.stack([arrived[sector][shift][turn] for shift in range(s...  7.65 us
    concatenate x6, other arithmetic, shards(): jnp.concatenate([lax.dynamic_slice_in_dim(left, place(near_at + shift, fa...  5.36 us
    dynamic_slice x2, local copies, waits for them, and re-layouts, shards(): lax.dynamic_slice_in_dim(left, place(near_at + shift, far_at + turn) * se...  4.98 us
  transfers between devices with their start and end apart: 20, of which 4 were waited for; matrix products, arithmetic and copies ran while one was open for 10% of the time, Pallas kernels for 28%

profile of v3, /device:TPU:8, one launch (start us, length us, event | category | flops | bytes accessed | tf_op | source)
XLA Modules:
  0.0 114.6 jit_solution(12241568148549559216)
XLA Ops:
  0.0 2.6 %dynamic-slice_bitcast_fusion.19 = (bf16[1,256,256]{2,1,0:T(8,128)(2,1)S(1)}, bf16[1,256,256]{2,1,0:T(8,128)(2,1)}, bf16[1,256,256]{2,1,0:T(8,128)(2,1)}, bf16[1...) fusion(bf16[32,1,256,256]{3,2,1,0:T(8,128)(2,1)} %param.7, ...), kind=kLoop, calls=%fused_computation.38 | loop fusion | bytes 4718664 | tf_op jit(solution)/shard_map/dynamic_slice | solution.py:187
  2.6 0.1 pad_maximum_fusion.3
  2.7 2.8 %collective-permute-start.2 = (bf16[4,256,256]{2,1,0:T(8,128)(2,1)S(1)}, bf16[4,256,256]{2,1,0:T(8,128)(2,1)S(1)}, u32[]{:S(2)}, u32[]{:S(2)}) collective-permute-start(bf16[4,256,256]{2,1,0:T(8,128)(2,1)S(1)} %pad_maximum_fusion.3), channel_id=1, source_target_pairs={{0,96},{1,25},{8,104},{9,1},{16,112},{17,9},{24,120},{25,17},{32,0... | collective-permute-start | bytes 1572872 | tf_op jit(solution)/shard_map/ppermute | solution.py:198
  5.5 2.3 %dynamic-slice_bitcast_fusion.23 = (bf16[1,256,256]{2,1,0:T(8,128)(2,1)S(1)}, bf16[1,256,256]{2,1,0:T(8,128)(2,1)S(1)}, bf16[1,256,256]{2,1,0:T(8,128)(2,1)S(1)}...) fusion(bf16[32,1,256,256]{3,2,1,0:T(8,128)(2,1)} %param.7, ...), kind=kLoop, calls=%fused_computation.42 | loop fusion | bytes 3670072 | tf_op jit(solution)/shard_map/dynamic_slice | solution.py:187
  7.9 0.9 pad_maximum_fusion.1
  8.7 0.0 collective-permute-start
  8.8 0.9 pad_maximum_fusion.2
  9.6 2.3 %collective-permute-start.1 = (bf16[4,256,256]{2,1,0:T(8,128)(2,1)}, bf16[4,256,256]{2,1,0:T(8,128)(2,1)S(1)}, u32[]{:S(2)}, u32[]{:S(2)}) collective-permute-start(bf16[4,256,256]{2,1,0:T(8,128)(2,1)} %pad_maximum_fusion.2), channel_id=1, source_target_pairs={{0,64},{1,17},{8,72},{9,25},{16,80},{17,1},{24,88},{25,9},{32,96},... | collective-permute-start | bytes 1572872 | tf_op jit(solution)/shard_map/ppermute | solution.py:198
  11.9 0.9 pad_maximum_fusion.8
  12.8 1.8 %collective-permute-start.10 = (bf16[4,256,256]{2,1,0:T(8,128)(2,1)}, bf16[4,256,256]{2,1,0:T(8,128)(2,1)S(1)}, u32[]{:S(2)}, u32[]{:S(2)}) collective-permute-start(bf16[4,256,256]{2,1,0:T(8,128)(2,1)} %pad_maximum_fusion.8), channel_id=1, source_target_pairs={{0,32},{1,9},{8,40},{9,17},{16,48},{17,25},{24,56},{25,1},{32,64},... | collective-permute-start | bytes 1572872 | tf_op jit(solution)/shard_map/ppermute | solution.py:198
  14.6 0.9 pad_maximum_fusion.9
  15.4 0.8 collective-permute-start.11
  16.2 1.8 %pad_maximum_fusion.10 = bf16[4,256,256]{2,1,0:T(8,128)(2,1)} fusion(bf16[1,256,256]{2,1,0:T(8,128)(2,1)S(1)} %get-tuple-element.59, bf16[1,256,256]{2,1,0:T(8,128)(2,1)S(1)} %get-tuple-element.60, bf16[1,256,256]{2,1,0:T(8,128)(2,1)} %get-tuple-element.30, bf16[1,256,256]{2,1,0:T(8,128)(2,1)} %get-tuple-element.31), kind=kLoop, calls=%fused_computation.12 | loop fusion | flops 786432 | bytes 1048576 | tf_op jit(solution)/shard_map/concatenate | solution.py:185
  18.1 0.1 copy.10.site_ref
  18.2 0.1 dynamic_slice.201
  18.3 0.1 stack.102.meta
  18.5 1.9 %collective-permute-start.12 = (bf16[4,256,256]{2,1,0:T(8,128)(2,1)}, bf16[4,256,256]{2,1,0:T(8,128)(2,1)S(1)}, u32[]{:S(2)}, u32[]{:S(2)}) collective-permute-start(bf16[4,256,256]{2,1,0:T(8,128)(2,1)} %pad_maximum_fusion.10), channel_id=1, source_target_pairs={{0,96},{1,25},{8,104},{9,1},{16,112},{17,9},{24,120},{25,17},{32,0... | collective-permute-start | bytes 1572872 | tf_op jit(solution)/shard_map/ppermute | solution.py:198
  20.4 5.3 %collective-permute-done.refs_1_ = bf16[4,256,256]{2,1,0:T(8,128)(2,1)S(1)} collective-permute-done((bf16[4,256,256]{2,1,0:T(8,128)(2,1)}, bf16[4,256,256]{2,1,0:T(8,128)(2,1)S(1)}, u32[]{:S(2)}, u32[]{:S(2)}) %collective-permute-start) | collective-permute-done | bytes 524320 | tf_op jit(solution)/shard_map/ppermute | solution.py:198
  25.8 0.0 collective-permute-done.1.refs_2_
  25.8 0.0 copy-start.15
  25.8 1.6 %pad_maximum_fusion.6 = (bf16[4,256,256]{2,1,0:T(8,128)(2,1)S(1)}, bf16[4,256,256]{2,1,0:T(8,128)(2,1)S(1)}, bf16[4,256,256]{2,1,0:T(8,128)(2,1)S(1)}, bf16[4,256,256]{2,1,0:T(8,128)(2,1)S(1)}) fusion(bf16[1,256,256]{2,1,0:T(8,128)(2,1)S(1)} %get-tuple-element.67, bf16[1,256,256]{2,1,0:T(8,128)(2,1)S(1)} %get-tuple-element.64, ...), kind=kLoop, calls=%fused_computation.8 | loop fusion | flops 3145728 | bytes 3801088 | tf_op jit(solution)/shard_map/stack | solution.py:203
  27.5 0.0 copy-start
  27.5 0.9 collective-permute-start.3
  28.4 1.2 %collective-permute-start.4 = (bf16[4,256,256]{2,1,0:T(8,128)(2,1)S(1)}, bf16[4,256,256]{2,1,0:T(8,128)(2,1)S(1)}, u32[]{:S(2)}, u32[]{:S(2)}) collective-permute-start(bf16[4,256,256]{2,1,0:T(8,128)(2,1)S(1)} %get-tuple-element.81), channel_id=1, source_target_pairs={{0,24},{1,97},{8,0},{9,105},{16,8},{17,113},{24,16},{25,121},{32,5... | collective-permute-start | bytes 1572872 | tf_op jit(solution)/shard_map/ppermute | solution.py:202
  29.6 18.6 %collective-permute-done.10.refs_1_ = bf16[4,256,256]{2,1,0:T(8,128)(2,1)S(1)} collective-permute-done((bf16[4,256,256]{2,1,0:T(8,128)(2,1)}, bf16[4,256,256]{2,1,0:T(8,128)(2,1)S(1)}, u32[]{:S(2)}, u32[]{:S(2)}) %collective-permute-start.10) | collective-permute-done | bytes 524320 | tf_op jit(solution)/shard_map/ppermute | solution.py:198
  48.2 0.0 collective-permute-start.5
  48.3 0.0 collective-permute-done.11.refs_2_
  48.3 0.0 collective-permute-done.12.refs_3_
  48.4 0.8 copy-done.11
  49.1 1.3 %pad_maximum_fusion.13 = (bf16[4,256,256]{2,1,0:T(8,128)(2,1)}, bf16[4,256,256]{2,1,0:T(8,128)(2,1)S(1)}, bf16[4,256,256]{2,1,0:T(8,128)(2,1)}, bf16[4,256,256]{2,1,0:T(8,128)(2,1)}) fusion(bf16[1,256,256]{2,1,0:T(8,128)(2,1)S(1)} %get-tuple-element.76, bf16[1,256,256]{2,1,0:T(8,128)(2,1)S(1)} %get-tuple-element.73, ...), kind=kLoop, calls=%fused_computation.15 | loop fusion | flops 3145728 | bytes 3801088 | tf_op jit(solution)/shard_map/stack | solution.py:203
  50.4 0.0 collective-permute-start.13
  50.4 2.0 %collective-permute-start.14 = (bf16[4,256,256]{2,1,0:T(8,128)(2,1)}, bf16[4,256,256]{2,1,0:T(8,128)(2,1)}, u32[]{:S(2)}, u32[]{:S(2)}) collective-permute-start(bf16[4,256,256]{2,1,0:T(8,128)(2,1)} %get-tuple-element.85), channel_id=1, source_target_pairs={{0,24},{1,97},{8,0},{9,105},{16,8},{17,113},{24,16},{25,121},{32,5... | collective-permute-start | bytes 1572872 | tf_op jit(solution)/shard_map/ppermute | solution.py:202
  52.5 3.5 %collective-permute-start.15 = (bf16[4,256,256]{2,1,0:T(8,128)(2,1)}, bf16[4,256,256]{2,1,0:T(8,128)(2,1)}, u32[]{:S(2)}, u32[]{:S(2)}) collective-permute-start(bf16[4,256,256]{2,1,0:T(8,128)(2,1)} %get-tuple-element.83), channel_id=1, source_target_pairs={{0,16},{1,65},{8,24},{9,73},{16,0},{17,81},{24,8},{25,89},{32,48},... | collective-permute-start | bytes 1572872 | tf_op jit(solution)/shard_map/ppermute | solution.py:202
  56.0 0.1 compare_convert_fusion
  56.1 0.3 fusion.wave_ref
  56.4 5.7 %right_terms.4.refs_6_ = bf16[8,256,1024]{2,1,0:T(8,128)(2,1)S(1)} custom-call(s32[19]{0:T(128)S(1)} %stack.102.meta, f32[128,16]{1,0:T(8,128)S(1)} %copy.10.site_ref, bf16[2,4,256,256]{3,2,1,0:T(8,128)(2,1)S(1)} %fusion.wave_ref, bf16[2,16,1,256,256]{4,3,2,1,0:T(8,128)(2,1)S(1)} %copy-done, bf16[2,16,1,256,256]{4,3,2,1,0:T(8,128)(2,1)S(1)} %copy-done), custom_call_target="tpu_custom_call" | custom-call | tf_op jit(solution)/shard_map/right_terms/pallas_call | solution.py:49
  62.1 5.7 %right_terms.5.refs_7_.refs_1_ = bf16[8,256,1024]{2,1,0:T(8,128)(2,1)S(1)} custom-call(s32[19]{0:T(128)S(1)} %stack.102.meta, f32[128,16]{1,0:T(8,128)S(1)} %copy.10.site_ref, bf16[2,4,256,256]{3,2,1,0:T(8,128)(2,1)S(1)} %fusion.wave_ref, bf16[2,16,1,256,256]{4,3,2,1,0:T(8,128)(2,1)S(1)} %copy-done, bf16[2,16,1,256,256]{4,3,2,1,0:T(8,128)(2,1)S(1)} %copy-done), custom_call_target="tpu_custom_call" | custom-call | tf_op jit(solution)/shard_map/right_terms/pallas_call | solution.py:49
  67.8 1.8 %left_start.2.total_ref = f32[256,1024]{1,0:T(8,128)S(1)} custom-call(bf16[4,256,256]{2,1,0:T(8,128)(2,1)S(1)} %get-tuple-element.80.refs_0_, bf16[4,256,256]{2,1,0:T(8,128)(2,1)S(1)} %copy-done.8, bf16[4,256,256]{2,1,0:T(8,128)(2,1)S(1)} %copy-done.10, bf16[4,256,256]{2,1,0:T(8,128)(2,1)S(1)} %collective-permute-done.2.refs_3_, ...), custom_call_target="tpu_custom_call" | custom-call | tf_op jit(solution)/shard_map/left_start/pallas_call | solution.py:110
  69.6 2.0 %left_finish.2 = (f32[4,4,32,256]{3,2,1,0:T(8,128)S(1)}, bf16[4,4,32,256]{3,2,1,0:T(8,128)(2,1)}) custom-call(s32[19]{0:T(128)S(1)} %stack.102.meta, f32[256,1024]{1,0:T(8,128)S(1)} %left_start.2.total_ref, bf16[4,256,256]{2,1,0:T(8,128)(2,1)S(1)} %collective-permute-done.5.refs_0_, bf16[8,256,1024]{2,1,0:T(8,128)(2,1)S(1)} %right_terms.5.refs_7_.refs_1_), custom_call_target="tpu_custom_call" | custom-call | tf_op jit(solution)/shard_map/left_finish/pallas_call | solution.py:124
  71.6 0.8 copy-done.13
  72.4 0.0 collective-permute-start.6
  72.4 2.2 %copy-done.1 = bf16[2,16,1,256,256]{4,3,2,1,0:T(8,128)(2,1)S(1)} copy-done((bf16[2,16,1,256,256]{4,3,2,1,0:T(8,128)(2,1)S(1)}, bf16[2,16,1,256,256]{4,3,2,1,0:T(8,128)(2,1)}, u32[]{:S(2)}) %copy-start.1) | copy-done | bytes 4194328
  74.6 5.7 %right_terms.6.refs_6_ = bf16[8,256,1024]{2,1,0:T(8,128)(2,1)S(1)} custom-call(s32[19]{0:T(128)S(1)} %stack.102.meta, f32[128,16]{1,0:T(8,128)S(1)} %copy.10.site_ref, bf16[2,4,256,256]{3,2,1,0:T(8,128)(2,1)S(1)} %fusion.wave_ref, bf16[2,16,1,256,256]{4,3,2,1,0:T(8,128)(2,1)S(1)} %copy-done.1, bf16[2,16,1,256,256]{4,3,2,1,0:T(8,128)(2,1)S(1)} %copy-done.1), custom_call_target="tpu_custom_call" | custom-call | tf_op jit(solution)/shard_map/right_terms/pallas_call | solution.py:49
  80.2 2.0 %copy-done.5 = bf16[8,256,1024]{2,1,0:T(8,128)(2,1)} copy-done((bf16[8,256,1024]{2,1,0:T(8,128)(2,1)}, bf16[8,256,1024]{2,1,0:T(8,128)(2,1)S(1)}, u32[]{:S(2)}) %copy-start.5) | copy-done | bytes 4194328
  82.2 5.7 %right_terms.7.refs_7_.refs_1_ = bf16[8,256,1024]{2,1,0:T(8,128)(2,1)S(1)} custom-call(s32[19]{0:T(128)S(1)} %stack.102.meta, f32[128,16]{1,0:T(8,128)S(1)} %copy.10.site_ref, bf16[2,4,256,256]{3,2,1,0:T(8,128)(2,1)S(1)} %fusion.wave_ref, bf16[2,16,1,256,256]{4,3,2,1,0:T(8,128)(2,1)S(1)} %copy-done.1, bf16[2,16,1,256,256]{4,3,2,1,0:T(8,128)(2,1)S(1)} %copy-done.1), custom_call_target="tpu_custom_call" | custom-call | tf_op jit(solution)/shard_map/right_terms/pallas_call | solution.py:49
  87.9 2.0 %copy-done.2 = bf16[8,256,1024]{2,1,0:T(8,128)(2,1)} copy-done((bf16[8,256,1024]{2,1,0:T(8,128)(2,1)}, bf16[8,256,1024]{2,1,0:T(8,128)(2,1)S(1)}, u32[]{:S(2)}) %copy-start.2) | copy-done | bytes 4194328
  89.9 2.2 %copy-done.3 = bf16[8,256,1024]{2,1,0:T(8,128)(2,1)S(1)} copy-done((bf16[8,256,1024]{2,1,0:T(8,128)(2,1)S(1)}, bf16[8,256,1024]{2,1,0:T(8,128)(2,1)}, u32[]{:S(2)}) %copy-start.3) | copy-done | bytes 4194328
  92.1 2.2 %copy-done.6 = bf16[8,256,1024]{2,1,0:T(8,128)(2,1)S(1)} copy-done((bf16[8,256,1024]{2,1,0:T(8,128)(2,1)S(1)}, bf16[8,256,1024]{2,1,0:T(8,128)(2,1)}, u32[]{:S(2)}) %copy-start.6) | copy-done | bytes 4194328
  94.3 3.1 %left_start.3.total_ref = f32[256,1024]{1,0:T(8,128)S(1)} custom-call(bf16[4,256,256]{2,1,0:T(8,128)(2,1)S(1)} %get-tuple-element.84.refs_0_, bf16[4,256,256]{2,1,0:T(8,128)(2,1)S(1)} %collective-permute-done.10.refs_1_, bf16[4,256,256]{2,1,0:T(8,128)(2,1)S(1)} %collective-permute-done.11.refs_2_, bf16[4,256,256]{2,1,0:T(8,128)(2,1)S(1)} %copy-done.12, ...), custom_call_target="tpu_custom_call" | custom-call | tf_op jit(solution)/shard_map/left_start/pallas_call | solution.py:110
  97.5 1.9 %left_finish.3 = (f32[4,4,32,256]{3,2,1,0:T(8,128)S(1)}, bf16[4,4,32,256]{3,2,1,0:T(8,128)(2,1)S(1)}) custom-call(s32[19]{0:T(128)S(1)} %stack.102.meta, f32[256,1024]{1,0:T(8,128)S(1)} %left_start.3.total_ref, bf16[4,256,256]{2,1,0:T(8,128)(2,1)} %collective-permute-done.15.refs_0_, bf16[8,256,1024]{2,1,0:T(8,128)(2,1)S(1)} %copy-done.4), custom_call_target="tpu_custom_call" | custom-call | tf_op jit(solution)/shard_map/left_finish/pallas_call | solution.py:124
  99.3 0.6 collective-permute-start.16
  100.0 4.0 %collective-permute-start.7 = (bf16[4,32,256]{2,1,0:T(8,128)(2,1)S(1)}, bf16[4,32,256]{2,1,0:T(8,128)(2,1)S(1)}, u32[]{:S(2)}, u32[]{:S(2)}) collective-permute-start(bf16[4,32,256]{2,1,0:T(8,128)(2,1)S(1)} %get-tuple-element.20), channel_id=1, source_target_pairs={{0,4},{2,6},{4,0},{6,2},{1,5},{3,7},{5,1},{7,3},{8,12},{10,14},{12... | collective-permute-start | bytes 196616 | tf_op jit(solution)/shard_map/ppermute | solution.py:249
  104.0 1.0 collective-permute-start.8
  105.0 2.2 %collective-permute-start.9 = (bf16[4,32,256]{2,1,0:T(8,128)(2,1)S(1)}, bf16[4,32,256]{2,1,0:T(8,128)(2,1)S(1)}, u32[]{:S(2)}, u32[]{:S(2)}) collective-permute-start(bf16[4,32,256]{2,1,0:T(8,128)(2,1)S(1)} %get-tuple-element.22), channel_id=1, source_target_pairs={{0,6},{2,0},{4,2},{6,4},{1,7},{3,1},{5,3},{7,5},{8,14},{10,8},{12,... | collective-permute-start | bytes 196616 | tf_op jit(solution)/shard_map/ppermute | solution.py:249
  107.2 0.1 fusion.3
  107.3 0.1 join_cores.3
  107.3 0.1 collective-permute-start.17
  107.4 0.8 collective-permute-start.18
  108.3 2.5 %collective-permute-start.19 = (bf16[4,32,256]{2,1,0:T(8,128)(2,1)S(1)}, bf16[4,32,256]{2,1,0:T(8,128)(2,1)S(1)}, u32[]{:S(2)}, u32[]{:S(2)}) collective-permute-start(bf16[4,32,256]{2,1,0:T(8,128)(2,1)S(1)} %get-tuple-element.28), channel_id=1, source_target_pairs={{0,6},{2,0},{4,2},{6,4},{1,7},{3,1},{5,3},{7,5},{8,14},{10,8},{12,... | collective-permute-start | bytes 196616 | tf_op jit(solution)/shard_map/ppermute | solution.py:249
  110.7 0.1 fusion.1
  110.8 2.4 %collective-permute-done.17 = bf16[4,32,256]{2,1,0:T(8,128)(2,1)S(1)} collective-permute-done((bf16[4,32,256]{2,1,0:T(8,128)(2,1)S(1)}, bf16[4,32,256]{2,1,0:T(8,128)(2,1)S(1)}, u32[]{:S(2)}, u32[]{:S(2)}) %collective-permute-start.17) | collective-permute-done | bytes 65568 | tf_op jit(solution)/shard_map/ppermute | solution.py:249
  113.2 0.4 collective-permute-done.18
  113.7 0.1 fusion.2
  113.8 0.8 copy.14
  (57 shorter events, 0.3 us)
Async XLA Ops:
  2.7 15.7 %collective-permute-start.2 = (bf16[4,256,256]{2,1,0:T(8,128)(2,1)S(1)}, bf16[4,256,256]{2,1,0:T(8,128)(2,1)S(1)}, u32[]{:S(2)}, u32[]{:S(2)}) collective-permute-start(bf16[4,256,256]{2,1,0:T(8,128)(2,1)S(1)} %pad_maximum_fusion.3), channel_id=1, source_target_pairs={{0,96},{1,25},{8,104},{9,1},{16,112},{17,9},{24,120},{25,17},{32,0... | collective-permute-start | bytes 1572872 | tf_op jit(solution)/shard_map/ppermute | solution.py:198
  5.5 12.5 %copy-start.20 = (f32[128,4,4]{0,2,1:T(4,128)S(1)}, f32[128,4,4]{0,2,1:T(4,128)}, u32[]{:S(2)}) copy-start(f32[128,4,4]{0,2,1:T(4,128)} %param.9) | copy-start | bytes 24580
  5.5 12.7 %copy-start.21 = (s32[32]{0:T(128)S(1)}, s32[32]{0:T(128)}, u32[]{:S(2)}) copy-start(s32[32]{0:T(128)} %param.6) | copy-start | bytes 388
  8.7 17.0 %collective-permute-start = (bf16[4,256,256]{2,1,0:T(8,128)(2,1)}, bf16[4,256,256]{2,1,0:T(8,128)(2,1)S(1)}, u32[]{:S(2)}, u32[]{:S(2)}) collective-permute-start(bf16[4,256,256]{2,1,0:T(8,128)(2,1)} %pad_maximum_fusion.1), channel_id=1, source_target_pairs={{0,32},{1,9},{8,40},{9,17},{16,48},{17,25},{24,56},{25,1},{32,64},... | collective-permute-start | bytes 1572872 | tf_op jit(solution)/shard_map/ppermute | solution.py:198
  9.6 16.2 %collective-permute-start.1 = (bf16[4,256,256]{2,1,0:T(8,128)(2,1)}, bf16[4,256,256]{2,1,0:T(8,128)(2,1)S(1)}, u32[]{:S(2)}, u32[]{:S(2)}) collective-permute-start(bf16[4,256,256]{2,1,0:T(8,128)(2,1)} %pad_maximum_fusion.2), channel_id=1, source_target_pairs={{0,64},{1,17},{8,72},{9,25},{16,80},{17,1},{24,88},{25,9},{32,96},... | collective-permute-start | bytes 1572872 | tf_op jit(solution)/shard_map/ppermute | solution.py:198
  12.8 35.5 %collective-permute-start.10 = (bf16[4,256,256]{2,1,0:T(8,128)(2,1)}, bf16[4,256,256]{2,1,0:T(8,128)(2,1)S(1)}, u32[]{:S(2)}, u32[]{:S(2)}) collective-permute-start(bf16[4,256,256]{2,1,0:T(8,128)(2,1)} %pad_maximum_fusion.8), channel_id=1, source_target_pairs={{0,32},{1,9},{8,40},{9,17},{16,48},{17,25},{24,56},{25,1},{32,64},... | collective-permute-start | bytes 1572872 | tf_op jit(solution)/shard_map/ppermute | solution.py:198
  15.4 32.8 %collective-permute-start.11 = (bf16[4,256,256]{2,1,0:T(8,128)(2,1)}, bf16[4,256,256]{2,1,0:T(8,128)(2,1)S(1)}, u32[]{:S(2)}, u32[]{:S(2)}) collective-permute-start(bf16[4,256,256]{2,1,0:T(8,128)(2,1)} %pad_maximum_fusion.9), channel_id=1, source_target_pairs={{0,64},{1,17},{8,72},{9,25},{16,80},{17,1},{24,88},{25,9},{32,96},... | collective-permute-start | bytes 1572872 | tf_op jit(solution)/shard_map/ppermute | solution.py:198
  18.4 30.7 %copy-start.16 = (bf16[1,256,256]{2,1,0:T(8,128)(2,1)S(1)}, bf16[1,256,256]{2,1,0:T(8,128)(2,1)}, u32[]{:S(2)}) copy-start(bf16[1,256,256]{2,1,0:T(8,128)(2,1)} %get-tuple-element.40) | copy-start | bytes 393220
  18.4 30.7 %copy-start.17 = (bf16[1,256,256]{2,1,0:T(8,128)(2,1)S(1)}, bf16[1,256,256]{2,1,0:T(8,128)(2,1)}, u32[]{:S(2)}) copy-start(bf16[1,256,256]{2,1,0:T(8,128)(2,1)} %get-tuple-element.41) | copy-start | bytes 393220
  18.4 30.7 %copy-start.18 = (bf16[1,256,256]{2,1,0:T(8,128)(2,1)S(1)}, bf16[1,256,256]{2,1,0:T(8,128)(2,1)}, u32[]{:S(2)}) copy-start(bf16[1,256,256]{2,1,0:T(8,128)(2,1)} %get-tuple-element.42) | copy-start | bytes 393220
  18.4 30.7 %copy-start.19 = (bf16[1,256,256]{2,1,0:T(8,128)(2,1)S(1)}, bf16[1,256,256]{2,1,0:T(8,128)(2,1)}, u32[]{:S(2)}) copy-start(bf16[1,256,256]{2,1,0:T(8,128)(2,1)} %get-tuple-element.43) | copy-start | bytes 393220
  18.5 29.8 %collective-permute-start.12 = (bf16[4,256,256]{2,1,0:T(8,128)(2,1)}, bf16[4,256,256]{2,1,0:T(8,128)(2,1)S(1)}, u32[]{:S(2)}, u32[]{:S(2)}) collective-permute-start(bf16[4,256,256]{2,1,0:T(8,128)(2,1)} %pad_maximum_fusion.10), channel_id=1, source_target_pairs={{0,96},{1,25},{8,104},{9,1},{16,112},{17,9},{24,120},{25,17},{32,0... | collective-permute-start | bytes 1572872 | tf_op jit(solution)/shard_map/ppermute | solution.py:198
  25.7 24.7 %copy-start.7 = (bf16[4,256,256]{2,1,0:T(8,128)(2,1)}, bf16[4,256,256]{2,1,0:T(8,128)(2,1)S(1)}, u32[]{:S(2)}) copy-start(bf16[4,256,256]{2,1,0:T(8,128)(2,1)S(1)} %collective-permute-done.refs_1_) | copy-start | bytes 1572868
  25.8 24.6 %copy-start.9 = (bf16[4,256,256]{2,1,0:T(8,128)(2,1)}, bf16[4,256,256]{2,1,0:T(8,128)(2,1)S(1)}, u32[]{:S(2)}) copy-start(bf16[4,256,256]{2,1,0:T(8,128)(2,1)S(1)} %collective-permute-done.1.refs_2_) | copy-start | bytes 1572868
  25.8 30.2 %copy-start.15 = (bf16[2,256,4,256]{3,2,1,0:T(4,128)(2,1)S(1)}, bf16[2,256,4,256]{3,2,1,0:T(4,128)(2,1)}, u32[]{:S(2)}) copy-start(bf16[2,256,4,256]{3,2,1,0:T(4,128)(2,1)} %param.5) | copy-start | bytes 3145732
  27.5 28.9 %copy-start = (bf16[2,16,1,256,256]{4,3,2,1,0:T(8,128)(2,1)S(1)}, bf16[2,16,1,256,256]{4,3,2,1,0:T(8,128)(2,1)}, u32[]{:S(2)}) copy-start(bf16[2,16,1,256,256]{4,3,2,1,0:T(8,128)(2,1)} %refs_1_.7) | copy-start | bytes 12582916
  27.5 25.0 %collective-permute-start.3 = (bf16[4,256,256]{2,1,0:T(8,128)(2,1)S(1)}, bf16[4,256,256]{2,1,0:T(8,128)(2,1)S(1)}, u32[]{:S(2)}, u32[]{:S(2)}) collective-permute-start(bf16[4,256,256]{2,1,0:T(8,128)(2,1)S(1)} %get-tuple-element.82), channel_id=1, source_target_pairs={{0,8},{1,33},{8,16},{9,41},{16,24},{17,49},{24,0},{25,57},{32,40},... | collective-permute-start | bytes 1572872 | tf_op jit(solution)/shard_map/ppermute | solution.py:202
  28.4 39.4 %collective-permute-start.4 = (bf16[4,256,256]{2,1,0:T(8,128)(2,1)S(1)}, bf16[4,256,256]{2,1,0:T(8,128)(2,1)S(1)}, u32[]{:S(2)}, u32[]{:S(2)}) collective-permute-start(bf16[4,256,256]{2,1,0:T(8,128)(2,1)S(1)} %get-tuple-element.81), channel_id=1, source_target_pairs={{0,24},{1,97},{8,0},{9,105},{16,8},{17,113},{24,16},{25,121},{32,5... | collective-permute-start | bytes 1572872 | tf_op jit(solution)/shard_map/ppermute | solution.py:202
  48.2 21.3 %collective-permute-start.5 = (bf16[4,256,256]{2,1,0:T(8,128)(2,1)S(1)}, bf16[4,256,256]{2,1,0:T(8,128)(2,1)S(1)}, u32[]{:S(2)}, u32[]{:S(2)}) collective-permute-start(bf16[4,256,256]{2,1,0:T(8,128)(2,1)S(1)} %get-tuple-element.79), channel_id=1, source_target_pairs={{0,16},{1,65},{8,24},{9,73},{16,0},{17,81},{24,8},{25,89},{32,48},... | collective-permute-start | bytes 1572872 | tf_op jit(solution)/shard_map/ppermute | solution.py:202
  48.3 0.8 copy-start.11
  50.4 39.5 %collective-permute-start.13 = (bf16[4,256,256]{2,1,0:T(8,128)(2,1)}, bf16[4,256,256]{2,1,0:T(8,128)(2,1)}, u32[]{:S(2)}, u32[]{:S(2)}) collective-permute-start(bf16[4,256,256]{2,1,0:T(8,128)(2,1)} %get-tuple-element.86), channel_id=1, source_target_pairs={{0,8},{1,33},{8,16},{9,41},{16,24},{17,49},{24,0},{25,57},{32,40},... | collective-permute-start | bytes 1572872 | tf_op jit(solution)/shard_map/ppermute | solution.py:202
  50.4 39.5 %collective-permute-start.14 = (bf16[4,256,256]{2,1,0:T(8,128)(2,1)}, bf16[4,256,256]{2,1,0:T(8,128)(2,1)}, u32[]{:S(2)}, u32[]{:S(2)}) collective-permute-start(bf16[4,256,256]{2,1,0:T(8,128)(2,1)} %get-tuple-element.85), channel_id=1, source_target_pairs={{0,24},{1,97},{8,0},{9,105},{16,8},{17,113},{24,16},{25,121},{32,5... | collective-permute-start | bytes 1572872 | tf_op jit(solution)/shard_map/ppermute | solution.py:202
  52.5 45.0 %collective-permute-start.15 = (bf16[4,256,256]{2,1,0:T(8,128)(2,1)}, bf16[4,256,256]{2,1,0:T(8,128)(2,1)}, u32[]{:S(2)}, u32[]{:S(2)}) collective-permute-start(bf16[4,256,256]{2,1,0:T(8,128)(2,1)} %get-tuple-element.83), channel_id=1, source_target_pairs={{0,16},{1,65},{8,24},{9,73},{16,0},{17,81},{24,8},{25,89},{32,48},... | collective-permute-start | bytes 1572872 | tf_op jit(solution)/shard_map/ppermute | solution.py:202
  62.0 5.7 %copy-start.8 = (bf16[4,256,256]{2,1,0:T(8,128)(2,1)S(1)}, bf16[4,256,256]{2,1,0:T(8,128)(2,1)}, u32[]{:S(2)}) copy-start(bf16[4,256,256]{2,1,0:T(8,128)(2,1)} %copy-done.7) | copy-start | bytes 1572868
  62.1 5.7 %copy-start.10 = (bf16[4,256,256]{2,1,0:T(8,128)(2,1)S(1)}, bf16[4,256,256]{2,1,0:T(8,128)(2,1)}, u32[]{:S(2)}) copy-start(bf16[4,256,256]{2,1,0:T(8,128)(2,1)} %copy-done.9) | copy-start | bytes 1572868
  71.6 0.8 copy-start.13
  72.4 27.6 %collective-permute-start.6 = (bf16[4,4,32,256]{3,2,1,0:T(8,128)(2,1)}, bf16[4,4,32,256]{3,2,1,0:T(8,128)(2,1)S(1)}, u32[]{:S(2)}, u32[]{:S(2)}) collective-permute-start(bf16[4,4,32,256]{3,2,1,0:T(8,128)(2,1)} %get-tuple-element.18), channel_id=1, source_target_pairs={{0,1},{1,0},{2,3},{3,2},{4,5},{5,4},{6,7},{7,6},{8,9},{9,8},{10,11... | collective-permute-start | bytes 786440 | tf_op jit(solution)/shard_map/ppermute | solution.py:245
  72.4 2.2 %copy-start.1 = (bf16[2,16,1,256,256]{4,3,2,1,0:T(8,128)(2,1)S(1)}, bf16[2,16,1,256,256]{4,3,2,1,0:T(8,128)(2,1)}, u32[]{:S(2)}) copy-start(bf16[2,16,1,256,256]{4,3,2,1,0:T(8,128)(2,1)} %refs_1_.7) | copy-start | bytes 12582916
  80.2 2.0 %copy-start.5 = (bf16[8,256,1024]{2,1,0:T(8,128)(2,1)}, bf16[8,256,1024]{2,1,0:T(8,128)(2,1)S(1)}, u32[]{:S(2)}) copy-start(bf16[8,256,1024]{2,1,0:T(8,128)(2,1)S(1)} %right_terms.6.refs_6_) | copy-start | bytes 12582916
  82.2 7.7 %copy-start.12 = (bf16[4,256,256]{2,1,0:T(8,128)(2,1)S(1)}, bf16[4,256,256]{2,1,0:T(8,128)(2,1)}, u32[]{:S(2)}) copy-start(bf16[4,256,256]{2,1,0:T(8,128)(2,1)} %copy-done.11) | copy-start | bytes 1572868
  87.9 2.0 %copy-start.2 = (bf16[8,256,1024]{2,1,0:T(8,128)(2,1)}, bf16[8,256,1024]{2,1,0:T(8,128)(2,1)S(1)}, u32[]{:S(2)}) copy-start(bf16[8,256,1024]{2,1,0:T(8,128)(2,1)S(1)} %right_terms.7.refs_7_.refs_1_) | copy-start | bytes 12582916
  89.9 2.2 %copy-start.3 = (bf16[8,256,1024]{2,1,0:T(8,128)(2,1)S(1)}, bf16[8,256,1024]{2,1,0:T(8,128)(2,1)}, u32[]{:S(2)}) copy-start(bf16[8,256,1024]{2,1,0:T(8,128)(2,1)} %copy-done.2) | copy-start | bytes 12582916
  92.1 2.2 %copy-start.6 = (bf16[8,256,1024]{2,1,0:T(8,128)(2,1)S(1)}, bf16[8,256,1024]{2,1,0:T(8,128)(2,1)}, u32[]{:S(2)}) copy-start(bf16[8,256,1024]{2,1,0:T(8,128)(2,1)} %copy-done.5) | copy-start | bytes 12582916
  94.3 3.2 %copy-start.4 = (bf16[8,256,1024]{2,1,0:T(8,128)(2,1)S(1)}, bf16[8,256,1024]{2,1,0:T(8,128)(2,1)}, u32[]{:S(2)}) copy-start(bf16[8,256,1024]{2,1,0:T(8,128)(2,1)} %copy-done.2) | copy-start | bytes 12582916
  97.4 2.5 %copy-start.14 = (f32[4,4,32,256]{3,2,1,0:T(8,128)S(1)}, f32[4,4,32,256]{3,2,1,0:T(8,128)}, u32[]{:S(2)}) copy-start(f32[4,4,32,256]{3,2,1,0:T(8,128)} %copy-done.13) | copy-start | bytes 1572868
  99.3 7.9 %collective-permute-start.16 = (bf16[4,4,32,256]{3,2,1,0:T(8,128)(2,1)S(1)}, bf16[4,4,32,256]{3,2,1,0:T(8,128)(2,1)S(1)}, u32[]{:S(2)}, u32[]{:S(2)}) collective-permute-start(bf16[4,4,32,256]{3,2,1,0:T(8,128)(2,1)S(1)} %get-tuple-element.24), channel_id=1, source_target_pairs={{0,1},{1,0},{2,3},{3,2},{4,5},{5,4},{6,7},{7,6},{8,9},{9,8},{10,11... | collective-permute-start | bytes 786440 | tf_op jit(solution)/shard_map/ppermute | solution.py:245
  100.0 8.3 %collective-permute-start.7 = (bf16[4,32,256]{2,1,0:T(8,128)(2,1)S(1)}, bf16[4,32,256]{2,1,0:T(8,128)(2,1)S(1)}, u32[]{:S(2)}, u32[]{:S(2)}) collective-permute-start(bf16[4,32,256]{2,1,0:T(8,128)(2,1)S(1)} %get-tuple-element.20), channel_id=1, source_target_pairs={{0,4},{2,6},{4,0},{6,2},{1,5},{3,7},{5,1},{7,3},{8,12},{10,14},{12... | collective-permute-start | bytes 196616 | tf_op jit(solution)/shard_map/ppermute | solution.py:249
  104.0 6.8 %collective-permute-start.8 = (bf16[4,32,256]{2,1,0:T(8,128)(2,1)S(1)}, bf16[4,32,256]{2,1,0:T(8,128)(2,1)S(1)}, u32[]{:S(2)}, u32[]{:S(2)}) collective-permute-start(bf16[4,32,256]{2,1,0:T(8,128)(2,1)S(1)} %get-tuple-element.21), channel_id=1, source_target_pairs={{0,2},{2,4},{4,6},{6,0},{1,3},{3,5},{5,7},{7,1},{8,10},{10,12},{12... | collective-permute-start | bytes 196616 | tf_op jit(solution)/shard_map/ppermute | solution.py:249
  105.0 5.8 %collective-permute-start.9 = (bf16[4,32,256]{2,1,0:T(8,128)(2,1)S(1)}, bf16[4,32,256]{2,1,0:T(8,128)(2,1)S(1)}, u32[]{:S(2)}, u32[]{:S(2)}) collective-permute-start(bf16[4,32,256]{2,1,0:T(8,128)(2,1)S(1)} %get-tuple-element.22), channel_id=1, source_target_pairs={{0,6},{2,0},{4,2},{6,4},{1,7},{3,1},{5,3},{7,5},{8,14},{10,8},{12,... | collective-permute-start | bytes 196616 | tf_op jit(solution)/shard_map/ppermute | solution.py:249
  107.3 5.9 %collective-permute-start.17 = (bf16[4,32,256]{2,1,0:T(8,128)(2,1)S(1)}, bf16[4,32,256]{2,1,0:T(8,128)(2,1)S(1)}, u32[]{:S(2)}, u32[]{:S(2)}) collective-permute-start(bf16[4,32,256]{2,1,0:T(8,128)(2,1)S(1)} %get-tuple-element.26), channel_id=1, source_target_pairs={{0,4},{2,6},{4,0},{6,2},{1,5},{3,7},{5,1},{7,3},{8,12},{10,14},{12... | collective-permute-start | bytes 196616 | tf_op jit(solution)/shard_map/ppermute | solution.py:249
  107.4 6.2 %collective-permute-start.18 = (bf16[4,32,256]{2,1,0:T(8,128)(2,1)S(1)}, bf16[4,32,256]{2,1,0:T(8,128)(2,1)S(1)}, u32[]{:S(2)}, u32[]{:S(2)}) collective-permute-start(bf16[4,32,256]{2,1,0:T(8,128)(2,1)S(1)} %get-tuple-element.27), channel_id=1, source_target_pairs={{0,2},{2,4},{4,6},{6,0},{1,3},{3,5},{5,7},{7,1},{8,10},{10,12},{12... | collective-permute-start | bytes 196616 | tf_op jit(solution)/shard_map/ppermute | solution.py:249
  108.3 5.4 %collective-permute-start.19 = (bf16[4,32,256]{2,1,0:T(8,128)(2,1)S(1)}, bf16[4,32,256]{2,1,0:T(8,128)(2,1)S(1)}, u32[]{:S(2)}, u32[]{:S(2)}) collective-permute-start(bf16[4,32,256]{2,1,0:T(8,128)(2,1)S(1)} %get-tuple-element.28), channel_id=1, source_target_pairs={{0,6},{2,0},{4,2},{6,4},{1,7},{3,1},{5,3},{7,5},{8,14},{10,8},{12,... | collective-permute-start | bytes 196616 | tf_op jit(solution)/shard_map/ppermute | solution.py:249

commit v4 on v0

v4 whole, which is shorter than its diff:
```python
import functools

import jax
import jax.numpy as jnp
from jax import lax
from jax.experimental import pallas as pl
from jax.experimental.pallas import tpu as pltpu
from jax.sharding import Mesh, PartitionSpec as P

CORES = 2
GROUP = 2
ROWS = 16
LEFT_TERMS = 2
VMEM_LIMIT = 48 << 20


def right_kernel(group, meta, site_ref, wave_ref, right_ref, held_ref, first):
    source = pl.program_id(1) * group
    p_size, width = wave_ref.shape[1], wave_ref.shape[2]
    waves = wave_ref[0].reshape(p_size * width, width)
    for at in range(group):
        term = (source + at) * meta[2] + meta[1]
        buf = at % 2
        first[buf] = lax.dot_general(
            waves, right_ref[0, at, 0], (((1,), (1,)), ((), ())),
            preferred_element_type=jnp.float32,
        )
        scale = [[site_ref[term, q * p_size + p] for p in range(p_size)] for q in range(p_size)]
        for low in range(0, width, ROWS):
            parts = [first[buf, p * width + low : p * width + low + ROWS] for p in range(p_size)]
            for q in range(p_size):
                second = parts[0] * scale[q][0]
                for p in range(1, p_size):
                    second = second + parts[p] * scale[q][p]
                held_ref[0, at, low : low + ROWS, q * width : (q + 1) * width] = second.astype(
                    jnp.bfloat16
                )


def right_call(meta, site, wave, right):
    sectors, sources, width = right.shape[0], right.shape[1], right.shape[-1]
    p_size = wave.shape[1]
    return pl.pallas_call(
        functools.partial(right_kernel, GROUP),
        grid=(sectors, sources // GROUP),
        in_specs=[
            pl.BlockSpec(memory_space=pltpu.SMEM),
            pl.BlockSpec(memory_space=pltpu.SMEM),
            pl.BlockSpec((1, p_size, width, width), lambda sector, step: (sector, 0, 0, 0)),
            pl.BlockSpec((1, GROUP, 1, width, width), lambda sector, step: (sector, step, 0, 0, 0)),
        ],
        out_specs=pl.BlockSpec(
            (1, GROUP, width, p_size * width), lambda sector, step: (sector, step, 0, 0)
        ),
        out_shape=jax.ShapeDtypeStruct((sectors, sources, width, p_size * width), jnp.bfloat16),
        scratch_shapes=[pltpu.VMEM((2, p_size * width, width), jnp.float32)],
        compiler_params=pltpu.CompilerParams(vmem_limit_bytes=VMEM_LIMIT),
        name="right_terms",
    )(meta, site, wave, right)


def left_kernel(z_count, p_size, meta, left_hbm, held_hbm, keep_ref, give_ref, *scratch):
    left, held, total, left_sem, held_sem = scratch
    sectors, sources = held.shape[0], held.shape[1]
    width = total.shape[0]
    rows = width // (z_count * CORES)
    core = lax.rem(meta[1], CORES)
    steps = sources // LEFT_TERMS
    copies = []
    for sector in range(sectors):
        for step in range(steps):
            span = pl.ds(step * LEFT_TERMS, LEFT_TERMS)
            slot = sector * steps + step
            pair = (
                pltpu.make_async_copy(
                    left_hbm.at[span, sector], left.at[sector, span], left_sem.at[slot]
                ),
                pltpu.make_async_copy(
                    held_hbm.at[sector, span], held.at[sector, span], held_sem.at[slot]
                ),
            )
            for copy in pair:
                copy.start()
            copies.append(pair)

    for sector in range(sectors):
        for step in range(steps):
            for copy in copies[sector * steps + step]:
                copy.wait()
            add = None
            for at in range(step * LEFT_TERMS, (step + 1) * LEFT_TERMS):
                product = jnp.dot(
                    left[sector, at], held[sector, at], preferred_element_type=jnp.float32
                )
                add = product if add is None else add + product
            if step == 0:
                total[...] = add
            else:
                total[...] += add
        for shift in range(z_count):
            z_to = lax.rem(meta[0] + shift, z_count)
            for out, side in ((keep_ref, core), (give_ref, 1 - core)):
                start = pl.multiple_of((z_to * CORES + side) * rows, rows)
                block = total[pl.ds(start, rows), :]
                for q in range(p_size):
                    out[shift, sector, q] = block[:, q * width : (q + 1) * width].astype(out.dtype)


def left_call(meta, left, held, z_count):
    sectors, sources, width, columns = held.shape
    p_size = columns // width
    shape = (z_count, sectors, p_size, width // (z_count * CORES), width)
    steps = sectors * sources // LEFT_TERMS
    return pl.pallas_call(
        functools.partial(left_kernel, z_count, p_size),
        in_specs=[
            pl.BlockSpec(memory_space=pltpu.SMEM),
            pl.BlockSpec(memory_space=pl.ANY),
            pl.BlockSpec(memory_space=pl.ANY),
        ],
        out_specs=[pl.BlockSpec(memory_space=pltpu.VMEM)] * 2,
        out_shape=[
            jax.ShapeDtypeStruct(shape, jnp.float32),
            jax.ShapeDtypeStruct(shape, jnp.bfloat16),
        ],
        scratch_shapes=[
            pltpu.VMEM((sectors, sources, width, width), jnp.bfloat16),
            pltpu.VMEM((sectors, sources, width, columns), jnp.bfloat16),
            pltpu.VMEM((width, columns), jnp.float32),
            pltpu.SemaphoreType.DMA((steps,)),
            pltpu.SemaphoreType.DMA((steps,)),
        ],
        compiler_params=pltpu.CompilerParams(vmem_limit_bytes=VMEM_LIMIT),
        name="left_terms",
    )(meta, left, held)


def join_kernel(keep_ref, take_ref, *outs):
    for shift, out in enumerate(outs):
        out[...] = (keep_ref[shift] + take_ref[shift].astype(jnp.float32)).astype(out.dtype)


def join_call(keep, take):
    z_count, shape = keep.shape[0], keep.shape[1:]
    return pl.pallas_call(
        join_kernel,
        in_specs=[pl.BlockSpec(memory_space=pltpu.VMEM)] * 2,
        out_specs=[pl.BlockSpec(memory_space=pltpu.VMEM)] * z_count,
        out_shape=[
            jax.ShapeDtypeStruct(shape, jnp.float32 if s == 0 else jnp.bfloat16)
            for s in range(z_count)
        ],
        compiler_params=pltpu.CompilerParams(vmem_limit_bytes=16 << 20),
        name="join_cores",
    )(keep, take)


def shards(wave, sector_dims, left_ops, right_ops, site_ops):
    z_count = lax.axis_size("z")
    op_at, z_at, core = lax.axis_index("op"), lax.axis_index("z"), lax.axis_index("core")
    sectors, width = wave.shape[0], wave.shape[1]

    left = lax.all_to_all(left_ops[:, 0], "op", split_axis=0, concat_axis=0, tiled=True)
    left = left.reshape(-1, sectors, width, width)

    sizes = lax.dynamic_slice_in_dim(sector_dims, op_at * sectors, sectors)
    mask = (lax.broadcasted_iota(jnp.int32, (sectors, width), 1) < sizes[:, None]).astype(
        jnp.float32
    )
    masked = wave.astype(jnp.float32) * mask[:, :, None, None] * mask[:, None, None, :]
    masked = masked.astype(jnp.bfloat16).transpose(0, 2, 1, 3)
    site = site_ops.reshape(site_ops.shape[0], -1)
    sec_at = z_at * CORES + core
    meta = jnp.stack([z_at, sec_at, jnp.int32(z_count * CORES)]).astype(jnp.int32)
    held = right_call(meta, site, masked, right_ops)

    keep, give = left_call(meta, left, held, z_count)
    parts = join_call(keep, lax.ppermute(give, "core", [(0, 1), (1, 0)]))
    total = parts[0]
    for shift in sorted(range(1, z_count), key=lambda s: -min(s, z_count - s)):
        ring = [(z, (z + shift) % z_count) for z in range(z_count)]
        total = total + lax.ppermute(parts[shift], "z", ring).astype(jnp.float32)

    rows = width // (z_count * CORES)
    row_mask = lax.dynamic_slice_in_dim(mask, sec_at * rows, rows, 1)
    share = total * row_mask[:, None, :, None] * mask[:, None, None, :]
    return share.astype(jnp.bfloat16).transpose(0, 2, 1, 3)


def solution(mesh):
    op_count, sec_count = mesh.shape["op"], mesh.shape["sec"]
    split = Mesh(
        mesh.devices.reshape(op_count, sec_count // CORES, CORES), ("op", "z", "core")
    )
    placed = (
        P("op", None, None, None),
        P(),
        P(None, ("op", "z", "core"), None, None),
        P("op", None, ("z", "core"), None, None),
        P(),
    )
    return jax.shard_map(
        shards, mesh=split, in_specs=placed,
        out_specs=P("op", ("z", "core"), None, None), check_vma=False,
    )
```

time: 556 us -> 96.2 us (0.17)
  the two profiles are of different devices: /device:TPU:8 before, /device:TPU:28 now
where the time goes in v4:
time: 96.2 us; the launch traced here: 96 us
  waiting for transfers between devices  51.9 us (54%)
  Pallas kernels  25.8 us (27%)
  starting transfers between devices  14.5 us (15%)
  local copies, waits for them, and re-layouts  3.2 us (3%)
    all_to_all x1, waiting for transfers between devices, shards(): lax.all_to_all(left_ops[:, 0], 'op', split_axis=0, concat_axis=0, tiled=T...  46 us
    pallas_call x1, Pallas kernels, right_call(): pl.pallas_call(functools.partial(right_kernel, GROUP), grid=(sectors, sou...  17.4 us
    pallas_call x1, Pallas kernels, left_call(): pl.pallas_call(functools.partial(left_kernel, z_count, p_size), in_specs=...  8.31 us
    all_to_all x1, starting transfers between devices, shards(): lax.all_to_all(left_ops[:, 0], 'op', split_axis=0, concat_axis=0, tiled=T...  7.26 us
    ppermute x3, starting transfers between devices, shards(): total = total + lax.ppermute(parts[shift], 'z', ring).astype(jnp.float32)  7.19 us
    ppermute x3, waiting for transfers between devices, shards(): total = total + lax.ppermute(parts[shift], 'z', ring).astype(jnp.float32)  4.03 us
    unnamed x8, local copies, waits for them, and re-layouts  2.19 us
  transfers between devices with their start and end apart: 5, of which 5 were waited for; matrix products, arithmetic and copies ran while one was open for 1% of the time, Pallas kernels for 18%

profile of v4, /device:TPU:28, one launch (start us, length us, event | category | flops | bytes accessed | tf_op | source)
XLA Modules:
  0.0 96.0 jit_solution(4995164588466853606)
XLA Ops:
  0.0 0.0 copy-start.2
  0.0 0.0 copy-start.3
  0.0 0.0 copy-start.1
  0.0 7.3 %all-to-all-start = ((bf16[32,256,256]{2,1,0:T(8,128)(2,1)}), bf16[32,256,256]{2,1,0:T(8,128)(2,1)}, u32[]{:S(2)}, u32[]{:S(2)}) async-start(bf16[32,256,256]{2,1,0:T(8,128)(2,1)} %bitcast.9), calls=%async_computation | async-start | bytes 8388608 | tf_op jit(solution)/shard_map/all_to_all | solution.py:163
  7.3 0.0 copy-done.2
  7.3 0.1 copy.10.site_ref
  7.4 0.0 copy-done.3
  7.4 0.1 dynamic_slice.6
  7.5 0.1 pad_add_fusion.meta
  7.5 0.1 compare_convert_fusion
  7.6 0.0 copy-done.1
  7.6 0.3 fusion.wave_ref
  7.9 0.0 copy-start
  7.9 2.2 %copy-done = bf16[2,16,1,256,256]{4,3,2,1,0:T(8,128)(2,1)S(1)} copy-done((bf16[2,16,1,256,256]{4,3,2,1,0:T(8,128)(2,1)S(1)}, bf16[2,16,1,256,256]{4,3,2,1,0:T(8,128)(2,1)}, u32[]{:S(2)}) %copy-start) | copy-done | bytes 4194328
  10.1 17.4 %right_terms.1.held_hbm = bf16[2,16,256,1024]{3,2,1,0:T(8,128)(2,1)} custom-call(s32[3]{0:T(128)S(1)} %pad_add_fusion.meta, f32[128,16]{1,0:T(8,128)S(1)} %copy.10.site_ref, bf16[2,4,256,256]{3,2,1,0:T(8,128)(2,1)S(1)} %fusion.wave_ref, bf16[2,16,1,256,256]{4,3,2,1,0:T(8,128)(2,1)S(1)} %copy-done), custom_call_target="tpu_custom_call" | custom-call | tf_op jit(solution)/shard_map/right_terms/pallas_call | solution.py:43
  27.5 46.0 %all-to-all-done = bf16[32,256,256]{2,1,0:T(8,128)(2,1)} async-done(((bf16[32,256,256]{2,1,0:T(8,128)(2,1)}), bf16[32,256,256]{2,1,0:T(8,128)(2,1)}, u32[]{:S(2)}, u32[]{:S(2)}) %all-to-all-start) | async-done | bytes 4194336 | tf_op jit(solution)/shard_map/all_to_all | solution.py:163
  73.5 8.3 %left_terms.1 = (f32[4,2,4,32,256]{4,3,2,1,0:T(8,128)S(1)}, bf16[4,2,4,32,256]{4,3,2,1,0:T(8,128)(2,1)S(1)}) custom-call(s32[3]{0:T(128)S(1)} %pad_add_fusion.meta, bf16[16,2,256,256]{3,2,1,0:T(8,128)(2,1)} %bitcast.3.left_hbm, bf16[2,16,256,1024]{3,2,1,0:T(8,128)(2,1)} %right_terms.1.held_hbm), custom_call_target="tpu_custom_call" | custom-call | tf_op jit(solution)/shard_map/left_terms/pallas_call | solution.py:114
  81.8 0.1 collective-permute-start
  81.9 1.9 %collective-permute-done.take_ref = bf16[4,2,4,32,256]{4,3,2,1,0:T(8,128)(2,1)S(1)} collective-permute-done((bf16[4,2,4,32,256]{4,3,2,1,0:T(8,128)(2,1)S(1)}, bf16[4,2,4,32,256]{4,3,2,1,0:T(8,128)(2,1)S(1)}, u32[]{:S(2)}, u32[]{:S(2)}) %collective-permute-start) | collective-permute-done | bytes 524320 | tf_op jit(solution)/shard_map/ppermute | solution.py:178
  83.8 0.1 join_cores.1
  83.9 4.0 %collective-permute-start.1 = (bf16[2,4,32,256]{3,2,1,0:T(8,128)(2,1)S(1)}, bf16[2,4,32,256]{3,2,1,0:T(8,128)(2,1)S(1)}, u32[]{:S(2)}, u32[]{:S(2)}) collective-permute-start(bf16[2,4,32,256]{3,2,1,0:T(8,128)(2,1)S(1)} %get-tuple-element.14), channel_id=1, source_target_pairs={{0,4},{2,6},{4,0},{6,2},{1,5},{3,7},{5,1},{7,3},{8,12},{10,14},{12... | collective-permute-start | bytes 393224 | tf_op jit(solution)/shard_map/ppermute | solution.py:182
  87.8 1.0 %collective-permute-start.2 = (bf16[2,4,32,256]{3,2,1,0:T(8,128)(2,1)S(1)}, bf16[2,4,32,256]{3,2,1,0:T(8,128)(2,1)S(1)}, u32[]{:S(2)}, u32[]{:S(2)}) collective-permute-start(bf16[2,4,32,256]{3,2,1,0:T(8,128)(2,1)S(1)} %get-tuple-element.15), channel_id=1, source_target_pairs={{0,2},{2,4},{4,6},{6,0},{1,3},{3,5},{5,7},{7,1},{8,10},{10,12},{12... | collective-permute-start | bytes 393224 | tf_op jit(solution)/shard_map/ppermute | solution.py:182
  88.9 2.2 %collective-permute-start.3 = (bf16[2,4,32,256]{3,2,1,0:T(8,128)(2,1)S(1)}, bf16[2,4,32,256]{3,2,1,0:T(8,128)(2,1)S(1)}, u32[]{:S(2)}, u32[]{:S(2)}) collective-permute-start(bf16[2,4,32,256]{3,2,1,0:T(8,128)(2,1)S(1)} %get-tuple-element.16), channel_id=1, source_target_pairs={{0,6},{2,0},{4,2},{6,4},{1,7},{3,1},{5,3},{7,5},{8,14},{10,8},{12,... | collective-permute-start | bytes 393224 | tf_op jit(solution)/shard_map/ppermute | solution.py:182
  91.1 0.1 constant_dynamic-slice_fusion
  91.2 1.0 %collective-permute-done.1 = bf16[2,4,32,256]{3,2,1,0:T(8,128)(2,1)S(1)} collective-permute-done((bf16[2,4,32,256]{3,2,1,0:T(8,128)(2,1)S(1)}, bf16[2,4,32,256]{3,2,1,0:T(8,128)(2,1)S(1)}, u32[]{:S(2)}, u32[]{:S(2)}) %collective-permute-start.1) | collective-permute-done | bytes 131104 | tf_op jit(solution)/shard_map/ppermute | solution.py:182
  92.1 2.5 %collective-permute-done.2 = bf16[2,4,32,256]{3,2,1,0:T(8,128)(2,1)S(1)} collective-permute-done((bf16[2,4,32,256]{3,2,1,0:T(8,128)(2,1)S(1)}, bf16[2,4,32,256]{3,2,1,0:T(8,128)(2,1)S(1)}, u32[]{:S(2)}, u32[]{:S(2)}) %collective-permute-start.2) | collective-permute-done | bytes 131104 | tf_op jit(solution)/shard_map/ppermute | solution.py:182
  94.6 0.6 collective-permute-done.3
  95.2 0.1 fusion.1
  95.3 0.8 copy.11
Async XLA Ops:
  0.0 7.3 %copy-start.2 = (f32[128,4,4]{0,2,1:T(4,128)S(1)}, f32[128,4,4]{0,2,1:T(4,128)}, u32[]{:S(2)}) copy-start(f32[128,4,4]{0,2,1:T(4,128)} %param.9) | copy-start | bytes 24580
  0.0 7.4 %copy-start.3 = (s32[32]{0:T(128)S(1)}, s32[32]{0:T(128)}, u32[]{:S(2)}) copy-start(s32[32]{0:T(128)} %param.6) | copy-start | bytes 388
  0.0 7.6 %copy-start.1 = (bf16[2,256,4,256]{3,2,1,0:T(4,128)(2,1)S(1)}, bf16[2,256,4,256]{3,2,1,0:T(4,128)(2,1)}, u32[]{:S(2)}) copy-start(bf16[2,256,4,256]{3,2,1,0:T(4,128)(2,1)} %param.5) | copy-start | bytes 3145732
  0.0 73.5 %all-to-all-start = ((bf16[32,256,256]{2,1,0:T(8,128)(2,1)}), bf16[32,256,256]{2,1,0:T(8,128)(2,1)}, u32[]{:S(2)}, u32[]{:S(2)}) async-start(bf16[32,256,256]{2,1,0:T(8,128)(2,1)} %bitcast.9), calls=%async_computation | async-start | bytes 8388608 | tf_op jit(solution)/shard_map/all_to_all | solution.py:163
  7.9 2.2 %copy-start = (bf16[2,16,1,256,256]{4,3,2,1,0:T(8,128)(2,1)S(1)}, bf16[2,16,1,256,256]{4,3,2,1,0:T(8,128)(2,1)}, u32[]{:S(2)}) copy-start(bf16[2,16,1,256,256]{4,3,2,1,0:T(8,128)(2,1)} %right_ref.1) | copy-start | bytes 12582916
  81.8 2.0 %collective-permute-start = (bf16[4,2,4,32,256]{4,3,2,1,0:T(8,128)(2,1)S(1)}, bf16[4,2,4,32,256]{4,3,2,1,0:T(8,128)(2,1)S(1)}, u32[]{:S(2)}, u32[]{:S(2)}) collective-permute-start(bf16[4,2,4,32,256]{4,3,2,1,0:T(8,128)(2,1)S(1)} %get-tuple-element.12), channel_id=1, source_target_pairs={{0,1},{1,0},{2,3},{3,2},{4,5},{5,4},{6,7},{7,6},{8,9},{9,8},{10,11... | collective-permute-start | bytes 1572872 | tf_op jit(solution)/shard_map/ppermute | solution.py:178
  83.9 8.2 %collective-permute-start.1 = (bf16[2,4,32,256]{3,2,1,0:T(8,128)(2,1)S(1)}, bf16[2,4,32,256]{3,2,1,0:T(8,128)(2,1)S(1)}, u32[]{:S(2)}, u32[]{:S(2)}) collective-permute-start(bf16[2,4,32,256]{3,2,1,0:T(8,128)(2,1)S(1)} %get-tuple-element.14), channel_id=1, source_target_pairs={{0,4},{2,6},{4,0},{6,2},{1,5},{3,7},{5,1},{7,3},{8,12},{10,14},{12... | collective-permute-start | bytes 393224 | tf_op jit(solution)/shard_map/ppermute | solution.py:182
  87.8 6.8 %collective-permute-start.2 = (bf16[2,4,32,256]{3,2,1,0:T(8,128)(2,1)S(1)}, bf16[2,4,32,256]{3,2,1,0:T(8,128)(2,1)S(1)}, u32[]{:S(2)}, u32[]{:S(2)}) collective-permute-start(bf16[2,4,32,256]{3,2,1,0:T(8,128)(2,1)S(1)} %get-tuple-element.15), channel_id=1, source_target_pairs={{0,2},{2,4},{4,6},{6,0},{1,3},{3,5},{5,7},{7,1},{8,10},{10,12},{12... | collective-permute-start | bytes 393224 | tf_op jit(solution)/shard_map/ppermute | solution.py:182
  88.9 6.3 %collective-permute-start.3 = (bf16[2,4,32,256]{3,2,1,0:T(8,128)(2,1)S(1)}, bf16[2,4,32,256]{3,2,1,0:T(8,128)(2,1)S(1)}, u32[]{:S(2)}, u32[]{:S(2)}) collective-permute-start(bf16[2,4,32,256]{3,2,1,0:T(8,128)(2,1)S(1)} %get-tuple-element.16), channel_id=1, source_target_pairs={{0,6},{2,0},{4,2},{6,4},{1,7},{3,1},{5,3},{7,5},{8,14},{10,8},{12,... | collective-permute-start | bytes 393224 | tf_op jit(solution)/shard_map/ppermute | solution.py:182

commit v5 on v2

--- a/solution.py
+++ b/solution.py
@@ -11,6 +11,7 @@
 GROUP = 2
 ROWS = 16
 LEFT_TERMS = 2
+DIRECT = 4
 VMEM_LIMIT = 48 << 20
 
 
@@ -43,7 +44,7 @@
 
 
 def right_call(meta, site, wave, own, other):
-    sources, width = own.shape[1], own.shape[-1]
+    sources, width = own.shape[1] - DIRECT, own.shape[-1]
     p_size = wave.shape[0]
     right_spec = pl.BlockSpec(
         (1, GROUP, 1, width, width), lambda step, meta: (meta[0], step, 0, 0, 0)
@@ -70,34 +71,88 @@
     )(meta, site, wave, own, other)
 
 
-def left_kernel(z_count, p_size, meta, left_hbm, held_hbm, *refs):
+def left_kernel(z_count, p_size, meta, site_ref, left_hbm, held_hbm, wave_hbm, own_hbm, other_hbm, *refs):
     outs = refs[:z_count]
-    left, held, total, left_sem, held_sem = refs[z_count:]
-    z_at = meta[1]
+    left, held, wave, rights, first, mixed, total, left_sem, held_sem, side_sem = refs[z_count:]
+    z_at, core, sec_count = meta[1], meta[0], meta[2]
     terms, width = left.shape[0], left.shape[1]
-    copies = []
-    for at in range(0, terms, LEFT_TERMS):
-        span = pl.ds(at, LEFT_TERMS)
-        slot = at // LEFT_TERMS
-        pair = (
-            pltpu.make_async_copy(left_hbm.at[span], left.at[span], left_sem.at[slot]),
-            pltpu.make_async_copy(held_hbm.at[span], held.at[span], held_sem.at[slot]),
-        )
+    sources = terms // CORES
+    ready = sources - DIRECT
+
+    def left_copy(slot):
+        span = pl.ds(slot * LEFT_TERMS, LEFT_TERMS)
+        return pltpu.make_async_copy(left_hbm.at[span], left.at[span], left_sem.at[slot])
+
+    def held_copy(slot):
+        span = pl.ds(slot * LEFT_TERMS, LEFT_TERMS)
+        return pltpu.make_async_copy(held_hbm.at[span], held.at[span], held_sem.at[slot])
+
+    held_slots = ready * CORES // LEFT_TERMS
+    slots = terms // LEFT_TERMS
+    side_copies = [
+        pltpu.make_async_copy(wave_hbm, wave, side_sem.at[0]),
+        pltpu.make_async_copy(
+            own_hbm.at[core, pl.ds(ready, DIRECT), 0], rights.at[0], side_sem.at[1]
+        ),
+        pltpu.make_async_copy(
+            other_hbm.at[core, pl.ds(ready, DIRECT), 0], rights.at[1], side_sem.at[2]
+        ),
+    ]
+    late = [left_copy(slot) for slot in range(held_slots, slots)]
+    side_copies[0].start()
+    for copy in late:
+        copy.start()
+    for copy in side_copies[1:]:
+        copy.start()
+    pairs = [(left_copy(slot), held_copy(slot)) for slot in range(held_slots)]
+    for pair in pairs:
         for copy in pair:
             copy.start()
-        copies.append(pair)
-
-    for slot, pair in enumerate(copies):
+
+    side_copies[0].wait()
+    for copy in late:
+        copy.wait()
+    for copy in side_copies[1:]:
+        copy.wait()
+    for at in range(DIRECT):
+        for slot in range(CORES):
+            side = core if slot == 0 else 1 - core
+            source = ready + at
+            term = source * sec_count + z_at * CORES + side
+            for p in range(p_size):
+                first[slot, p] = jnp.dot(
+                    left[source * CORES + side], wave[p], preferred_element_type=jnp.float32
+                )
+            scale = [[site_ref[term, q * p_size + p] for p in range(p_size)] for q in range(p_size)]
+            for low in range(0, width, ROWS):
+                parts = [first[slot, p, low : low + ROWS] for p in range(p_size)]
+                for q in range(p_size):
+                    second = parts[0] * scale[q][0]
+                    for p in range(1, p_size):
+                        second = second + parts[p] * scale[q][p]
+                    mixed[at % 2, q, low : low + ROWS, slot * width : (slot + 1) * width] = (
+                        second.astype(jnp.bfloat16)
+                    )
+        right = jnp.concatenate([rights[slot, at] for slot in range(CORES)], axis=1)
+        for q in range(p_size):
+            product = lax.dot_general(
+                mixed[at % 2, q], right, (((1,), (1,)), ((), ())),
+                preferred_element_type=jnp.float32,
+            )
+            columns = slice(q * width, (q + 1) * width)
+            if at == 0:
+                total[:, columns] = product
+            else:
+                total[:, columns] += product
+
+    for slot, pair in enumerate(pairs):
         for copy in pair:
             copy.wait()
         add = None
         for at in range(slot * LEFT_TERMS, (slot + 1) * LEFT_TERMS):
             product = jnp.dot(left[at], held[at], preferred_element_type=jnp.float32)
             add = product if add is None else add + product
-        if slot == 0:
-            total[...] = add
-        else:
-            total[...] += add
+        total[...] += add
 
     rows = width // z_count
     for shift in range(z_count):
@@ -107,17 +162,15 @@
             outs[shift][q] = block[:, q * width : (q + 1) * width].astype(outs[shift].dtype)
 
 
-def left_call(meta, left, held, z_count):
-    terms, width, columns = held.shape
+def left_call(meta, site, left, held, wave, own, other, z_count):
+    terms, width = left.shape[0], left.shape[1]
+    ready, columns = held.shape[0], held.shape[2]
     p_size = columns // width
     rows = width // z_count
     return pl.pallas_call(
         functools.partial(left_kernel, z_count, p_size),
-        in_specs=[
-            pl.BlockSpec(memory_space=pltpu.SMEM),
-            pl.BlockSpec(memory_space=pl.ANY),
-            pl.BlockSpec(memory_space=pl.ANY),
-        ],
+        in_specs=[pl.BlockSpec(memory_space=pltpu.SMEM)] * 2
+        + [pl.BlockSpec(memory_space=pl.ANY)] * 5,
         out_specs=[pl.BlockSpec(memory_space=pltpu.VMEM)] * z_count,
         out_shape=[
             jax.ShapeDtypeStruct((p_size, rows, width), jnp.float32 if s == 0 else jnp.bfloat16)
@@ -125,14 +178,19 @@
         ],
         scratch_shapes=[
             pltpu.VMEM((terms, width, width), jnp.bfloat16),
-            pltpu.VMEM((terms, width, columns), jnp.bfloat16),
+            pltpu.VMEM((ready, width, columns), jnp.bfloat16),
+            pltpu.VMEM((p_size, width, width), jnp.bfloat16),
+            pltpu.VMEM((CORES, DIRECT, width, width), jnp.bfloat16),
+            pltpu.VMEM((CORES, p_size, width, width), jnp.float32),
+            pltpu.VMEM((2, p_size, width, CORES * width), jnp.bfloat16),
             pltpu.VMEM((width, columns), jnp.float32),
             pltpu.SemaphoreType.DMA((terms // LEFT_TERMS,)),
-            pltpu.SemaphoreType.DMA((terms // LEFT_TERMS,)),
+            pltpu.SemaphoreType.DMA((ready // LEFT_TERMS,)),
+            pltpu.SemaphoreType.DMA((3,)),
         ],
         compiler_params=pltpu.CompilerParams(vmem_limit_bytes=VMEM_LIMIT),
         name="left_terms",
-    )(meta, left, held)
+    )(meta, site, left, held, wave, own, other)
 
 
 def shards(wave, sector_dims, left_ops, right_ops, site_ops):
@@ -153,7 +211,7 @@
     meta = jnp.stack([core, z_at, jnp.int32(z_count * CORES)]).astype(jnp.int32)
     site = site_ops.reshape(site_ops.shape[0], -1)
     held = right_call(meta, site, masked, right_ops, other)
-    parts = left_call(meta, left, held, z_count)
+    parts = left_call(meta, site, left, held, masked, right_ops, other, z_count)
 
     total = parts[0]
     for shift in sorted(range(1, z_count), key=lambda s: -min(s, z_count - s)):

time: 84.4 us -> 90.9 us (1.077)
  Pallas kernels: 25 us -> 28.4 us
  waiting for transfers between devices: 38.7 us -> 41.8 us
    pallas_call x1, Pallas kernels: 8.33 us -> 14.9 us  [left_call(): pl.pallas_call(functools.partial(left_kernel, z_count, p_size), in_specs=...]
    all_to_all x1, waiting for transfers between devices: 33.9 us -> 37 us  [shards(): lax.all_to_all(left_ops[:, 0], ('op', 'core'), split_axis=0, concat_axis=...]
    pallas_call x1, Pallas kernels: 16.7 us -> 13.6 us  [right_call(): pl.pallas_call(functools.partial(right_kernel, GROUP), grid_spec=pltpu.Pr...]
  transfers between devices with their start and end apart: 6 -> 6, of which waited for: 5 -> 5; matrix products, arithmetic and copies ran while one was open for 2% -> 2% of each run, Pallas kernels for 20% -> 15%
where the time goes in v5:
time: 90.9 us; the launch traced here: 90.4 us
  waiting for transfers between devices  41.8 us (46%)
  Pallas kernels  28.4 us (31%)
  starting transfers between devices  15.1 us (17%)
  local copies, waits for them, and re-layouts  3.23 us (4%)
  other arithmetic  1.75 us (2%)
    all_to_all x1, waiting for transfers between devices, shards(): lax.all_to_all(left_ops[:, 0], ('op', 'core'), split_axis=0, concat_axis=...  37 us
    pallas_call x1, Pallas kernels, left_call(): pl.pallas_call(functools.partial(left_kernel, z_count, p_size), in_specs=...  14.9 us
    pallas_call x1, Pallas kernels, right_call(): pl.pallas_call(functools.partial(right_kernel, GROUP), grid_spec=pltpu.Pr...  13.6 us
    all_to_all x1, starting transfers between devices, shards(): lax.all_to_all(left_ops[:, 0], ('op', 'core'), split_axis=0, concat_axis=...  7.81 us
    ppermute x3, starting transfers between devices, shards(): total = total + lax.ppermute(parts[shift], 'z', ring).astype(jnp.float32)  7.19 us
    ppermute x3, waiting for transfers between devices, shards(): total = total + lax.ppermute(parts[shift], 'z', ring).astype(jnp.float32)  3.53 us
    unnamed x8, local copies, waits for them, and re-layouts  2.2 us
  transfers between devices with their start and end apart: 6, of which 5 were waited for; matrix products, arithmetic and copies ran while one was open for 2% of the time, Pallas kernels for 15%

profile of v5, /device:TPU:8, one launch (start us, length us, event | category | flops | bytes accessed | tf_op | source)
XLA Modules:
  0.0 90.4 jit_solution(8476035454652146218)
XLA Ops:
  0.0 0.0 copy-start
  0.0 0.0 collective-permute-start
  0.0 0.0 copy-start.2
  0.0 0.0 copy-start.3
  0.0 7.8 %all-to-all-start = ((bf16[32,256,256]{2,1,0:T(8,128)(2,1)}), bf16[32,256,256]{2,1,0:T(8,128)(2,1)}, u32[]{:S(2)}, u32[]{:S(2)}) async-start(bf16[32,256,256]{2,1,0:T(8,128)(2,1)} %bitcast.29), calls=%async_computation | async-start | bytes 8388608 | tf_op jit(solution)/shard_map/all_to_all | solution.py:203
  7.9 0.0 copy-done.2
  7.9 0.1 copy.12.site_ref
  8.0 0.0 copy-done.3
  8.0 0.6 dynamic_slice.18
  8.6 0.1 pad_add_fusion.meta
  8.6 0.6 compare_convert_fusion
  9.2 0.0 copy-done
  9.2 0.2 constant_dynamic-slice_fusion.2
  9.4 0.2 fusion.2.wave_ref.wave_hbm
  9.6 0.0 collective-permute-done.other_ref.other_hbm
  9.6 0.0 copy-start.1
  9.6 2.2 %copy-done.1 = bf16[2,16,1,256,256]{4,3,2,1,0:T(8,128)(2,1)S(1)} copy-done((bf16[2,16,1,256,256]{4,3,2,1,0:T(8,128)(2,1)S(1)}, bf16[2,16,1,256,256]{4,3,2,1,0:T(8,128)(2,1)}, u32[]{:S(2)}) %copy-start.1) | copy-done | bytes 4194328
  11.8 13.6 %right_terms.1.held_hbm = bf16[24,256,1024]{2,1,0:T(8,128)(2,1)} custom-call(s32[3]{0:T(128)S(1)} %pad_add_fusion.meta, f32[128,16]{1,0:T(8,128)S(1)} %copy.12.site_ref, bf16[4,256,256]{2,1,0:T(8,128)(2,1)S(1)} %fusion.2.wave_ref.wave_hbm, bf16[2,16,1,256,256]{4,3,2,1,0:T(8,128)(2,1)S(1)} %copy-done.1, ...), custom_call_target="tpu_custom_call" | custom-call | tf_op jit(solution)/shard_map/right_terms/pallas_call | solution.py:52
  25.4 37.0 %all-to-all-done.left_hbm = bf16[32,256,256]{2,1,0:T(8,128)(2,1)} async-done(((bf16[32,256,256]{2,1,0:T(8,128)(2,1)}), bf16[32,256,256]{2,1,0:T(8,128)(2,1)}, u32[]{:S(2)}, u32[]{:S(2)}) %all-to-all-start) | async-done | bytes 4194336 | tf_op jit(solution)/shard_map/all_to_all | solution.py:203
  62.4 14.9 %left_terms.1 = (f32[4,64,256]{2,1,0:T(8,128)S(1)}, bf16[4,64,256]{2,1,0:T(8,128)(2,1)S(1)}, bf16[4,64,256]{2,1,0:T(8,128)(2,1)S(1)}, bf16[4,64,256]{2,1,0:T(8,128)(2,1)S(1)}) custom-call(s32[3]{0:T(128)S(1)} %pad_add_fusion.meta, f32[128,16]{1,0:T(8,128)S(1)} %copy.12.site_ref, bf16[32,256,256]{2,1,0:T(8,128)(2,1)} %all-to-all-done.left_hbm, ...), custom_call_target="tpu_custom_call" | custom-call | tf_op jit(solution)/shard_map/left_terms/pallas_call | solution.py:170
  77.3 4.0 %collective-permute-start.1 = (bf16[4,64,256]{2,1,0:T(8,128)(2,1)S(1)}, bf16[4,64,256]{2,1,0:T(8,128)(2,1)S(1)}, u32[]{:S(2)}, u32[]{:S(2)}) collective-permute-start(bf16[4,64,256]{2,1,0:T(8,128)(2,1)S(1)} %get-tuple-element.10), channel_id=1, source_target_pairs={{0,4},{2,6},{4,0},{6,2},{1,5},{3,7},{5,1},{7,3},{8,12},{10,14},{12... | collective-permute-start | bytes 393224 | tf_op jit(solution)/shard_map/ppermute | solution.py:219
  81.2 1.0 %collective-permute-start.2 = (bf16[4,64,256]{2,1,0:T(8,128)(2,1)S(1)}, bf16[4,64,256]{2,1,0:T(8,128)(2,1)S(1)}, u32[]{:S(2)}, u32[]{:S(2)}) collective-permute-start(bf16[4,64,256]{2,1,0:T(8,128)(2,1)S(1)} %get-tuple-element.11), channel_id=1, source_target_pairs={{0,2},{2,4},{4,6},{6,0},{1,3},{3,5},{5,7},{7,1},{8,10},{10,12},{12... | collective-permute-start | bytes 393224 | tf_op jit(solution)/shard_map/ppermute | solution.py:219
  82.2 2.2 %collective-permute-start.3 = (bf16[4,64,256]{2,1,0:T(8,128)(2,1)S(1)}, bf16[4,64,256]{2,1,0:T(8,128)(2,1)S(1)}, u32[]{:S(2)}, u32[]{:S(2)}) collective-permute-start(bf16[4,64,256]{2,1,0:T(8,128)(2,1)S(1)} %get-tuple-element.12), channel_id=1, source_target_pairs={{0,6},{2,0},{4,2},{6,4},{1,7},{3,1},{5,3},{7,5},{8,14},{10,8},{12,... | collective-permute-start | bytes 393224 | tf_op jit(solution)/shard_map/ppermute | solution.py:219
  84.4 0.1 dynamic_slice.19
  84.5 1.0 %collective-permute-done.1 = bf16[4,64,256]{2,1,0:T(8,128)(2,1)S(1)} collective-permute-done((bf16[4,64,256]{2,1,0:T(8,128)(2,1)S(1)}, bf16[4,64,256]{2,1,0:T(8,128)(2,1)S(1)}, u32[]{:S(2)}, u32[]{:S(2)}) %collective-permute-start.1) | collective-permute-done | bytes 131104 | tf_op jit(solution)/shard_map/ppermute | solution.py:219
  85.6 2.2 %collective-permute-done.2 = bf16[4,64,256]{2,1,0:T(8,128)(2,1)S(1)} collective-permute-done((bf16[4,64,256]{2,1,0:T(8,128)(2,1)S(1)}, bf16[4,64,256]{2,1,0:T(8,128)(2,1)S(1)}, u32[]{:S(2)}, u32[]{:S(2)}) %collective-permute-start.2) | collective-permute-done | bytes 131104 | tf_op jit(solution)/shard_map/ppermute | solution.py:219
  87.8 0.3 collective-permute-done.3
  88.0 0.1 multiply_convert_fusion
  88.2 0.1 copy.22
  88.2 0.1 collective-permute-start.4
  88.3 1.2 %collective-permute-done.4 = bf16[32,4,256]{2,1,0:T(4,128)(2,1)S(1)} collective-permute-done((bf16[32,4,256]{2,1,0:T(4,128)(2,1)S(1)}, bf16[32,4,256]{2,1,0:T(4,128)(2,1)S(1)}, u32[]{:S(2)}, u32[]{:S(2)}) %collective-permute-start.4) | collective-permute-done | bytes 65568 | tf_op jit(solution)/shard_map/ppermute | solution.py:227
  89.6 0.1 fusion.3
  89.7 0.7 pad_maximum_fusion
  (1 shorter events, 0.0 us)
Async XLA Ops:
  0.0 9.2 %copy-start = (bf16[2,256,4,256]{3,2,1,0:T(4,128)(2,1)S(1)}, bf16[2,256,4,256]{3,2,1,0:T(4,128)(2,1)}, u32[]{:S(2)}) copy-start(bf16[2,256,4,256]{3,2,1,0:T(4,128)(2,1)} %param.5) | copy-start | bytes 3145732
  0.0 9.6 %collective-permute-start = (bf16[2,16,1,256,256]{4,3,2,1,0:T(8,128)(2,1)}, bf16[2,16,1,256,256]{4,3,2,1,0:T(8,128)(2,1)}, u32[]{:S(2)}, u32[]{:S(2)}) collective-permute-start(bf16[2,16,1,256,256]{4,3,2,1,0:T(8,128)(2,1)} %own_hbm.1), channel_id=1, source_target_pairs={{0,1},{1,0},{2,3},{3,2},{4,5},{5,4},{6,7},{7,6},{8,9},{9,8},{10,11... | collective-permute-start | bytes 12582920 | tf_op jit(solution)/shard_map/ppermute | solution.py:202
  0.0 7.9 %copy-start.2 = (f32[128,4,4]{0,2,1:T(4,128)S(1)}, f32[128,4,4]{0,2,1:T(4,128)}, u32[]{:S(2)}) copy-start(f32[128,4,4]{0,2,1:T(4,128)} %param.9) | copy-start | bytes 24580
  0.0 8.0 %copy-start.3 = (s32[32]{0:T(128)S(1)}, s32[32]{0:T(128)}, u32[]{:S(2)}) copy-start(s32[32]{0:T(128)} %param.6) | copy-start | bytes 388
  0.0 62.4 %all-to-all-start = ((bf16[32,256,256]{2,1,0:T(8,128)(2,1)}), bf16[32,256,256]{2,1,0:T(8,128)(2,1)}, u32[]{:S(2)}, u32[]{:S(2)}) async-start(bf16[32,256,256]{2,1,0:T(8,128)(2,1)} %bitcast.29), calls=%async_computation | async-start | bytes 8388608 | tf_op jit(solution)/shard_map/all_to_all | solution.py:203
  9.6 2.2 %copy-start.1 = (bf16[2,16,1,256,256]{4,3,2,1,0:T(8,128)(2,1)S(1)}, bf16[2,16,1,256,256]{4,3,2,1,0:T(8,128)(2,1)}, u32[]{:S(2)}) copy-start(bf16[2,16,1,256,256]{4,3,2,1,0:T(8,128)(2,1)} %own_hbm.1) | copy-start | bytes 12582916
  77.3 8.3 %collective-permute-start.1 = (bf16[4,64,256]{2,1,0:T(8,128)(2,1)S(1)}, bf16[4,64,256]{2,1,0:T(8,128)(2,1)S(1)}, u32[]{:S(2)}, u32[]{:S(2)}) collective-permute-start(bf16[4,64,256]{2,1,0:T(8,128)(2,1)S(1)} %get-tuple-element.10), channel_id=1, source_target_pairs={{0,4},{2,6},{4,0},{6,2},{1,5},{3,7},{5,1},{7,3},{8,12},{10,14},{12... | collective-permute-start | bytes 393224 | tf_op jit(solution)/shard_map/ppermute | solution.py:219
  81.2 6.6 %collective-permute-start.2 = (bf16[4,64,256]{2,1,0:T(8,128)(2,1)S(1)}, bf16[4,64,256]{2,1,0:T(8,128)(2,1)S(1)}, u32[]{:S(2)}, u32[]{:S(2)}) collective-permute-start(bf16[4,64,256]{2,1,0:T(8,128)(2,1)S(1)} %get-tuple-element.11), channel_id=1, source_target_pairs={{0,2},{2,4},{4,6},{6,0},{1,3},{3,5},{5,7},{7,1},{8,10},{10,12},{12... | collective-permute-start | bytes 393224 | tf_op jit(solution)/shard_map/ppermute | solution.py:219
  82.2 5.8 %collective-permute-start.3 = (bf16[4,64,256]{2,1,0:T(8,128)(2,1)S(1)}, bf16[4,64,256]{2,1,0:T(8,128)(2,1)S(1)}, u32[]{:S(2)}, u32[]{:S(2)}) collective-permute-start(bf16[4,64,256]{2,1,0:T(8,128)(2,1)S(1)} %get-tuple-element.12), channel_id=1, source_target_pairs={{0,6},{2,0},{4,2},{6,4},{1,7},{3,1},{5,3},{7,5},{8,14},{10,8},{12,... | collective-permute-start | bytes 393224 | tf_op jit(solution)/shard_map/ppermute | solution.py:219
  88.2 1.3 %collective-permute-start.4 = (bf16[32,4,256]{2,1,0:T(4,128)(2,1)S(1)}, bf16[32,4,256]{2,1,0:T(4,128)(2,1)S(1)}, u32[]{:S(2)}, u32[]{:S(2)}) collective-permute-start(bf16[32,4,256]{2,1,0:T(4,128)(2,1)S(1)} %bitcast.31), channel_id=1, source_target_pairs={{0,1},{1,0},{2,3},{3,2},{4,5},{5,4},{6,7},{7,6},{8,9},{9,8},{10,11... | collective-permute-start | bytes 196616 | tf_op jit(solution)/shard_map/ppermute | solution.py:227

commit v6 on v2

--- a/solution.py
+++ b/solution.py
@@ -11,16 +11,17 @@
 GROUP = 2
 ROWS = 16
 LEFT_TERMS = 2
-VMEM_LIMIT = 48 << 20
+KEPT = 2
+VMEM_LIMIT = 52 << 20
 
 
-def right_kernel(group, meta, site_ref, wave_ref, own_ref, other_ref, held_ref, first):
+def right_kernel(group, base, meta, site_ref, wave_ref, own_ref, other_ref, held_ref, first):
     step = pl.program_id(0)
     core, z_at, sec_count = meta[0], meta[1], meta[2]
     p_size, width = wave_ref.shape[0], wave_ref.shape[1]
     waves = wave_ref[...].reshape(p_size * width, width)
     for at in range(group):
-        source = step * group + at
+        source = base + step * group + at
         for slot in range(CORES):
             side = core if slot == 0 else 1 - core
             term = source * sec_count + z_at * CORES + side
@@ -42,14 +43,14 @@
                     )
 
 
-def right_call(meta, site, wave, own, other):
-    sources, width = own.shape[1], own.shape[-1]
+def right_call(meta, site, wave, own, other, base, sources):
+    width = own.shape[-1]
     p_size = wave.shape[0]
     right_spec = pl.BlockSpec(
-        (1, GROUP, 1, width, width), lambda step, meta: (meta[0], step, 0, 0, 0)
+        (1, GROUP, 1, width, width), lambda step, meta: (meta[0], base // GROUP + step, 0, 0, 0)
     )
     return pl.pallas_call(
-        functools.partial(right_kernel, GROUP),
+        functools.partial(right_kernel, GROUP, base),
         grid_spec=pltpu.PrefetchScalarGridSpec(
             num_scalar_prefetch=1,
             grid=(sources // GROUP,),
@@ -70,29 +71,31 @@
     )(meta, site, wave, own, other)
 
 
-def left_kernel(z_count, p_size, meta, left_hbm, held_hbm, *refs):
+def left_kernel(z_count, p_size, meta, left_hbm, kept_ref, held_hbm, *refs):
     outs = refs[:z_count]
     left, held, total, left_sem, held_sem = refs[z_count:]
     z_at = meta[1]
     terms, width = left.shape[0], left.shape[1]
+    kept = kept_ref.shape[0]
     copies = []
     for at in range(0, terms, LEFT_TERMS):
         span = pl.ds(at, LEFT_TERMS)
         slot = at // LEFT_TERMS
-        pair = (
-            pltpu.make_async_copy(left_hbm.at[span], left.at[span], left_sem.at[slot]),
-            pltpu.make_async_copy(held_hbm.at[span], held.at[span], held_sem.at[slot]),
-        )
-        for copy in pair:
+        now = [pltpu.make_async_copy(left_hbm.at[span], left.at[span], left_sem.at[slot])]
+        if at >= kept:
+            span = pl.ds(at - kept, LEFT_TERMS)
+            now.append(pltpu.make_async_copy(held_hbm.at[span], held.at[span], held_sem.at[slot]))
+        for copy in now:
             copy.start()
-        copies.append(pair)
+        copies.append(now)
 
-    for slot, pair in enumerate(copies):
-        for copy in pair:
+    for slot, now in enumerate(copies):
+        for copy in now:
             copy.wait()
         add = None
         for at in range(slot * LEFT_TERMS, (slot + 1) * LEFT_TERMS):
-            product = jnp.dot(left[at], held[at], preferred_element_type=jnp.float32)
+            right = kept_ref[at] if at < kept else held[at - kept]
+            product = jnp.dot(left[at], right, preferred_element_type=jnp.float32)
             add = product if add is None else add + product
         if slot == 0:
             total[...] = add
@@ -107,8 +110,9 @@
             outs[shift][q] = block[:, q * width : (q + 1) * width].astype(outs[shift].dtype)
 
 
-def left_call(meta, left, held, z_count):
-    terms, width, columns = held.shape
+def left_call(meta, left, kept, held, z_count):
+    terms, width = left.shape[:2]
+    columns = held.shape[2]
     p_size = columns // width
     rows = width // z_count
     return pl.pallas_call(
@@ -116,6 +120,7 @@
         in_specs=[
             pl.BlockSpec(memory_space=pltpu.SMEM),
             pl.BlockSpec(memory_space=pl.ANY),
+            pl.BlockSpec(memory_space=pltpu.VMEM),
             pl.BlockSpec(memory_space=pl.ANY),
         ],
         out_specs=[pl.BlockSpec(memory_space=pltpu.VMEM)] * z_count,
@@ -125,14 +130,14 @@
         ],
         scratch_shapes=[
             pltpu.VMEM((terms, width, width), jnp.bfloat16),
-            pltpu.VMEM((terms, width, columns), jnp.bfloat16),
+            pltpu.VMEM(held.shape, jnp.bfloat16),
             pltpu.VMEM((width, columns), jnp.float32),
             pltpu.SemaphoreType.DMA((terms // LEFT_TERMS,)),
             pltpu.SemaphoreType.DMA((terms // LEFT_TERMS,)),
         ],
         compiler_params=pltpu.CompilerParams(vmem_limit_bytes=VMEM_LIMIT),
         name="left_terms",
-    )(meta, left, held)
+    )(meta, left, kept, held)
 
 
 def shards(wave, sector_dims, left_ops, right_ops, site_ops):
@@ -152,8 +157,10 @@
 
     meta = jnp.stack([core, z_at, jnp.int32(z_count * CORES)]).astype(jnp.int32)
     site = site_ops.reshape(site_ops.shape[0], -1)
-    held = right_call(meta, site, masked, right_ops, other)
-    parts = left_call(meta, left, held, z_count)
+    sources = right_ops.shape[1]
+    held = right_call(meta, site, masked, right_ops, other, KEPT, sources - KEPT)
+    kept = right_call(meta, site, masked, right_ops, other, 0, KEPT)
+    parts = left_call(meta, left, kept, held, z_count)
 
     total = parts[0]
     for shift in sorted(range(1, z_count), key=lambda s: -min(s, z_count - s)):

time: 84.4 us -> 84.9 us (level)
  Pallas kernels: 25 us -> 29.1 us
  local copies, waits for them, and re-layouts: 3.23 us -> 1.06 us
  waiting for transfers between devices: 38.7 us -> 37.1 us
    pallas_call x1 -> x2, Pallas kernels: 16.7 us -> 20.3 us  [right_call(): pl.pallas_call(functools.partial(right_kernel, GROUP, base), grid_spec=pl...]
    unnamed x8 -> x6, local copies, waits for them, and re-layouts: 2.2 us -> 0.01 us
    all_to_all x1, waiting for transfers between devices: 33.9 us -> 32.4 us  [shards(): lax.all_to_all(left_ops[:, 0], ('op', 'core'), split_axis=0, concat_axis=...]
  transfers between devices with their start and end apart: 6 -> 6, of which waited for: 5 -> 5; matrix products, arithmetic and copies ran while one was open for 2% -> 2% of each run, Pallas kernels for 20% -> 24%
where the time goes in v6:
time: 84.9 us; the launch traced here: 84.4 us
  waiting for transfers between devices  37.1 us (44%)
  Pallas kernels  29.1 us (34%)
  starting transfers between devices  15.1 us (18%)
  other arithmetic  1.82 us (2%)
  local copies, waits for them, and re-layouts  1.06 us (1%)
    all_to_all x1, waiting for transfers between devices, shards(): lax.all_to_all(left_ops[:, 0], ('op', 'core'), split_axis=0, concat_axis=...  32.4 us
    pallas_call x2, Pallas kernels, right_call(): pl.pallas_call(functools.partial(right_kernel, GROUP, base), grid_spec=pl...  20.3 us
    pallas_call x1, Pallas kernels, left_call(): pl.pallas_call(functools.partial(left_kernel, z_count, p_size), in_specs=...  8.8 us
    all_to_all x1, starting transfers between devices, shards(): lax.all_to_all(left_ops[:, 0], ('op', 'core'), split_axis=0, concat_axis=...  7.81 us
    ppermute x3, starting transfers between devices, shards(): total = total + lax.ppermute(parts[shift], 'z', ring).astype(jnp.float32)  7.19 us
    ppermute x3, waiting for transfers between devices, shards(): total = total + lax.ppermute(parts[shift], 'z', ring).astype(jnp.float32)  3.53 us
  transfers between devices with their start and end apart: 6, of which 5 were waited for; matrix products, arithmetic and copies ran while one was open for 2% of the time, Pallas kernels for 24%

profile of v6, /device:TPU:8, one launch (start us, length us, event | category | flops | bytes accessed | tf_op | source)
XLA Modules:
  0.0 84.4 jit_solution(2106094189022865418)
XLA Ops:
  0.0 0.0 copy-start
  0.0 0.0 collective-permute-start
  0.0 0.0 copy-start.1
  0.0 0.0 copy-start.2
  0.0 7.8 %all-to-all-start = ((bf16[32,256,256]{2,1,0:T(8,128)(2,1)}), bf16[32,256,256]{2,1,0:T(8,128)(2,1)}, u32[]{:S(2)}, u32[]{:S(2)}) async-start(bf16[32,256,256]{2,1,0:T(8,128)(2,1)} %bitcast.29), calls=%async_computation | async-start | bytes 8388608 | tf_op jit(solution)/shard_map/all_to_all | solution.py:150
  7.9 0.0 copy-done.1
  7.9 0.1 copy.11.site_ref
  8.0 0.0 copy-done.2
  8.0 0.6 dynamic_slice.18
  8.6 0.1 pad_add_fusion.meta
  8.7 0.6 compare_convert_fusion
  9.3 0.0 copy-done
  9.3 0.2 constant_dynamic-slice_fusion.2
  9.5 0.2 fusion.2.wave_ref
  9.7 0.0 collective-permute-done.other_ref
  9.7 15.2 %right_terms.3.held_hbm = bf16[28,256,1024]{2,1,0:T(8,128)(2,1)} custom-call(s32[3]{0:T(128)S(1)} %pad_add_fusion.meta, f32[128,16]{1,0:T(8,128)S(1)} %copy.11.site_ref, bf16[4,256,256]{2,1,0:T(8,128)(2,1)S(1)} %fusion.2.wave_ref, bf16[2,16,1,256,256]{4,3,2,1,0:T(8,128)(2,1)} %own_ref.3, bf16[2,16,1,256,256]{4,3,2,1,0:T(8,128)(2,1)} %collective-permute-done.other_ref), custom_call_target="tpu_custom_call" | custom-call | tf_op jit(solution)/shard_map/right_terms/pallas_call | solution.py:52
  24.9 5.1 %right_terms.2.kept_ref = bf16[4,256,1024]{2,1,0:T(8,128)(2,1)} custom-call(s32[3]{0:T(128)S(1)} %pad_add_fusion.meta, f32[128,16]{1,0:T(8,128)S(1)} %copy.11.site_ref, bf16[4,256,256]{2,1,0:T(8,128)(2,1)S(1)} %fusion.2.wave_ref, bf16[2,16,1,256,256]{4,3,2,1,0:T(8,128)(2,1)} %own_ref.3, bf16[2,16,1,256,256]{4,3,2,1,0:T(8,128)(2,1)} %collective-permute-done.other_ref), custom_call_target="tpu_custom_call" | custom-call | tf_op jit(solution)/shard_map/right_terms/pallas_call | solution.py:52
  30.0 32.4 %all-to-all-done.left_hbm = bf16[32,256,256]{2,1,0:T(8,128)(2,1)} async-done(((bf16[32,256,256]{2,1,0:T(8,128)(2,1)}), bf16[32,256,256]{2,1,0:T(8,128)(2,1)}, u32[]{:S(2)}, u32[]{:S(2)}) %all-to-all-start) | async-done | bytes 4194336 | tf_op jit(solution)/shard_map/all_to_all | solution.py:150
  62.4 8.8 %left_terms.1 = (f32[4,64,256]{2,1,0:T(8,128)S(1)}, bf16[4,64,256]{2,1,0:T(8,128)(2,1)S(1)}, bf16[4,64,256]{2,1,0:T(8,128)(2,1)S(1)}, bf16[4,64,256]{2,1,0:T(8,128)(2,1)S(1)}) custom-call(s32[3]{0:T(128)S(1)} %pad_add_fusion.meta, bf16[32,256,256]{2,1,0:T(8,128)(2,1)} %all-to-all-done.left_hbm, bf16[4,256,1024]{2,1,0:T(8,128)(2,1)} %right_terms.2.kept_ref, ...), custom_call_target="tpu_custom_call" | custom-call | tf_op jit(solution)/shard_map/left_terms/pallas_call | solution.py:118
  71.2 4.0 %collective-permute-start.1 = (bf16[4,64,256]{2,1,0:T(8,128)(2,1)S(1)}, bf16[4,64,256]{2,1,0:T(8,128)(2,1)S(1)}, u32[]{:S(2)}, u32[]{:S(2)}) collective-permute-start(bf16[4,64,256]{2,1,0:T(8,128)(2,1)S(1)} %get-tuple-element.10), channel_id=1, source_target_pairs={{0,4},{2,6},{4,0},{6,2},{1,5},{3,7},{5,1},{7,3},{8,12},{10,14},{12... | collective-permute-start | bytes 393224 | tf_op jit(solution)/shard_map/ppermute | solution.py:168
  75.2 1.0 %collective-permute-start.2 = (bf16[4,64,256]{2,1,0:T(8,128)(2,1)S(1)}, bf16[4,64,256]{2,1,0:T(8,128)(2,1)S(1)}, u32[]{:S(2)}, u32[]{:S(2)}) collective-permute-start(bf16[4,64,256]{2,1,0:T(8,128)(2,1)S(1)} %get-tuple-element.11), channel_id=1, source_target_pairs={{0,2},{2,4},{4,6},{6,0},{1,3},{3,5},{5,7},{7,1},{8,10},{10,12},{12... | collective-permute-start | bytes 393224 | tf_op jit(solution)/shard_map/ppermute | solution.py:168
  76.2 2.2 %collective-permute-start.3 = (bf16[4,64,256]{2,1,0:T(8,128)(2,1)S(1)}, bf16[4,64,256]{2,1,0:T(8,128)(2,1)S(1)}, u32[]{:S(2)}, u32[]{:S(2)}) collective-permute-start(bf16[4,64,256]{2,1,0:T(8,128)(2,1)S(1)} %get-tuple-element.12), channel_id=1, source_target_pairs={{0,6},{2,0},{4,2},{6,4},{1,7},{3,1},{5,3},{7,5},{8,14},{10,8},{12,... | collective-permute-start | bytes 393224 | tf_op jit(solution)/shard_map/ppermute | solution.py:168
  78.4 0.1 dynamic_slice.19
  78.5 1.0 %collective-permute-done.1 = bf16[4,64,256]{2,1,0:T(8,128)(2,1)S(1)} collective-permute-done((bf16[4,64,256]{2,1,0:T(8,128)(2,1)S(1)}, bf16[4,64,256]{2,1,0:T(8,128)(2,1)S(1)}, u32[]{:S(2)}, u32[]{:S(2)}) %collective-permute-start.1) | collective-permute-done | bytes 131104 | tf_op jit(solution)/shard_map/ppermute | solution.py:168
  79.5 2.2 %collective-permute-done.2 = bf16[4,64,256]{2,1,0:T(8,128)(2,1)S(1)} collective-permute-done((bf16[4,64,256]{2,1,0:T(8,128)(2,1)S(1)}, bf16[4,64,256]{2,1,0:T(8,128)(2,1)S(1)}, u32[]{:S(2)}, u32[]{:S(2)}) %collective-permute-start.2) | collective-permute-done | bytes 131104 | tf_op jit(solution)/shard_map/ppermute | solution.py:168
  81.7 0.3 collective-permute-done.3
  82.0 0.1 multiply_convert_fusion
  82.1 0.1 copy.22
  82.2 0.1 collective-permute-start.4
  82.3 1.2 %collective-permute-done.4 = bf16[32,4,256]{2,1,0:T(4,128)(2,1)S(1)} collective-permute-done((bf16[32,4,256]{2,1,0:T(4,128)(2,1)S(1)}, bf16[32,4,256]{2,1,0:T(4,128)(2,1)S(1)}, u32[]{:S(2)}, u32[]{:S(2)}) %collective-permute-start.4) | collective-permute-done | bytes 65568 | tf_op jit(solution)/shard_map/ppermute | solution.py:176
  83.5 0.1 fusion.3
  83.6 0.7 pad_maximum_fusion
  (1 shorter events, 0.0 us)
Async XLA Ops:
  0.0 9.3 %copy-start = (bf16[2,256,4,256]{3,2,1,0:T(4,128)(2,1)S(1)}, bf16[2,256,4,256]{3,2,1,0:T(4,128)(2,1)}, u32[]{:S(2)}) copy-start(bf16[2,256,4,256]{3,2,1,0:T(4,128)(2,1)} %param.5) | copy-start | bytes 3145732
  0.0 9.7 %collective-permute-start = (bf16[2,16,1,256,256]{4,3,2,1,0:T(8,128)(2,1)}, bf16[2,16,1,256,256]{4,3,2,1,0:T(8,128)(2,1)}, u32[]{:S(2)}, u32[]{:S(2)}) collective-permute-start(bf16[2,16,1,256,256]{4,3,2,1,0:T(8,128)(2,1)} %own_ref.3), channel_id=1, source_target_pairs={{0,1},{1,0},{2,3},{3,2},{4,5},{5,4},{6,7},{7,6},{8,9},{9,8},{10,11... | collective-permute-start | bytes 12582920 | tf_op jit(solution)/shard_map/ppermute | solution.py:149
  0.0 7.9 %copy-start.1 = (f32[128,4,4]{0,2,1:T(4,128)S(1)}, f32[128,4,4]{0,2,1:T(4,128)}, u32[]{:S(2)}) copy-start(f32[128,4,4]{0,2,1:T(4,128)} %param.9) | copy-start | bytes 24580
  0.0 8.0 %copy-start.2 = (s32[32]{0:T(128)S(1)}, s32[32]{0:T(128)}, u32[]{:S(2)}) copy-start(s32[32]{0:T(128)} %param.6) | copy-start | bytes 388
  0.0 62.4 %all-to-all-start = ((bf16[32,256,256]{2,1,0:T(8,128)(2,1)}), bf16[32,256,256]{2,1,0:T(8,128)(2,1)}, u32[]{:S(2)}, u32[]{:S(2)}) async-start(bf16[32,256,256]{2,1,0:T(8,128)(2,1)} %bitcast.29), calls=%async_computation | async-start | bytes 8388608 | tf_op jit(solution)/shard_map/all_to_all | solution.py:150
  71.2 8.3 %collective-permute-start.1 = (bf16[4,64,256]{2,1,0:T(8,128)(2,1)S(1)}, bf16[4,64,256]{2,1,0:T(8,128)(2,1)S(1)}, u32[]{:S(2)}, u32[]{:S(2)}) collective-permute-start(bf16[4,64,256]{2,1,0:T(8,128)(2,1)S(1)} %get-tuple-element.10), channel_id=1, source_target_pairs={{0,4},{2,6},{4,0},{6,2},{1,5},{3,7},{5,1},{7,3},{8,12},{10,14},{12... | collective-permute-start | bytes 393224 | tf_op jit(solution)/shard_map/ppermute | solution.py:168
  75.2 6.6 %collective-permute-start.2 = (bf16[4,64,256]{2,1,0:T(8,128)(2,1)S(1)}, bf16[4,64,256]{2,1,0:T(8,128)(2,1)S(1)}, u32[]{:S(2)}, u32[]{:S(2)}) collective-permute-start(bf16[4,64,256]{2,1,0:T(8,128)(2,1)S(1)} %get-tuple-element.11), channel_id=1, source_target_pairs={{0,2},{2,4},{4,6},{6,0},{1,3},{3,5},{5,7},{7,1},{8,10},{10,12},{12... | collective-permute-start | bytes 393224 | tf_op jit(solution)/shard_map/ppermute | solution.py:168
  76.2 5.8 %collective-permute-start.3 = (bf16[4,64,256]{2,1,0:T(8,128)(2,1)S(1)}, bf16[4,64,256]{2,1,0:T(8,128)(2,1)S(1)}, u32[]{:S(2)}, u32[]{:S(2)}) collective-permute-start(bf16[4,64,256]{2,1,0:T(8,128)(2,1)S(1)} %get-tuple-element.12), channel_id=1, source_target_pairs={{0,6},{2,0},{4,2},{6,4},{1,7},{3,1},{5,3},{7,5},{8,14},{10,8},{12,... | collective-permute-start | bytes 393224 | tf_op jit(solution)/shard_map/ppermute | solution.py:168
  82.2 1.3 %collective-permute-start.4 = (bf16[32,4,256]{2,1,0:T(4,128)(2,1)S(1)}, bf16[32,4,256]{2,1,0:T(4,128)(2,1)S(1)}, u32[]{:S(2)}, u32[]{:S(2)}) collective-permute-start(bf16[32,4,256]{2,1,0:T(4,128)(2,1)S(1)} %bitcast.31), channel_id=1, source_target_pairs={{0,1},{1,0},{2,3},{3,2},{4,5},{5,4},{6,7},{7,6},{8,9},{9,8},{10,11... | collective-permute-start | bytes 196616 | tf_op jit(solution)/shard_map/ppermute | solution.py:176

commit v7 on v6

--- a/solution.py
+++ b/solution.py
@@ -12,7 +12,8 @@
 ROWS = 16
 LEFT_TERMS = 2
 KEPT = 2
-VMEM_LIMIT = 52 << 20
+VMEM_LIMIT = 32 << 20
+TAIL_VMEM = 48 << 20
 
 
 def right_kernel(group, base, meta, site_ref, wave_ref, own_ref, other_ref, held_ref, first):
@@ -135,7 +136,7 @@
             pltpu.SemaphoreType.DMA((terms // LEFT_TERMS,)),
             pltpu.SemaphoreType.DMA((terms // LEFT_TERMS,)),
         ],
-        compiler_params=pltpu.CompilerParams(vmem_limit_bytes=VMEM_LIMIT),
+        compiler_params=pltpu.CompilerParams(vmem_limit_bytes=TAIL_VMEM),
         name="left_terms",
     )(meta, left, kept, held)
 

time: 84.9 us -> 84.7 us (level)
  local copies, waits for them, and re-layouts: 1.06 us -> 3.22 us
  Pallas kernels: 29.1 us -> 27.3 us
    unnamed x6 -> x8, local copies, waits for them, and re-layouts: 0.01 us -> 2.2 us
    pallas_call x2, Pallas kernels: 20.3 us -> 18.8 us  [right_call(): pl.pallas_call(functools.partial(right_kernel, GROUP, base), grid_spec=pl...]
  transfers between devices with their start and end apart: 6 -> 6, of which waited for: 5 -> 5; matrix products, arithmetic and copies ran while one was open for 2% -> 2% of each run, Pallas kernels for 24% -> 22%
where the time goes in v7:
time: 84.7 us; the launch traced here: 84.2 us
  waiting for transfers between devices  36.6 us (43%)
  Pallas kernels  27.3 us (32%)
  starting transfers between devices  15.1 us (18%)
  local copies, waits for them, and re-layouts  3.22 us (4%)
  other arithmetic  1.83 us (2%)
    all_to_all x1, waiting for transfers between devices, shards(): lax.all_to_all(left_ops[:, 0], ('op', 'core'), split_axis=0, concat_axis=...  31.6 us
    pallas_call x2, Pallas kernels, right_call(): pl.pallas_call(functools.partial(right_kernel, GROUP, base), grid_spec=pl...  18.8 us
    pallas_call x1, Pallas kernels, left_call(): pl.pallas_call(functools.partial(left_kernel, z_count, p_size), in_specs=...  8.42 us
    all_to_all x1, starting transfers between devices, shards(): lax.all_to_all(left_ops[:, 0], ('op', 'core'), split_axis=0, concat_axis=...  7.81 us
    ppermute x3, starting transfers between devices, shards(): total = total + lax.ppermute(parts[shift], 'z', ring).astype(jnp.float32)  7.19 us
    ppermute x3, waiting for transfers between devices, shards(): total = total + lax.ppermute(parts[shift], 'z', ring).astype(jnp.float32)  3.74 us
    unnamed x8, local copies, waits for them, and re-layouts  2.2 us
  transfers between devices with their start and end apart: 6, of which 5 were waited for; matrix products, arithmetic and copies ran while one was open for 2% of the time, Pallas kernels for 22%

profile of v7, /device:TPU:8, one launch (start us, length us, event | category | flops | bytes accessed | tf_op | source)
XLA Modules:
  0.0 84.2 jit_solution(8133135341325248766)
XLA Ops:
  0.0 0.0 copy-start
  0.0 0.0 collective-permute-start
  0.0 0.0 copy-start.2
  0.0 0.0 copy-start.3
  0.0 7.8 %all-to-all-start = ((bf16[32,256,256]{2,1,0:T(8,128)(2,1)}), bf16[32,256,256]{2,1,0:T(8,128)(2,1)}, u32[]{:S(2)}, u32[]{:S(2)}) async-start(bf16[32,256,256]{2,1,0:T(8,128)(2,1)} %bitcast.29), calls=%async_computation | async-start | bytes 8388608 | tf_op jit(solution)/shard_map/all_to_all | solution.py:151
  7.9 0.0 copy-done.2
  7.9 0.1 copy.11.site_ref
  8.0 0.0 copy-done.3
  8.0 0.6 dynamic_slice.18
  8.6 0.1 pad_add_fusion.meta
  8.6 0.6 compare_convert_fusion
  9.3 0.0 copy-done
  9.3 0.2 constant_dynamic-slice_fusion.2
  9.5 0.2 fusion.2.wave_ref
  9.7 0.0 collective-permute-done.other_ref
  9.7 0.0 copy-start.1
  9.7 2.2 %copy-done.1 = bf16[2,16,1,256,256]{4,3,2,1,0:T(8,128)(2,1)S(1)} copy-done((bf16[2,16,1,256,256]{4,3,2,1,0:T(8,128)(2,1)S(1)}, bf16[2,16,1,256,256]{4,3,2,1,0:T(8,128)(2,1)}, u32[]{:S(2)}) %copy-start.1) | copy-done | bytes 4194328
  11.9 15.1 %right_terms.3.held_hbm = bf16[28,256,1024]{2,1,0:T(8,128)(2,1)} custom-call(s32[3]{0:T(128)S(1)} %pad_add_fusion.meta, f32[128,16]{1,0:T(8,128)S(1)} %copy.11.site_ref, bf16[4,256,256]{2,1,0:T(8,128)(2,1)S(1)} %fusion.2.wave_ref, bf16[2,16,1,256,256]{4,3,2,1,0:T(8,128)(2,1)S(1)} %copy-done.1, bf16[2,16,1,256,256]{4,3,2,1,0:T(8,128)(2,1)} %collective-permute-done.other_ref), custom_call_target="tpu_custom_call" | custom-call | tf_op jit(solution)/shard_map/right_terms/pallas_call | solution.py:53
  27.0 3.8 %right_terms.2.kept_ref = bf16[4,256,1024]{2,1,0:T(8,128)(2,1)S(1)} custom-call(s32[3]{0:T(128)S(1)} %pad_add_fusion.meta, f32[128,16]{1,0:T(8,128)S(1)} %copy.11.site_ref, bf16[4,256,256]{2,1,0:T(8,128)(2,1)S(1)} %fusion.2.wave_ref, bf16[2,16,1,256,256]{4,3,2,1,0:T(8,128)(2,1)S(1)} %copy-done.1, bf16[2,16,1,256,256]{4,3,2,1,0:T(8,128)(2,1)} %collective-permute-done.other_ref), custom_call_target="tpu_custom_call" | custom-call | tf_op jit(solution)/shard_map/right_terms/pallas_call | solution.py:53
  30.7 31.6 %all-to-all-done.left_hbm = bf16[32,256,256]{2,1,0:T(8,128)(2,1)} async-done(((bf16[32,256,256]{2,1,0:T(8,128)(2,1)}), bf16[32,256,256]{2,1,0:T(8,128)(2,1)}, u32[]{:S(2)}, u32[]{:S(2)}) %all-to-all-start) | async-done | bytes 4194336 | tf_op jit(solution)/shard_map/all_to_all | solution.py:151
  62.4 8.4 %left_terms.1 = (f32[4,64,256]{2,1,0:T(8,128)S(1)}, bf16[4,64,256]{2,1,0:T(8,128)(2,1)}, bf16[4,64,256]{2,1,0:T(8,128)(2,1)}, bf16[4,64,256]{2,1,0:T(8,128)(2,1)S(1)}) custom-call(s32[3]{0:T(128)S(1)} %pad_add_fusion.meta, bf16[32,256,256]{2,1,0:T(8,128)(2,1)} %all-to-all-done.left_hbm, bf16[4,256,1024]{2,1,0:T(8,128)(2,1)S(1)} %right_terms.2.kept_ref, ...), custom_call_target="tpu_custom_call" | custom-call | tf_op jit(solution)/shard_map/left_terms/pallas_call | solution.py:119
  70.8 4.0 %collective-permute-start.1 = (bf16[4,64,256]{2,1,0:T(8,128)(2,1)}, bf16[4,64,256]{2,1,0:T(8,128)(2,1)S(1)}, u32[]{:S(2)}, u32[]{:S(2)}) collective-permute-start(bf16[4,64,256]{2,1,0:T(8,128)(2,1)} %get-tuple-element.10), channel_id=1, source_target_pairs={{0,4},{2,6},{4,0},{6,2},{1,5},{3,7},{5,1},{7,3},{8,12},{10,14},{12... | collective-permute-start | bytes 393224 | tf_op jit(solution)/shard_map/ppermute | solution.py:169
  74.8 1.0 %collective-permute-start.2 = (bf16[4,64,256]{2,1,0:T(8,128)(2,1)}, bf16[4,64,256]{2,1,0:T(8,128)(2,1)S(1)}, u32[]{:S(2)}, u32[]{:S(2)}) collective-permute-start(bf16[4,64,256]{2,1,0:T(8,128)(2,1)} %get-tuple-element.11), channel_id=1, source_target_pairs={{0,2},{2,4},{4,6},{6,0},{1,3},{3,5},{5,7},{7,1},{8,10},{10,12},{12... | collective-permute-start | bytes 393224 | tf_op jit(solution)/shard_map/ppermute | solution.py:169
  75.8 2.2 %collective-permute-start.3 = (bf16[4,64,256]{2,1,0:T(8,128)(2,1)S(1)}, bf16[4,64,256]{2,1,0:T(8,128)(2,1)S(1)}, u32[]{:S(2)}, u32[]{:S(2)}) collective-permute-start(bf16[4,64,256]{2,1,0:T(8,128)(2,1)S(1)} %get-tuple-element.12), channel_id=1, source_target_pairs={{0,6},{2,0},{4,2},{6,4},{1,7},{3,1},{5,3},{7,5},{8,14},{10,8},{12,... | collective-permute-start | bytes 393224 | tf_op jit(solution)/shard_map/ppermute | solution.py:169
  78.0 0.1 dynamic_slice.19
  78.1 1.3 %collective-permute-done.1 = bf16[4,64,256]{2,1,0:T(8,128)(2,1)S(1)} collective-permute-done((bf16[4,64,256]{2,1,0:T(8,128)(2,1)}, bf16[4,64,256]{2,1,0:T(8,128)(2,1)S(1)}, u32[]{:S(2)}, u32[]{:S(2)}) %collective-permute-start.1) | collective-permute-done | bytes 131104 | tf_op jit(solution)/shard_map/ppermute | solution.py:169
  79.3 2.2 %collective-permute-done.2 = bf16[4,64,256]{2,1,0:T(8,128)(2,1)S(1)} collective-permute-done((bf16[4,64,256]{2,1,0:T(8,128)(2,1)}, bf16[4,64,256]{2,1,0:T(8,128)(2,1)S(1)}, u32[]{:S(2)}, u32[]{:S(2)}) %collective-permute-start.2) | collective-permute-done | bytes 131104 | tf_op jit(solution)/shard_map/ppermute | solution.py:169
  81.6 0.3 collective-permute-done.3
  81.8 0.1 multiply_convert_fusion
  82.0 0.1 copy.22
  82.0 0.1 collective-permute-start.4
  82.1 1.2 %collective-permute-done.4 = bf16[32,4,256]{2,1,0:T(4,128)(2,1)S(1)} collective-permute-done((bf16[32,4,256]{2,1,0:T(4,128)(2,1)S(1)}, bf16[32,4,256]{2,1,0:T(4,128)(2,1)S(1)}, u32[]{:S(2)}, u32[]{:S(2)}) %collective-permute-start.4) | collective-permute-done | bytes 65568 | tf_op jit(solution)/shard_map/ppermute | solution.py:177
  83.3 0.1 fusion.3
  83.4 0.7 pad_maximum_fusion
  (1 shorter events, 0.0 us)
Async XLA Ops:
  0.0 9.3 %copy-start = (bf16[2,256,4,256]{3,2,1,0:T(4,128)(2,1)S(1)}, bf16[2,256,4,256]{3,2,1,0:T(4,128)(2,1)}, u32[]{:S(2)}) copy-start(bf16[2,256,4,256]{3,2,1,0:T(4,128)(2,1)} %param.5) | copy-start | bytes 3145732
  0.0 9.7 %collective-permute-start = (bf16[2,16,1,256,256]{4,3,2,1,0:T(8,128)(2,1)}, bf16[2,16,1,256,256]{4,3,2,1,0:T(8,128)(2,1)}, u32[]{:S(2)}, u32[]{:S(2)}) collective-permute-start(bf16[2,16,1,256,256]{4,3,2,1,0:T(8,128)(2,1)} %own_ref.3), channel_id=1, source_target_pairs={{0,1},{1,0},{2,3},{3,2},{4,5},{5,4},{6,7},{7,6},{8,9},{9,8},{10,11... | collective-permute-start | bytes 12582920 | tf_op jit(solution)/shard_map/ppermute | solution.py:150
  0.0 7.9 %copy-start.2 = (f32[128,4,4]{0,2,1:T(4,128)S(1)}, f32[128,4,4]{0,2,1:T(4,128)}, u32[]{:S(2)}) copy-start(f32[128,4,4]{0,2,1:T(4,128)} %param.9) | copy-start | bytes 24580
  0.0 8.0 %copy-start.3 = (s32[32]{0:T(128)S(1)}, s32[32]{0:T(128)}, u32[]{:S(2)}) copy-start(s32[32]{0:T(128)} %param.6) | copy-start | bytes 388
  0.0 62.4 %all-to-all-start = ((bf16[32,256,256]{2,1,0:T(8,128)(2,1)}), bf16[32,256,256]{2,1,0:T(8,128)(2,1)}, u32[]{:S(2)}, u32[]{:S(2)}) async-start(bf16[32,256,256]{2,1,0:T(8,128)(2,1)} %bitcast.29), calls=%async_computation | async-start | bytes 8388608 | tf_op jit(solution)/shard_map/all_to_all | solution.py:151
  9.7 2.2 %copy-start.1 = (bf16[2,16,1,256,256]{4,3,2,1,0:T(8,128)(2,1)S(1)}, bf16[2,16,1,256,256]{4,3,2,1,0:T(8,128)(2,1)}, u32[]{:S(2)}) copy-start(bf16[2,16,1,256,256]{4,3,2,1,0:T(8,128)(2,1)} %own_ref.3) | copy-start | bytes 12582916
  70.8 8.5 %collective-permute-start.1 = (bf16[4,64,256]{2,1,0:T(8,128)(2,1)}, bf16[4,64,256]{2,1,0:T(8,128)(2,1)S(1)}, u32[]{:S(2)}, u32[]{:S(2)}) collective-permute-start(bf16[4,64,256]{2,1,0:T(8,128)(2,1)} %get-tuple-element.10), channel_id=1, source_target_pairs={{0,4},{2,6},{4,0},{6,2},{1,5},{3,7},{5,1},{7,3},{8,12},{10,14},{12... | collective-permute-start | bytes 393224 | tf_op jit(solution)/shard_map/ppermute | solution.py:169
  74.8 6.8 %collective-permute-start.2 = (bf16[4,64,256]{2,1,0:T(8,128)(2,1)}, bf16[4,64,256]{2,1,0:T(8,128)(2,1)S(1)}, u32[]{:S(2)}, u32[]{:S(2)}) collective-permute-start(bf16[4,64,256]{2,1,0:T(8,128)(2,1)} %get-tuple-element.11), channel_id=1, source_target_pairs={{0,2},{2,4},{4,6},{6,0},{1,3},{3,5},{5,7},{7,1},{8,10},{10,12},{12... | collective-permute-start | bytes 393224 | tf_op jit(solution)/shard_map/ppermute | solution.py:169
  75.8 6.0 %collective-permute-start.3 = (bf16[4,64,256]{2,1,0:T(8,128)(2,1)S(1)}, bf16[4,64,256]{2,1,0:T(8,128)(2,1)S(1)}, u32[]{:S(2)}, u32[]{:S(2)}) collective-permute-start(bf16[4,64,256]{2,1,0:T(8,128)(2,1)S(1)} %get-tuple-element.12), channel_id=1, source_target_pairs={{0,6},{2,0},{4,2},{6,4},{1,7},{3,1},{5,3},{7,5},{8,14},{10,8},{12,... | collective-permute-start | bytes 393224 | tf_op jit(solution)/shard_map/ppermute | solution.py:169
  82.0 1.3 %collective-permute-start.4 = (bf16[32,4,256]{2,1,0:T(4,128)(2,1)S(1)}, bf16[32,4,256]{2,1,0:T(4,128)(2,1)S(1)}, u32[]{:S(2)}, u32[]{:S(2)}) collective-permute-start(bf16[32,4,256]{2,1,0:T(4,128)(2,1)S(1)} %bitcast.31), channel_id=1, source_target_pairs={{0,1},{1,0},{2,3},{3,2},{4,5},{5,4},{6,7},{7,6},{8,9},{9,8},{10,11... | collective-permute-start | bytes 196616 | tf_op jit(solution)/shard_map/ppermute | solution.py:177

commit v8 on v2

--- a/solution.py
+++ b/solution.py
@@ -70,9 +70,12 @@
     )(meta, site, wave, own, other)
 
 
+def near_shifts(z_count):
+    return [shift for shift in range(z_count) if shift != z_count // 2]
+
+
 def left_kernel(z_count, p_size, meta, left_hbm, held_hbm, *refs):
-    outs = refs[:z_count]
-    left, held, total, left_sem, held_sem = refs[z_count:]
+    *outs, left, held, total, left_sem, held_sem = refs
     z_at = meta[1]
     terms, width = left.shape[0], left.shape[1]
     copies = []
@@ -100,17 +103,35 @@
             total[...] += add
 
     rows = width // z_count
-    for shift in range(z_count):
-        start = pl.multiple_of(lax.rem(z_at + shift, z_count) * rows, rows)
-        block = total[pl.ds(start, rows), :]
+    half = rows // CORES
+    core = meta[0]
+
+    def cut(out, shift, low, count):
+        start = lax.rem(z_at + shift, z_count) * rows + low
+        block = total[pl.ds(pl.multiple_of(start, half), count), :]
         for q in range(p_size):
-            outs[shift][q] = block[:, q * width : (q + 1) * width].astype(outs[shift].dtype)
+            out[q] = block[:, q * width : (q + 1) * width].astype(out.dtype)
+
+    far_ref, keep_ref, give_ref, *near_refs = outs
+    cut(far_ref, z_count // 2, 0, rows)
+    cut(keep_ref, 0, core * half, half)
+    for at, shift in enumerate(near_shifts(z_count)):
+        cut(give_ref.at[at], shift, (1 - core) * half, half)
+        if shift:
+            cut(near_refs[at - 1], shift, core * half, half)
 
 
 def left_call(meta, left, held, z_count):
     terms, width, columns = held.shape
     p_size = columns // width
     rows = width // z_count
+    half = (p_size, rows // CORES, width)
+    near = len(near_shifts(z_count))
+    out_shape = [
+        jax.ShapeDtypeStruct((p_size, rows, width), jnp.bfloat16),
+        jax.ShapeDtypeStruct(half, jnp.float32),
+        jax.ShapeDtypeStruct((near, *half), jnp.bfloat16),
+    ] + [jax.ShapeDtypeStruct(half, jnp.bfloat16)] * (near - 1)
     return pl.pallas_call(
         functools.partial(left_kernel, z_count, p_size),
         in_specs=[
@@ -118,11 +139,8 @@
             pl.BlockSpec(memory_space=pl.ANY),
             pl.BlockSpec(memory_space=pl.ANY),
         ],
-        out_specs=[pl.BlockSpec(memory_space=pltpu.VMEM)] * z_count,
-        out_shape=[
-            jax.ShapeDtypeStruct((p_size, rows, width), jnp.float32 if s == 0 else jnp.bfloat16)
-            for s in range(z_count)
-        ],
+        out_specs=[pl.BlockSpec(memory_space=pltpu.VMEM)] * len(out_shape),
+        out_shape=out_shape,
         scratch_shapes=[
             pltpu.VMEM((terms, width, width), jnp.bfloat16),
             pltpu.VMEM((terms, width, columns), jnp.bfloat16),
@@ -153,22 +171,38 @@
     meta = jnp.stack([core, z_at, jnp.int32(z_count * CORES)]).astype(jnp.int32)
     site = site_ops.reshape(site_ops.shape[0], -1)
     held = right_call(meta, site, masked, right_ops, other)
-    parts = left_call(meta, left, held, z_count)
-
-    total = parts[0]
-    for shift in sorted(range(1, z_count), key=lambda s: -min(s, z_count - s)):
-        ring = [(z, (z + shift) % z_count) for z in range(z_count)]
-        total = total + lax.ppermute(parts[shift], "z", ring).astype(jnp.float32)
-
-    rows = width // z_count
-    row_mask = lax.dynamic_slice_in_dim(mask, z_at * rows, rows)
-    share = (total * row_mask[None, :, None] * mask[None, None, :]).astype(jnp.bfloat16)
-    share = share.transpose(1, 0, 2).reshape(CORES, rows // CORES, p_size, width)
-    keep = lax.dynamic_index_in_dim(share, core, 0, keepdims=False)
-    give = lax.dynamic_index_in_dim(share, 1 - core, 0, keepdims=False)
+    far, keep, give, *near = left_call(meta, left, held, z_count)
+
+    def ring(block, shift):
+        pairs = [(z, (z + shift) % z_count) for z in range(z_count)]
+        return lax.ppermute(block, "z", pairs)
+
+    far = ring(far, z_count // 2)
     take = lax.ppermute(give, "core", swap)
+    mine, theirs = keep, take[0].astype(jnp.float32)
+    for at, shift in enumerate(near_shifts(z_count)):
+        if shift:
+            both = ring(jnp.stack([near[at - 1], take[at]]), shift).astype(jnp.float32)
+            mine, theirs = mine + both[0], theirs + both[1]
+    half = keep.shape[1]
+    far_mine = lax.dynamic_slice_in_dim(far, core * half, half, 1)
+    far_give = lax.dynamic_slice_in_dim(far, (1 - core) * half, half, 1)
+    mine = mine + far_mine.astype(jnp.float32)
+    theirs = theirs + lax.ppermute(far_give, "core", swap).astype(jnp.float32)
+
+    sizes = lax.dynamic_slice_in_dim(sector_dims, op_at * CORES, CORES)
+    columns = lax.iota(jnp.int32, width)
+    in_rows = (z_at * CORES + core) * half + lax.iota(jnp.int32, half)
     first = core == 0
-    return jnp.stack([jnp.where(first, keep, take), jnp.where(first, take, keep)])
+    shares = []
+    for sector, part in enumerate(
+        (jnp.where(first, mine, theirs), jnp.where(first, theirs, mine))
+    ):
+        row_mask = (in_rows < sizes[sector]).astype(jnp.float32)
+        column_mask = (columns < sizes[sector]).astype(jnp.float32)
+        share = part * row_mask[None, :, None] * column_mask[None, None, :]
+        shares.append(share.astype(jnp.bfloat16).transpose(1, 0, 2))
+    return jnp.stack(shares)
 
 
 def solution(mesh):

time: 84.4 us -> 84.9 us (level)
  waiting for transfers between devices: 38.7 us -> 36.1 us
  other arithmetic: 1.75 us -> 3.6 us
  local copies, waits for them, and re-layouts: 3.23 us -> 4.53 us
    convert_element_type x1 -> x6, other arithmetic: 0.09 us -> 2.48 us  [the longest x2 1.22 us: shards(): row_mask = (in_rows < sizes[sector]).astype(jnp.float32)]
    all_to_all x1, waiting for transfers between devices: 33.9 us -> 32.6 us  [shards(): lax.all_to_all(left_ops[:, 0], ('op', 'core'), split_axis=0, concat_axis=...]
    ppermute x1, waiting for transfers between devices: 1.24 us -> 0.01 us  [shards(): take = lax.ppermute(give, 'core', swap)]
    ppermute x3 -> x4, starting transfers between devices: 7.19 us -> 7.33 us  [the longest x3 7.33 us: ring(): return lax.ppermute(block, 'z', pairs)]
    ppermute x3 -> x4, waiting for transfers between devices: 3.53 us -> 3.57 us  [the longest x3 3.57 us: ring(): return lax.ppermute(block, 'z', pairs)]
  transfers between devices with their start and end apart: 6 -> 7, of which waited for: 5 -> 4; matrix products, arithmetic and copies ran while one was open for 2% -> 6% of each run, Pallas kernels for 20% -> 20%
where the time goes in v8:
time: 84.9 us; the launch traced here: 84.7 us
  waiting for transfers between devices  36.1 us (43%)
  Pallas kernels  25 us (29%)
  starting transfers between devices  15.2 us (18%)
  local copies, waits for them, and re-layouts  4.53 us (5%)
  other arithmetic  3.6 us (4%)
    all_to_all x1, waiting for transfers between devices, shards(): lax.all_to_all(left_ops[:, 0], ('op', 'core'), split_axis=0, concat_axis=...  32.6 us
    pallas_call x1, Pallas kernels, right_call(): pl.pallas_call(functools.partial(right_kernel, GROUP), grid_spec=pltpu.Pr...  16.7 us
    pallas_call x1, Pallas kernels, left_call(): pl.pallas_call(functools.partial(left_kernel, z_count, p_size), in_specs=...  8.32 us
    all_to_all x1, starting transfers between devices, shards(): lax.all_to_all(left_ops[:, 0], ('op', 'core'), split_axis=0, concat_axis=...  7.81 us
    ppermute x3, starting transfers between devices, ring(): return lax.ppermute(block, 'z', pairs)  7.33 us
    ppermute x3, waiting for transfers between devices, ring(): return lax.ppermute(block, 'z', pairs)  3.57 us
    unnamed x8, local copies, waits for them, and re-layouts  2.2 us
  transfers between devices with their start and end apart: 7, of which 4 were waited for; matrix products, arithmetic and copies ran while one was open for 6% of the time, Pallas kernels for 20%

profile of v8, /device:TPU:8, one launch (start us, length us, event | category | flops | bytes accessed | tf_op | source)
XLA Modules:
  0.0 84.7 jit_solution(9251462640729143932)
XLA Ops:
  0.0 0.0 copy-start
  0.0 0.0 collective-permute-start
  0.0 0.0 copy-start.2
  0.0 0.0 copy-start.3
  0.0 7.8 %all-to-all-start = ((bf16[32,256,256]{2,1,0:T(8,128)(2,1)}), bf16[32,256,256]{2,1,0:T(8,128)(2,1)}, u32[]{:S(2)}, u32[]{:S(2)}) async-start(bf16[32,256,256]{2,1,0:T(8,128)(2,1)} %bitcast.48), calls=%async_computation | async-start | bytes 8388608 | tf_op jit(solution)/shard_map/all_to_all | solution.py:163
  7.9 0.0 copy-done.2
  7.9 0.1 copy.10.site_ref
  8.0 0.0 copy-done.3
  8.0 0.6 dynamic_slice.17
  8.6 0.1 dynamic_slice.20
  8.7 0.1 pad_add_fusion.meta
  8.7 0.6 compare_convert_fusion.4
  9.4 0.6 fusion.12
  10.0 0.6 compare_convert_fusion.2
  10.6 0.0 copy-done
  10.6 0.2 constant_dynamic-slice_fusion.1
  10.8 0.2 fusion.2.wave_ref
  11.0 0.0 collective-permute-done.other_ref
  11.0 0.0 copy-start.1
  11.0 2.2 %copy-done.1 = bf16[2,16,1,256,256]{4,3,2,1,0:T(8,128)(2,1)S(1)} copy-done((bf16[2,16,1,256,256]{4,3,2,1,0:T(8,128)(2,1)S(1)}, bf16[2,16,1,256,256]{4,3,2,1,0:T(8,128)(2,1)}, u32[]{:S(2)}) %copy-start.1) | copy-done | bytes 4194328
  13.2 16.7 %right_terms.1.held_hbm = bf16[32,256,1024]{2,1,0:T(8,128)(2,1)} custom-call(s32[3]{0:T(128)S(1)} %pad_add_fusion.meta, f32[128,16]{1,0:T(8,128)S(1)} %copy.10.site_ref, bf16[4,256,256]{2,1,0:T(8,128)(2,1)S(1)} %fusion.2.wave_ref, bf16[2,16,1,256,256]{4,3,2,1,0:T(8,128)(2,1)S(1)} %copy-done.1, bf16[2,16,1,256,256]{4,3,2,1,0:T(8,128)(2,1)} %collective-permute-done.other_ref), custom_call_target="tpu_custom_call" | custom-call | tf_op jit(solution)/shard_map/right_terms/pallas_call | solution.py:51
  29.8 32.6 %all-to-all-done.left_hbm = bf16[32,256,256]{2,1,0:T(8,128)(2,1)} async-done(((bf16[32,256,256]{2,1,0:T(8,128)(2,1)}), bf16[32,256,256]{2,1,0:T(8,128)(2,1)}, u32[]{:S(2)}, u32[]{:S(2)}) %all-to-all-start) | async-done | bytes 4194336 | tf_op jit(solution)/shard_map/all_to_all | solution.py:163
  62.4 8.3 %left_terms.1 = (bf16[4,64,256]{2,1,0:T(8,128)(2,1)S(1)}, f32[4,32,256]{2,1,0:T(8,128)S(1)}, bf16[3,4,32,256]{3,2,1,0:T(8,128)(2,1)S(1)}, bf16[4,32,256]{2,1,0:T(8,128)(2,1)S(1)}, bf16[4,32,256]{2,1,0:T(8,128)(2,1)S(1)}) custom-call(s32[3]{0:T(128)S(1)} %pad_add_fusion.meta, bf16[32,256,256]{2,1,0:T(8,128)(2,1)} %all-to-all-done.left_hbm, ...), custom_call_target="tpu_custom_call" | custom-call | tf_op jit(solution)/shard_map/left_terms/pallas_call | solution.py:135
  70.7 0.1 collective-permute-start.1
  70.8 0.6 compare_convert_fusion.3
  71.4 0.7 compare_convert_fusion
  72.0 4.0 %collective-permute-start.4 = (bf16[4,64,256]{2,1,0:T(8,128)(2,1)S(1)}, bf16[4,64,256]{2,1,0:T(8,128)(2,1)S(1)}, u32[]{:S(2)}, u32[]{:S(2)}) collective-permute-start(bf16[4,64,256]{2,1,0:T(8,128)(2,1)S(1)} %get-tuple-element.14), channel_id=1, source_target_pairs={{0,4},{2,6},{4,0},{6,2},{1,5},{3,7},{5,1},{7,3},{8,12},{10,14},{12... | collective-permute-start | bytes 393224 | tf_op jit(solution)/shard_map/ppermute | solution.py:178
  76.0 0.0 collective-permute-done.1
  76.0 1.1 %collective-permute-start.2 = (bf16[2,4,32,256]{3,2,1,0:T(8,128)(2,1)S(1)}, bf16[2,4,32,256]{3,2,1,0:T(8,128)(2,1)S(1)}, u32[]{:S(2)}, u32[]{:S(2)}) collective-permute-start(bf16[2,4,32,256]{3,2,1,0:T(8,128)(2,1)S(1)} %pad_maximum_fusion), channel_id=1, source_target_pairs={{0,2},{2,4},{4,6},{6,0},{1,3},{3,5},{5,7},{7,1},{8,10},{10,12},{12... | collective-permute-start | bytes 393224 | tf_op jit(solution)/shard_map/ppermute | solution.py:178
  77.1 2.3 %collective-permute-start.3 = (bf16[2,4,32,256]{3,2,1,0:T(8,128)(2,1)S(1)}, bf16[2,4,32,256]{3,2,1,0:T(8,128)(2,1)S(1)}, u32[]{:S(2)}, u32[]{:S(2)}) collective-permute-start(bf16[2,4,32,256]{3,2,1,0:T(8,128)(2,1)S(1)} %pad_maximum_fusion.1), channel_id=1, source_target_pairs={{0,6},{2,0},{4,2},{6,4},{1,7},{3,1},{5,3},{7,5},{8,14},{10,8},{12,... | collective-permute-start | bytes 393224 | tf_op jit(solution)/shard_map/ppermute | solution.py:178
  79.4 0.9 %collective-permute-done.4 = bf16[4,64,256]{2,1,0:T(8,128)(2,1)S(1)} collective-permute-done((bf16[4,64,256]{2,1,0:T(8,128)(2,1)S(1)}, bf16[4,64,256]{2,1,0:T(8,128)(2,1)S(1)}, u32[]{:S(2)}, u32[]{:S(2)}) %collective-permute-start.4) | collective-permute-done | bytes 131104 | tf_op jit(solution)/shard_map/ppermute | solution.py:178
  80.4 0.0 collective-permute-start.5
  80.4 0.7 compare_convert_fusion.1
  81.0 2.0 %collective-permute-done.2 = bf16[2,4,32,256]{3,2,1,0:T(8,128)(2,1)S(1)} collective-permute-done((bf16[2,4,32,256]{3,2,1,0:T(8,128)(2,1)S(1)}, bf16[2,4,32,256]{3,2,1,0:T(8,128)(2,1)S(1)}, u32[]{:S(2)}, u32[]{:S(2)}) %collective-permute-start.2) | collective-permute-done | bytes 131104 | tf_op jit(solution)/shard_map/ppermute | solution.py:178
  83.1 0.6 collective-permute-done.3
  83.7 0.0 collective-permute-done.5
  83.7 0.1 fusion.8
  83.8 0.1 fusion.9
  83.9 0.8 copy.11
  (7 shorter events, 0.1 us)
Async XLA Ops:
  0.0 10.6 %copy-start = (bf16[2,256,4,256]{3,2,1,0:T(4,128)(2,1)S(1)}, bf16[2,256,4,256]{3,2,1,0:T(4,128)(2,1)}, u32[]{:S(2)}) copy-start(bf16[2,256,4,256]{3,2,1,0:T(4,128)(2,1)} %param.5) | copy-start | bytes 3145732
  0.0 11.0 %collective-permute-start = (bf16[2,16,1,256,256]{4,3,2,1,0:T(8,128)(2,1)}, bf16[2,16,1,256,256]{4,3,2,1,0:T(8,128)(2,1)}, u32[]{:S(2)}, u32[]{:S(2)}) collective-permute-start(bf16[2,16,1,256,256]{4,3,2,1,0:T(8,128)(2,1)} %own_ref.1), channel_id=1, source_target_pairs={{0,1},{1,0},{2,3},{3,2},{4,5},{5,4},{6,7},{7,6},{8,9},{9,8},{10,11... | collective-permute-start | bytes 12582920 | tf_op jit(solution)/shard_map/ppermute | solution.py:162
  0.0 7.9 %copy-start.2 = (f32[128,4,4]{0,2,1:T(4,128)S(1)}, f32[128,4,4]{0,2,1:T(4,128)}, u32[]{:S(2)}) copy-start(f32[128,4,4]{0,2,1:T(4,128)} %param.9) | copy-start | bytes 24580
  0.0 8.0 %copy-start.3 = (s32[32]{0:T(128)S(1)}, s32[32]{0:T(128)}, u32[]{:S(2)}) copy-start(s32[32]{0:T(128)} %param.6) | copy-start | bytes 388
  0.0 62.4 %all-to-all-start = ((bf16[32,256,256]{2,1,0:T(8,128)(2,1)}), bf16[32,256,256]{2,1,0:T(8,128)(2,1)}, u32[]{:S(2)}, u32[]{:S(2)}) async-start(bf16[32,256,256]{2,1,0:T(8,128)(2,1)} %bitcast.48), calls=%async_computation | async-start | bytes 8388608 | tf_op jit(solution)/shard_map/all_to_all | solution.py:163
  11.0 2.2 %copy-start.1 = (bf16[2,16,1,256,256]{4,3,2,1,0:T(8,128)(2,1)S(1)}, bf16[2,16,1,256,256]{4,3,2,1,0:T(8,128)(2,1)}, u32[]{:S(2)}) copy-start(bf16[2,16,1,256,256]{4,3,2,1,0:T(8,128)(2,1)} %own_ref.1) | copy-start | bytes 12582916
  70.7 5.3 %collective-permute-start.1 = (bf16[3,4,32,256]{3,2,1,0:T(8,128)(2,1)S(1)}, bf16[3,4,32,256]{3,2,1,0:T(8,128)(2,1)S(1)}, u32[]{:S(2)}, u32[]{:S(2)}) collective-permute-start(bf16[3,4,32,256]{3,2,1,0:T(8,128)(2,1)S(1)} %get-tuple-element.12), channel_id=1, source_target_pairs={{0,1},{1,0},{2,3},{3,2},{4,5},{5,4},{6,7},{7,6},{8,9},{9,8},{10,11... | collective-permute-start | bytes 589832 | tf_op jit(solution)/shard_map/ppermute | solution.py:181
  72.0 8.3 %collective-permute-start.4 = (bf16[4,64,256]{2,1,0:T(8,128)(2,1)S(1)}, bf16[4,64,256]{2,1,0:T(8,128)(2,1)S(1)}, u32[]{:S(2)}, u32[]{:S(2)}) collective-permute-start(bf16[4,64,256]{2,1,0:T(8,128)(2,1)S(1)} %get-tuple-element.14), channel_id=1, source_target_pairs={{0,4},{2,6},{4,0},{6,2},{1,5},{3,7},{5,1},{7,3},{8,12},{10,14},{12... | collective-permute-start | bytes 393224 | tf_op jit(solution)/shard_map/ppermute | solution.py:178
  76.0 7.0 %collective-permute-start.2 = (bf16[2,4,32,256]{3,2,1,0:T(8,128)(2,1)S(1)}, bf16[2,4,32,256]{3,2,1,0:T(8,128)(2,1)S(1)}, u32[]{:S(2)}, u32[]{:S(2)}) collective-permute-start(bf16[2,4,32,256]{3,2,1,0:T(8,128)(2,1)S(1)} %pad_maximum_fusion), channel_id=1, source_target_pairs={{0,2},{2,4},{4,6},{6,0},{1,3},{3,5},{5,7},{7,1},{8,10},{10,12},{12... | collective-permute-start | bytes 393224 | tf_op jit(solution)/shard_map/ppermute | solution.py:178
  77.1 6.6 %collective-permute-start.3 = (bf16[2,4,32,256]{3,2,1,0:T(8,128)(2,1)S(1)}, bf16[2,4,32,256]{3,2,1,0:T(8,128)(2,1)S(1)}, u32[]{:S(2)}, u32[]{:S(2)}) collective-permute-start(bf16[2,4,32,256]{3,2,1,0:T(8,128)(2,1)S(1)} %pad_maximum_fusion.1), channel_id=1, source_target_pairs={{0,6},{2,0},{4,2},{6,4},{1,7},{3,1},{5,3},{7,5},{8,14},{10,8},{12,... | collective-permute-start | bytes 393224 | tf_op jit(solution)/shard_map/ppermute | solution.py:178
  80.4 3.4 %collective-permute-start.5 = (bf16[4,32,256]{2,1,0:T(8,128)(2,1)S(1)}, bf16[4,32,256]{2,1,0:T(8,128)(2,1)S(1)}, u32[]{:S(2)}, u32[]{:S(2)}) collective-permute-start(bf16[4,32,256]{2,1,0:T(8,128)(2,1)S(1)} %constant_dynamic-slice_fusion), channel_id=1, source_target_pairs={{0,1},{1,0},{2,3},{3,2},{4,5},{5,4},{6,7},{7,6},{8,9},{9,8},{10,11... | collective-permute-start | bytes 196616 | tf_op jit(solution)/shard_map/ppermute | solution.py:191

commit v9 on v8

--- a/solution.py
+++ b/solution.py
@@ -162,8 +162,11 @@
     other = lax.ppermute(right_ops, "core", swap)
     left = lax.all_to_all(left_ops[:, 0], ("op", "core"), split_axis=0, concat_axis=0, tiled=True)
 
-    size = lax.dynamic_slice_in_dim(sector_dims, op_at * CORES + core, 1)
-    mask = (lax.iota(jnp.int32, width) < size).astype(jnp.float32)
+    sizes = lax.dynamic_slice_in_dim(sector_dims, op_at * CORES, CORES)
+    masks = (lax.broadcasted_iota(jnp.int32, (CORES, width), 1) < sizes[:, None]).astype(
+        jnp.float32
+    )
+    mask = lax.dynamic_index_in_dim(masks, core, 0, keepdims=False)
     block = lax.dynamic_index_in_dim(wave, core, 0, keepdims=False)
     masked = block.astype(jnp.float32) * mask[:, None, None] * mask[None, None, :]
     masked = masked.astype(jnp.bfloat16).transpose(1, 0, 2)
@@ -190,19 +193,11 @@
     mine = mine + far_mine.astype(jnp.float32)
     theirs = theirs + lax.ppermute(far_give, "core", swap).astype(jnp.float32)
 
-    sizes = lax.dynamic_slice_in_dim(sector_dims, op_at * CORES, CORES)
-    columns = lax.iota(jnp.int32, width)
-    in_rows = (z_at * CORES + core) * half + lax.iota(jnp.int32, half)
+    row_masks = lax.dynamic_slice_in_dim(masks, (z_at * CORES + core) * half, half, 1)
     first = core == 0
-    shares = []
-    for sector, part in enumerate(
-        (jnp.where(first, mine, theirs), jnp.where(first, theirs, mine))
-    ):
-        row_mask = (in_rows < sizes[sector]).astype(jnp.float32)
-        column_mask = (columns < sizes[sector]).astype(jnp.float32)
-        share = part * row_mask[None, :, None] * column_mask[None, None, :]
-        shares.append(share.astype(jnp.bfloat16).transpose(1, 0, 2))
-    return jnp.stack(shares)
+    parts = jnp.stack([jnp.where(first, mine, theirs), jnp.where(first, theirs, mine)])
+    share = parts * row_masks[:, None, :, None] * masks[:, None, None, :]
+    return share.astype(jnp.bfloat16).transpose(0, 2, 1, 3)
 
 
 def solution(mesh):

time: 84.9 us -> 83.6 us (0.985)
  other arithmetic: 3.6 us -> 0.62 us
  waiting for transfers between devices: 36.1 us -> 39 us
  local copies, waits for them, and re-layouts: 4.53 us -> 3.43 us
    convert_element_type x5 -> x1, other arithmetic: 3.08 us -> 0.07 us  [shards(): (lax.broadcasted_iota(jnp.int32, (CORES, width), 1) < sizes[:, None]).ast...]
    all_to_all x1, waiting for transfers between devices: 32.6 us -> 34.9 us  [shards(): lax.all_to_all(left_ops[:, 0], ('op', 'core'), split_axis=0, concat_axis=...]
  transfers between devices with their start and end apart: 7 -> 7, of which waited for: 4 -> 4; matrix products, arithmetic and copies ran while one was open for 6% -> 1% of each run, Pallas kernels for 20% -> 20%
where the time goes in v9:
time: 83.6 us; the launch traced here: 83.4 us
  waiting for transfers between devices  39 us (47%)
  Pallas kernels  25 us (30%)
  starting transfers between devices  15.2 us (18%)
  local copies, waits for them, and re-layouts  3.43 us (4%)
    all_to_all x1, waiting for transfers between devices, shards(): lax.all_to_all(left_ops[:, 0], ('op', 'core'), split_axis=0, concat_axis=...  34.9 us
    pallas_call x1, Pallas kernels, right_call(): pl.pallas_call(functools.partial(right_kernel, GROUP), grid_spec=pltpu.Pr...  16.7 us
    pallas_call x1, Pallas kernels, left_call(): pl.pallas_call(functools.partial(left_kernel, z_count, p_size), in_specs=...  8.32 us
    all_to_all x1, starting transfers between devices, shards(): lax.all_to_all(left_ops[:, 0], ('op', 'core'), split_axis=0, concat_axis=...  7.81 us
    ppermute x3, starting transfers between devices, ring(): return lax.ppermute(block, 'z', pairs)  7.33 us
    ppermute x3, waiting for transfers between devices, ring(): return lax.ppermute(block, 'z', pairs)  4.08 us
    unnamed x8, local copies, waits for them, and re-layouts  2.2 us
  transfers between devices with their start and end apart: 7, of which 4 were waited for; matrix products, arithmetic and copies ran while one was open for 1% of the time, Pallas kernels for 20%

profile of v9, /device:TPU:8, one launch (start us, length us, event | category | flops | bytes accessed | tf_op | source)
XLA Modules:
  0.0 83.4 jit_solution(5882526154454360461)
XLA Ops:
  0.0 0.0 copy-start
  0.0 0.0 collective-permute-start
  0.0 0.0 copy-start.2
  0.0 0.0 copy-start.3
  0.0 7.8 %all-to-all-start = ((bf16[32,256,256]{2,1,0:T(8,128)(2,1)}), bf16[32,256,256]{2,1,0:T(8,128)(2,1)}, u32[]{:S(2)}, u32[]{:S(2)}) async-start(bf16[32,256,256]{2,1,0:T(8,128)(2,1)} %bitcast.44), calls=%async_computation | async-start | bytes 8388608 | tf_op jit(solution)/shard_map/all_to_all | solution.py:163
  7.9 0.0 copy-done.2
  7.9 0.1 copy.10.site_ref
  8.0 0.0 copy-done.3
  8.0 0.1 dynamic_slice.21
  8.1 0.1 pad_add_fusion.meta
  8.1 0.1 compare_convert_fusion
  8.2 0.0 copy-done
  8.2 0.2 constant_dynamic-slice_fusion.3
  8.4 0.2 fusion.2.wave_ref
  8.6 0.0 collective-permute-done.other_ref
  8.6 0.0 copy-start.1
  8.6 2.2 %copy-done.1 = bf16[2,16,1,256,256]{4,3,2,1,0:T(8,128)(2,1)S(1)} copy-done((bf16[2,16,1,256,256]{4,3,2,1,0:T(8,128)(2,1)S(1)}, bf16[2,16,1,256,256]{4,3,2,1,0:T(8,128)(2,1)}, u32[]{:S(2)}) %copy-start.1) | copy-done | bytes 4194328
  10.8 16.7 %right_terms.1.held_hbm = bf16[32,256,1024]{2,1,0:T(8,128)(2,1)} custom-call(s32[3]{0:T(128)S(1)} %pad_add_fusion.meta, f32[128,16]{1,0:T(8,128)S(1)} %copy.10.site_ref, bf16[4,256,256]{2,1,0:T(8,128)(2,1)S(1)} %fusion.2.wave_ref, bf16[2,16,1,256,256]{4,3,2,1,0:T(8,128)(2,1)S(1)} %copy-done.1, bf16[2,16,1,256,256]{4,3,2,1,0:T(8,128)(2,1)} %collective-permute-done.other_ref), custom_call_target="tpu_custom_call" | custom-call | tf_op jit(solution)/shard_map/right_terms/pallas_call | solution.py:51
  27.5 34.9 %all-to-all-done.left_hbm = bf16[32,256,256]{2,1,0:T(8,128)(2,1)} async-done(((bf16[32,256,256]{2,1,0:T(8,128)(2,1)}), bf16[32,256,256]{2,1,0:T(8,128)(2,1)}, u32[]{:S(2)}, u32[]{:S(2)}) %all-to-all-start) | async-done | bytes 4194336 | tf_op jit(solution)/shard_map/all_to_all | solution.py:163
  62.4 8.3 %left_terms.1 = (bf16[4,64,256]{2,1,0:T(8,128)(2,1)S(1)}, f32[4,32,256]{2,1,0:T(8,128)S(1)}, bf16[3,4,32,256]{3,2,1,0:T(8,128)(2,1)S(1)}, bf16[4,32,256]{2,1,0:T(8,128)(2,1)S(1)}, bf16[4,32,256]{2,1,0:T(8,128)(2,1)S(1)}) custom-call(s32[3]{0:T(128)S(1)} %pad_add_fusion.meta, bf16[32,256,256]{2,1,0:T(8,128)(2,1)} %all-to-all-done.left_hbm, ...), custom_call_target="tpu_custom_call" | custom-call | tf_op jit(solution)/shard_map/left_terms/pallas_call | solution.py:135
  70.7 0.1 collective-permute-start.1
  70.8 4.0 %collective-permute-start.4 = (bf16[4,64,256]{2,1,0:T(8,128)(2,1)S(1)}, bf16[4,64,256]{2,1,0:T(8,128)(2,1)S(1)}, u32[]{:S(2)}, u32[]{:S(2)}) collective-permute-start(bf16[4,64,256]{2,1,0:T(8,128)(2,1)S(1)} %get-tuple-element.14), channel_id=1, source_target_pairs={{0,4},{2,6},{4,0},{6,2},{1,5},{3,7},{5,1},{7,3},{8,12},{10,14},{12... | collective-permute-start | bytes 393224 | tf_op jit(solution)/shard_map/ppermute | solution.py:181
  74.8 0.0 collective-permute-done.1
  74.8 1.1 %collective-permute-start.2 = (bf16[2,4,32,256]{3,2,1,0:T(8,128)(2,1)S(1)}, bf16[2,4,32,256]{3,2,1,0:T(8,128)(2,1)S(1)}, u32[]{:S(2)}, u32[]{:S(2)}) collective-permute-start(bf16[2,4,32,256]{3,2,1,0:T(8,128)(2,1)S(1)} %pad_maximum_fusion), channel_id=1, source_target_pairs={{0,2},{2,4},{4,6},{6,0},{1,3},{3,5},{5,7},{7,1},{8,10},{10,12},{12... | collective-permute-start | bytes 393224 | tf_op jit(solution)/shard_map/ppermute | solution.py:181
  75.9 2.3 %collective-permute-start.3 = (bf16[2,4,32,256]{3,2,1,0:T(8,128)(2,1)S(1)}, bf16[2,4,32,256]{3,2,1,0:T(8,128)(2,1)S(1)}, u32[]{:S(2)}, u32[]{:S(2)}) collective-permute-start(bf16[2,4,32,256]{3,2,1,0:T(8,128)(2,1)S(1)} %pad_maximum_fusion.1), channel_id=1, source_target_pairs={{0,6},{2,0},{4,2},{6,4},{1,7},{3,1},{5,3},{7,5},{8,14},{10,8},{12,... | collective-permute-start | bytes 393224 | tf_op jit(solution)/shard_map/ppermute | solution.py:181
  78.2 0.9 %collective-permute-done.4 = bf16[4,64,256]{2,1,0:T(8,128)(2,1)S(1)} collective-permute-done((bf16[4,64,256]{2,1,0:T(8,128)(2,1)S(1)}, bf16[4,64,256]{2,1,0:T(8,128)(2,1)S(1)}, u32[]{:S(2)}, u32[]{:S(2)}) %collective-permute-start.4) | collective-permute-done | bytes 131104 | tf_op jit(solution)/shard_map/ppermute | solution.py:181
  79.1 0.0 collective-permute-start.5
  79.1 0.1 constant_dynamic-slice_fusion
  79.2 2.6 %collective-permute-done.2 = bf16[2,4,32,256]{3,2,1,0:T(8,128)(2,1)S(1)} collective-permute-done((bf16[2,4,32,256]{3,2,1,0:T(8,128)(2,1)S(1)}, bf16[2,4,32,256]{3,2,1,0:T(8,128)(2,1)S(1)}, u32[]{:S(2)}, u32[]{:S(2)}) %collective-permute-start.2) | collective-permute-done | bytes 131104 | tf_op jit(solution)/shard_map/ppermute | solution.py:181
  81.8 0.6 collective-permute-done.3
  82.4 0.0 collective-permute-done.5
  82.4 0.1 select_bitcast_fusion.1
  82.6 0.1 fusion.5
  82.7 0.8 copy.11
  (8 shorter events, 0.1 us)
Async XLA Ops:
  0.0 8.2 %copy-start = (bf16[2,256,4,256]{3,2,1,0:T(4,128)(2,1)S(1)}, bf16[2,256,4,256]{3,2,1,0:T(4,128)(2,1)}, u32[]{:S(2)}) copy-start(bf16[2,256,4,256]{3,2,1,0:T(4,128)(2,1)} %param.5) | copy-start | bytes 3145732
  0.0 8.6 %collective-permute-start = (bf16[2,16,1,256,256]{4,3,2,1,0:T(8,128)(2,1)}, bf16[2,16,1,256,256]{4,3,2,1,0:T(8,128)(2,1)}, u32[]{:S(2)}, u32[]{:S(2)}) collective-permute-start(bf16[2,16,1,256,256]{4,3,2,1,0:T(8,128)(2,1)} %own_ref.1), channel_id=1, source_target_pairs={{0,1},{1,0},{2,3},{3,2},{4,5},{5,4},{6,7},{7,6},{8,9},{9,8},{10,11... | collective-permute-start | bytes 12582920 | tf_op jit(solution)/shard_map/ppermute | solution.py:162
  0.0 7.9 %copy-start.2 = (f32[128,4,4]{0,2,1:T(4,128)S(1)}, f32[128,4,4]{0,2,1:T(4,128)}, u32[]{:S(2)}) copy-start(f32[128,4,4]{0,2,1:T(4,128)} %param.9) | copy-start | bytes 24580
  0.0 8.0 %copy-start.3 = (s32[32]{0:T(128)S(1)}, s32[32]{0:T(128)}, u32[]{:S(2)}) copy-start(s32[32]{0:T(128)} %param.6) | copy-start | bytes 388
  0.0 62.4 %all-to-all-start = ((bf16[32,256,256]{2,1,0:T(8,128)(2,1)}), bf16[32,256,256]{2,1,0:T(8,128)(2,1)}, u32[]{:S(2)}, u32[]{:S(2)}) async-start(bf16[32,256,256]{2,1,0:T(8,128)(2,1)} %bitcast.44), calls=%async_computation | async-start | bytes 8388608 | tf_op jit(solution)/shard_map/all_to_all | solution.py:163
  8.6 2.2 %copy-start.1 = (bf16[2,16,1,256,256]{4,3,2,1,0:T(8,128)(2,1)S(1)}, bf16[2,16,1,256,256]{4,3,2,1,0:T(8,128)(2,1)}, u32[]{:S(2)}) copy-start(bf16[2,16,1,256,256]{4,3,2,1,0:T(8,128)(2,1)} %own_ref.1) | copy-start | bytes 12582916
  70.7 4.1 %collective-permute-start.1 = (bf16[3,4,32,256]{3,2,1,0:T(8,128)(2,1)S(1)}, bf16[3,4,32,256]{3,2,1,0:T(8,128)(2,1)S(1)}, u32[]{:S(2)}, u32[]{:S(2)}) collective-permute-start(bf16[3,4,32,256]{3,2,1,0:T(8,128)(2,1)S(1)} %get-tuple-element.12), channel_id=1, source_target_pairs={{0,1},{1,0},{2,3},{3,2},{4,5},{5,4},{6,7},{7,6},{8,9},{9,8},{10,11... | collective-permute-start | bytes 589832 | tf_op jit(solution)/shard_map/ppermute | solution.py:184
  70.8 8.3 %collective-permute-start.4 = (bf16[4,64,256]{2,1,0:T(8,128)(2,1)S(1)}, bf16[4,64,256]{2,1,0:T(8,128)(2,1)S(1)}, u32[]{:S(2)}, u32[]{:S(2)}) collective-permute-start(bf16[4,64,256]{2,1,0:T(8,128)(2,1)S(1)} %get-tuple-element.14), channel_id=1, source_target_pairs={{0,4},{2,6},{4,0},{6,2},{1,5},{3,7},{5,1},{7,3},{8,12},{10,14},{12... | collective-permute-start | bytes 393224 | tf_op jit(solution)/shard_map/ppermute | solution.py:181
  74.8 7.0 %collective-permute-start.2 = (bf16[2,4,32,256]{3,2,1,0:T(8,128)(2,1)S(1)}, bf16[2,4,32,256]{3,2,1,0:T(8,128)(2,1)S(1)}, u32[]{:S(2)}, u32[]{:S(2)}) collective-permute-start(bf16[2,4,32,256]{3,2,1,0:T(8,128)(2,1)S(1)} %pad_maximum_fusion), channel_id=1, source_target_pairs={{0,2},{2,4},{4,6},{6,0},{1,3},{3,5},{5,7},{7,1},{8,10},{10,12},{12... | collective-permute-start | bytes 393224 | tf_op jit(solution)/shard_map/ppermute | solution.py:181
  75.9 6.5 %collective-permute-start.3 = (bf16[2,4,32,256]{3,2,1,0:T(8,128)(2,1)S(1)}, bf16[2,4,32,256]{3,2,1,0:T(8,128)(2,1)S(1)}, u32[]{:S(2)}, u32[]{:S(2)}) collective-permute-start(bf16[2,4,32,256]{3,2,1,0:T(8,128)(2,1)S(1)} %pad_maximum_fusion.1), channel_id=1, source_target_pairs={{0,6},{2,0},{4,2},{6,4},{1,7},{3,1},{5,3},{7,5},{8,14},{10,8},{12,... | collective-permute-start | bytes 393224 | tf_op jit(solution)/shard_map/ppermute | solution.py:181
  79.1 3.3 %collective-permute-start.5 = (bf16[4,32,256]{2,1,0:T(8,128)(2,1)S(1)}, bf16[4,32,256]{2,1,0:T(8,128)(2,1)S(1)}, u32[]{:S(2)}, u32[]{:S(2)}) collective-permute-start(bf16[4,32,256]{2,1,0:T(8,128)(2,1)S(1)} %constant_dynamic-slice_fusion.1), channel_id=1, source_target_pairs={{0,1},{1,0},{2,3},{3,2},{4,5},{5,4},{6,7},{7,6},{8,9},{9,8},{10,11... | collective-permute-start | bytes 196616 | tf_op jit(solution)/shard_map/ppermute | solution.py:194

commit v10 on v9

--- a/solution.py
+++ b/solution.py
@@ -11,6 +11,7 @@
 GROUP = 2
 ROWS = 16
 LEFT_TERMS = 2
+DEPTHS = (128, 192, 256)
 VMEM_LIMIT = 48 << 20
 
 
@@ -78,29 +79,39 @@
     *outs, left, held, total, left_sem, held_sem = refs
     z_at = meta[1]
     terms, width = left.shape[0], left.shape[1]
-    copies = []
-    for at in range(0, terms, LEFT_TERMS):
-        span = pl.ds(at, LEFT_TERMS)
-        slot = at // LEFT_TERMS
-        pair = (
-            pltpu.make_async_copy(left_hbm.at[span], left.at[span], left_sem.at[slot]),
-            pltpu.make_async_copy(held_hbm.at[span], held.at[span], held_sem.at[slot]),
-        )
-        for copy in pair:
-            copy.start()
-        copies.append(pair)
-
-    for slot, pair in enumerate(copies):
-        for copy in pair:
-            copy.wait()
-        add = None
-        for at in range(slot * LEFT_TERMS, (slot + 1) * LEFT_TERMS):
-            product = jnp.dot(left[at], held[at], preferred_element_type=jnp.float32)
-            add = product if add is None else add + product
-        if slot == 0:
-            total[...] = add
-        else:
-            total[...] += add
+
+    def accumulate(depth):
+        copies = []
+        for at in range(0, terms, LEFT_TERMS):
+            span = pl.ds(at, LEFT_TERMS)
+            slot = at // LEFT_TERMS
+            used = (span, pl.ds(0, depth))
+            pair = (
+                pltpu.make_async_copy(left_hbm.at[span], left.at[span], left_sem.at[slot]),
+                pltpu.make_async_copy(held_hbm.at[used], held.at[used], held_sem.at[slot]),
+            )
+            for copy in pair:
+                copy.start()
+            copies.append(pair)
+
+        for slot, pair in enumerate(copies):
+            for copy in pair:
+                copy.wait()
+            add = None
+            for at in range(slot * LEFT_TERMS, (slot + 1) * LEFT_TERMS):
+                product = jnp.dot(
+                    left[at, :, :depth], held[at, :depth], preferred_element_type=jnp.float32
+                )
+                add = product if add is None else add + product
+            if slot == 0:
+                total[...] = add
+            else:
+                total[...] += add
+
+    size, low = meta[3], 0
+    for depth in DEPTHS:
+        pl.when((size > low) & (size <= depth))(functools.partial(accumulate, depth))
+        low = depth
 
     rows = width // z_count
     half = rows // CORES
@@ -171,7 +182,8 @@
     masked = block.astype(jnp.float32) * mask[:, None, None] * mask[None, None, :]
     masked = masked.astype(jnp.bfloat16).transpose(1, 0, 2)
 
-    meta = jnp.stack([core, z_at, jnp.int32(z_count * CORES)]).astype(jnp.int32)
+    size = lax.dynamic_index_in_dim(sizes, core, 0, keepdims=False)
+    meta = jnp.stack([core, z_at, jnp.int32(z_count * CORES), size]).astype(jnp.int32)
     site = site_ops.reshape(site_ops.shape[0], -1)
     held = right_call(meta, site, masked, right_ops, other)
     far, keep, give, *near = left_call(meta, left, held, z_count)

time: 83.6 us -> 82.6 us (0.988)
  waiting for transfers between devices: 39 us -> 37.4 us
  Pallas kernels: 25 us -> 23.6 us
  starting transfers between devices: 15.2 us -> 16.1 us
    pallas_call x1, Pallas kernels: 8.32 us -> 6.98 us  [left_call(): pl.pallas_call(functools.partial(left_kernel, z_count, p_size), in_specs=...]
    all_to_all x1, waiting for transfers between devices: 34.9 us -> 33.7 us  [shards(): lax.all_to_all(left_ops[:, 0], ('op', 'core'), split_axis=0, concat_axis=...]
    ppermute x1, starting transfers between devices: 0.09 us -> 1.06 us  [shards(): take = lax.ppermute(give, 'core', swap)]
  transfers between devices with their start and end apart: 7 -> 7, of which waited for: 4 -> 4; matrix products, arithmetic and copies ran while one was open for 1% -> 3% of each run, Pallas kernels for 20% -> 20%
where the time goes in v10:
time: 82.6 us
  waiting for transfers between devices  37.4 us (45%)
  Pallas kernels  23.6 us (29%)
  starting transfers between devices  16.1 us (19%)
  local copies, waits for them, and re-layouts  4.04 us (5%)
  other arithmetic  1.25 us (2%)
    all_to_all x1, waiting for transfers between devices, shards(): lax.all_to_all(left_ops[:, 0], ('op', 'core'), split_axis=0, concat_axis=...  33.7 us
    pallas_call x1, Pallas kernels, right_call(): pl.pallas_call(functools.partial(right_kernel, GROUP), grid_spec=pltpu.Pr...  16.7 us
    all_to_all x1, starting transfers between devices, shards(): lax.all_to_all(left_ops[:, 0], ('op', 'core'), split_axis=0, concat_axis=...  7.81 us
    ppermute x3, starting transfers between devices, ring(): return lax.ppermute(block, 'z', pairs)  7.25 us
    pallas_call x1, Pallas kernels, left_call(): pl.pallas_call(functools.partial(left_kernel, z_count, p_size), in_specs=...  6.98 us
    ppermute x3, waiting for transfers between devices, ring(): return lax.ppermute(block, 'z', pairs)  3.76 us
    unnamed x8, local copies, waits for them, and re-layouts  2.2 us
  transfers between devices with their start and end apart: 7, of which 4 were waited for; matrix products, arithmetic and copies ran while one was open for 3% of the time, Pallas kernels for 20%

profile of v10, /device:TPU:8, one launch (start us, length us, event | category | flops | bytes accessed | tf_op | source)
XLA Modules:
  0.0 82.6 jit_solution(1154275362669144597)
XLA Ops:
  0.0 0.0 copy-start
  0.0 0.0 collective-permute-start
  0.0 0.0 copy-start.3
  0.0 0.0 copy-start.2
  0.0 7.8 %all-to-all-start = ((bf16[32,256,256]{2,1,0:T(8,128)(2,1)}), bf16[32,256,256]{2,1,0:T(8,128)(2,1)}, u32[]{:S(2)}, u32[]{:S(2)}) async-start(bf16[32,256,256]{2,1,0:T(8,128)(2,1)} %bitcast.44), calls=%async_computation | async-start | bytes 8388608 | tf_op jit(solution)/shard_map/all_to_all | solution.py:174
  7.9 0.0 copy-done.3
  7.9 0.1 dynamic_slice.29
  7.9 0.6 dynamic_slice.27
  8.6 0.0 copy-done.2
  8.6 0.1 copy.10.site_ref
  8.7 0.7 pad_add_fusion.meta
  9.4 0.1 compare_convert_fusion
  9.5 0.0 copy-done
  9.5 0.2 constant_dynamic-slice_fusion.3
  9.7 0.2 fusion.2.wave_ref
  9.8 0.0 collective-permute-done.other_ref
  9.9 0.0 copy-start.1
  9.9 2.2 %copy-done.1 = bf16[2,16,1,256,256]{4,3,2,1,0:T(8,128)(2,1)S(1)} copy-done((bf16[2,16,1,256,256]{4,3,2,1,0:T(8,128)(2,1)S(1)}, bf16[2,16,1,256,256]{4,3,2,1,0:T(8,128)(2,1)}, u32[]{:S(2)}) %copy-start.1) | copy-done | bytes 4194328
  12.0 16.7 %right_terms.1.held_hbm = bf16[32,256,1024]{2,1,0:T(8,128)(2,1)} custom-call(s32[4]{0:T(128)S(1)} %pad_add_fusion.meta, f32[128,16]{1,0:T(8,128)S(1)} %copy.10.site_ref, bf16[4,256,256]{2,1,0:T(8,128)(2,1)S(1)} %fusion.2.wave_ref, bf16[2,16,1,256,256]{4,3,2,1,0:T(8,128)(2,1)S(1)} %copy-done.1, bf16[2,16,1,256,256]{4,3,2,1,0:T(8,128)(2,1)} %collective-permute-done.other_ref), custom_call_target="tpu_custom_call" | custom-call | tf_op jit(solution)/shard_map/right_terms/pallas_call | solution.py:52
  28.7 33.7 %all-to-all-done.left_hbm = bf16[32,256,256]{2,1,0:T(8,128)(2,1)} async-done(((bf16[32,256,256]{2,1,0:T(8,128)(2,1)}), bf16[32,256,256]{2,1,0:T(8,128)(2,1)}, u32[]{:S(2)}, u32[]{:S(2)}) %all-to-all-start) | async-done | bytes 4194336 | tf_op jit(solution)/shard_map/all_to_all | solution.py:174
  62.4 7.0 %left_terms.1 = (bf16[4,64,256]{2,1,0:T(8,128)(2,1)S(1)}, f32[4,32,256]{2,1,0:T(8,128)S(1)}, bf16[3,4,32,256]{3,2,1,0:T(8,128)(2,1)S(1)}, bf16[4,32,256]{2,1,0:T(8,128)(2,1)S(1)}, bf16[4,32,256]{2,1,0:T(8,128)(2,1)S(1)}) custom-call(s32[4]{0:T(128)S(1)} %pad_add_fusion.meta, bf16[32,256,256]{2,1,0:T(8,128)(2,1)} %all-to-all-done.left_hbm, ...), custom_call_target="tpu_custom_call" | custom-call | tf_op jit(solution)/shard_map/left_terms/pallas_call | solution.py:146
  69.4 1.1 %collective-permute-start.1 = (bf16[3,4,32,256]{3,2,1,0:T(8,128)(2,1)S(1)}, bf16[3,4,32,256]{3,2,1,0:T(8,128)(2,1)S(1)}, u32[]{:S(2)}, u32[]{:S(2)}) collective-permute-start(bf16[3,4,32,256]{3,2,1,0:T(8,128)(2,1)S(1)} %get-tuple-element.12), channel_id=1, source_target_pairs={{0,1},{1,0},{2,3},{3,2},{4,5},{5,4},{6,7},{7,6},{8,9},{9,8},{10,11... | collective-permute-start | bytes 589832 | tf_op jit(solution)/shard_map/ppermute | solution.py:196
  70.4 3.9 %collective-permute-start.4 = (bf16[4,64,256]{2,1,0:T(8,128)(2,1)S(1)}, bf16[4,64,256]{2,1,0:T(8,128)(2,1)S(1)}, u32[]{:S(2)}, u32[]{:S(2)}) collective-permute-start(bf16[4,64,256]{2,1,0:T(8,128)(2,1)S(1)} %get-tuple-element.14), channel_id=1, source_target_pairs={{0,4},{2,6},{4,0},{6,2},{1,5},{3,7},{5,1},{7,3},{8,12},{10,14},{12... | collective-permute-start | bytes 393224 | tf_op jit(solution)/shard_map/ppermute | solution.py:193
  74.3 0.0 collective-permute-done.1
  74.4 1.1 %collective-permute-start.2 = (bf16[2,4,32,256]{3,2,1,0:T(8,128)(2,1)S(1)}, bf16[2,4,32,256]{3,2,1,0:T(8,128)(2,1)S(1)}, u32[]{:S(2)}, u32[]{:S(2)}) collective-permute-start(bf16[2,4,32,256]{3,2,1,0:T(8,128)(2,1)S(1)} %pad_maximum_fusion), channel_id=1, source_target_pairs={{0,2},{2,4},{4,6},{6,0},{1,3},{3,5},{5,7},{7,1},{8,10},{10,12},{12... | collective-permute-start | bytes 393224 | tf_op jit(solution)/shard_map/ppermute | solution.py:193
  75.5 2.3 %collective-permute-start.3 = (bf16[2,4,32,256]{3,2,1,0:T(8,128)(2,1)S(1)}, bf16[2,4,32,256]{3,2,1,0:T(8,128)(2,1)S(1)}, u32[]{:S(2)}, u32[]{:S(2)}) collective-permute-start(bf16[2,4,32,256]{3,2,1,0:T(8,128)(2,1)S(1)} %pad_maximum_fusion.1), channel_id=1, source_target_pairs={{0,6},{2,0},{4,2},{6,4},{1,7},{3,1},{5,3},{7,5},{8,14},{10,8},{12,... | collective-permute-start | bytes 393224 | tf_op jit(solution)/shard_map/ppermute | solution.py:193
  77.7 0.5 collective-permute-done.4
  78.2 0.0 collective-permute-start.5
  78.2 0.1 constant_dynamic-slice_fusion
  78.3 2.6 %collective-permute-done.2 = bf16[2,4,32,256]{3,2,1,0:T(8,128)(2,1)S(1)} collective-permute-done((bf16[2,4,32,256]{3,2,1,0:T(8,128)(2,1)S(1)}, bf16[2,4,32,256]{3,2,1,0:T(8,128)(2,1)S(1)}, u32[]{:S(2)}, u32[]{:S(2)}) %collective-permute-start.2) | collective-permute-done | bytes 131104 | tf_op jit(solution)/shard_map/ppermute | solution.py:193
  80.9 0.7 collective-permute-done.3
  81.6 0.0 collective-permute-done.5
  81.7 0.1 select_bitcast_fusion.1
  81.8 0.1 fusion.5
  81.9 0.8 copy.11
  (8 shorter events, 0.1 us)
Async XLA Ops:
  0.0 9.5 %copy-start = (bf16[2,256,4,256]{3,2,1,0:T(4,128)(2,1)S(1)}, bf16[2,256,4,256]{3,2,1,0:T(4,128)(2,1)}, u32[]{:S(2)}) copy-start(bf16[2,256,4,256]{3,2,1,0:T(4,128)(2,1)} %param.5) | copy-start | bytes 3145732
  0.0 9.8 %collective-permute-start = (bf16[2,16,1,256,256]{4,3,2,1,0:T(8,128)(2,1)}, bf16[2,16,1,256,256]{4,3,2,1,0:T(8,128)(2,1)}, u32[]{:S(2)}, u32[]{:S(2)}) collective-permute-start(bf16[2,16,1,256,256]{4,3,2,1,0:T(8,128)(2,1)} %own_ref.1), channel_id=1, source_target_pairs={{0,1},{1,0},{2,3},{3,2},{4,5},{5,4},{6,7},{7,6},{8,9},{9,8},{10,11... | collective-permute-start | bytes 12582920 | tf_op jit(solution)/shard_map/ppermute | solution.py:173
  0.0 7.9 %copy-start.3 = (s32[32]{0:T(128)S(1)}, s32[32]{0:T(128)}, u32[]{:S(2)}) copy-start(s32[32]{0:T(128)} %param.6) | copy-start | bytes 388
  0.0 8.5 %copy-start.2 = (f32[128,4,4]{0,2,1:T(4,128)S(1)}, f32[128,4,4]{0,2,1:T(4,128)}, u32[]{:S(2)}) copy-start(f32[128,4,4]{0,2,1:T(4,128)} %param.9) | copy-start | bytes 24580
  0.0 62.4 %all-to-all-start = ((bf16[32,256,256]{2,1,0:T(8,128)(2,1)}), bf16[32,256,256]{2,1,0:T(8,128)(2,1)}, u32[]{:S(2)}, u32[]{:S(2)}) async-start(bf16[32,256,256]{2,1,0:T(8,128)(2,1)} %bitcast.44), calls=%async_computation | async-start | bytes 8388608 | tf_op jit(solution)/shard_map/all_to_all | solution.py:174
  9.9 2.2 %copy-start.1 = (bf16[2,16,1,256,256]{4,3,2,1,0:T(8,128)(2,1)S(1)}, bf16[2,16,1,256,256]{4,3,2,1,0:T(8,128)(2,1)}, u32[]{:S(2)}) copy-start(bf16[2,16,1,256,256]{4,3,2,1,0:T(8,128)(2,1)} %own_ref.1) | copy-start | bytes 12582916
  69.4 4.9 %collective-permute-start.1 = (bf16[3,4,32,256]{3,2,1,0:T(8,128)(2,1)S(1)}, bf16[3,4,32,256]{3,2,1,0:T(8,128)(2,1)S(1)}, u32[]{:S(2)}, u32[]{:S(2)}) collective-permute-start(bf16[3,4,32,256]{3,2,1,0:T(8,128)(2,1)S(1)} %get-tuple-element.12), channel_id=1, source_target_pairs={{0,1},{1,0},{2,3},{3,2},{4,5},{5,4},{6,7},{7,6},{8,9},{9,8},{10,11... | collective-permute-start | bytes 589832 | tf_op jit(solution)/shard_map/ppermute | solution.py:196
  70.4 7.8 %collective-permute-start.4 = (bf16[4,64,256]{2,1,0:T(8,128)(2,1)S(1)}, bf16[4,64,256]{2,1,0:T(8,128)(2,1)S(1)}, u32[]{:S(2)}, u32[]{:S(2)}) collective-permute-start(bf16[4,64,256]{2,1,0:T(8,128)(2,1)S(1)} %get-tuple-element.14), channel_id=1, source_target_pairs={{0,4},{2,6},{4,0},{6,2},{1,5},{3,7},{5,1},{7,3},{8,12},{10,14},{12... | collective-permute-start | bytes 393224 | tf_op jit(solution)/shard_map/ppermute | solution.py:193
  74.4 6.5 %collective-permute-start.2 = (bf16[2,4,32,256]{3,2,1,0:T(8,128)(2,1)S(1)}, bf16[2,4,32,256]{3,2,1,0:T(8,128)(2,1)S(1)}, u32[]{:S(2)}, u32[]{:S(2)}) collective-permute-start(bf16[2,4,32,256]{3,2,1,0:T(8,128)(2,1)S(1)} %pad_maximum_fusion), channel_id=1, source_target_pairs={{0,2},{2,4},{4,6},{6,0},{1,3},{3,5},{5,7},{7,1},{8,10},{10,12},{12... | collective-permute-start | bytes 393224 | tf_op jit(solution)/shard_map/ppermute | solution.py:193
  75.5 6.2 %collective-permute-start.3 = (bf16[2,4,32,256]{3,2,1,0:T(8,128)(2,1)S(1)}, bf16[2,4,32,256]{3,2,1,0:T(8,128)(2,1)S(1)}, u32[]{:S(2)}, u32[]{:S(2)}) collective-permute-start(bf16[2,4,32,256]{3,2,1,0:T(8,128)(2,1)S(1)} %pad_maximum_fusion.1), channel_id=1, source_target_pairs={{0,6},{2,0},{4,2},{6,4},{1,7},{3,1},{5,3},{7,5},{8,14},{10,8},{12,... | collective-permute-start | bytes 393224 | tf_op jit(solution)/shard_map/ppermute | solution.py:193
  78.2 3.4 %collective-permute-start.5 = (bf16[4,32,256]{2,1,0:T(8,128)(2,1)S(1)}, bf16[4,32,256]{2,1,0:T(8,128)(2,1)S(1)}, u32[]{:S(2)}, u32[]{:S(2)}) collective-permute-start(bf16[4,32,256]{2,1,0:T(8,128)(2,1)S(1)} %constant_dynamic-slice_fusion.1), channel_id=1, source_target_pairs={{0,1},{1,0},{2,3},{3,2},{4,5},{5,4},{6,7},{7,6},{8,9},{9,8},{10,11... | collective-permute-start | bytes 196616 | tf_op jit(solution)/shard_map/ppermute | solution.py:206
